TPU v7x, 32 devices: a whole 2x2x4 slice. The times are simulated.
32 devices in a mesh: fsdp: 4 (over y, x), seq: 8 (over z, core).
Axes of the slice: x: 2, y: 2, z: 4, core: 2. Of those that a mesh axis runs over, the one named last changes fastest.
Arguments:
- tokens: bfloat16 [2, 4, 2048, 2048], P(None, 'fsdp', 'seq'), may hold values from -6 to 6
- positions: int32 [2, 4, 2048], P(None, 'fsdp', 'seq'), may hold values from 0 to 2045, as said below
- out_grad: bfloat16 [2, 4, 2048, 2048], P(None, 'fsdp', 'seq'), may hold values from -6 to 6
- w_query: bfloat16 [2048, 2048], P(('fsdp', 'seq')), may hold values from -0.125 to 0.125
- w_key: bfloat16 [2048, 2048], P(('fsdp', 'seq')), may hold values from -0.125 to 0.125
- w_value: bfloat16 [2048, 2048], P(('fsdp', 'seq')), may hold values from -0.125 to 0.125
- w_output: bfloat16 [2048, 2048], P(('fsdp', 'seq')), may hold values from -0.125 to 0.125
- query_gain: bfloat16 [2048], P(('fsdp', 'seq')), may hold values from 0.5 to 1.5
- key_gain: bfloat16 [2048], P(('fsdp', 'seq')), may hold values from 0.5 to 1.5
- attn_gain: bfloat16 [2048], P(('fsdp', 'seq')), may hold values from 0.5 to 1.5
- w_gate: bfloat16 [2048, 8192], P(('fsdp', 'seq')), may hold values from -0.125 to 0.125
- w_up: bfloat16 [2048, 8192], P(('fsdp', 'seq')), may hold values from -0.125 to 0.125
- w_down: bfloat16 [8192, 2048], P(('fsdp', 'seq')), may hold values from -0.0625 to 0.0625
- mlp_gain: bfloat16 [2048], P(('fsdp', 'seq')), may hold values from 0.5 to 1.5
Outputs:
- mixed: bfloat16 [2, 4, 2048, 2048], P(None, 'fsdp', 'seq')
- input_grad: bfloat16 [2, 4, 2048, 2048], P(None, 'fsdp', 'seq')
- grad_w_query: float32 [2048, 2048], P(('fsdp', 'seq'))
- grad_w_key: float32 [2048, 2048], P(('fsdp', 'seq'))
- grad_w_value: float32 [2048, 2048], P(('fsdp', 'seq'))
- grad_w_output: float32 [2048, 2048], P(('fsdp', 'seq'))
- grad_query_gain: float32 [2048], P(('fsdp', 'seq'))
- grad_key_gain: float32 [2048], P(('fsdp', 'seq'))
- grad_attn_gain: float32 [2048], P(('fsdp', 'seq'))
- grad_w_gate: float32 [2048, 8192], P(('fsdp', 'seq'))
- grad_w_up: float32 [2048, 8192], P(('fsdp', 'seq'))
- grad_w_down: float32 [8192, 2048], P(('fsdp', 'seq'))
- grad_mlp_gain: float32 [2048], P(('fsdp', 'seq'))
Inputs may be any that keep to these rules, and one draw needn't show every extreme that they name: `positions`: positions count from 0 at the first token of each document; a sequence holds three documents back to back, the middle one beginning among its first 256 tokens and ending among its last 256. Some sequence reaches the largest position.
All inputs are finite; a program needn't handle non-finite values.
Results may differ from a plain program's by a relative error of at most 0.025.
Values may be sent and summed in bfloat16 or wider, within the bound.
No kernel may reach another device: no remote copies, remote signals or barrier semaphores. Data moves between devices by JAX's collectives and lax.ppermute only.
A program may use at most 512 MiB of HBM per device.

v0:
```python
import jax
import jax.numpy as jnp
from jax import lax
from jax.sharding import PartitionSpec as P

HEADS = 16
HEAD_DIM = 128


EPSILON = 1e-06
THETA = 500000.0


def project(former, latter):
    return jnp.dot(former, latter, preferred_element_type=jnp.float32)


def project_tn(former, latter):
    return lax.dot_general(
        former, latter, (((0,), (0,)), ((), ())), preferred_element_type=jnp.float32
    )


def project_nt(former, latter):
    return lax.dot_general(
        former, latter, (((1,), (1,)), ((), ())), preferred_element_type=jnp.float32
    )


def inv_rms(values):
    return lax.rsqrt(jnp.mean(values * values, axis=-1, keepdims=True) + EPSILON)


def norm_back(incoming, values, factor, gain_row):
    weighted = incoming * gain_row
    inner_mean = jnp.mean(weighted * values, axis=-1, keepdims=True)
    result_grad = factor * (weighted - values * factor * factor * inner_mean)
    return (result_grad, jnp.sum(incoming * values * factor, axis=0))


def rotate_half(values):
    half_size = values.shape[-1] // 2
    return jnp.concatenate([-values[..., half_size:], values[..., :half_size]], axis=-1)


def rope_tables(places_pos, head_size):
    exponent = jnp.arange(0, head_size // 2, dtype=jnp.float32) * (2.0 / head_size)
    frequency = THETA ** (-exponent)
    angles = places_pos.astype(jnp.float32)[:, None] * frequency[None, :]
    angles = jnp.concatenate([angles, angles], axis=-1)
    return (jnp.cos(angles), jnp.sin(angles))


def visible_mask(first_row, block_rows, starts, seq_count):
    places = jnp.arange(seq_count, dtype=jnp.int32)
    row_ids = first_row + jnp.arange(block_rows, dtype=jnp.int32)
    start_block = lax.dynamic_slice_in_dim(starts, first_row, block_rows, 1)
    return (places[None, None, :] <= row_ids[None, :, None]) & (
        starts[:, None, :] == start_block[:, :, None]
    )


def attend_forward(queries, keys_all, values_all, starts, factor):
    seq_count = queries.shape[1]
    block_rows = min(512, seq_count)

    def one_block(first_row):
        query_block = lax.dynamic_slice_in_dim(queries, first_row, block_rows, 1)
        visible = visible_mask(first_row, block_rows, starts, seq_count)
        scores = (
            jnp.einsum("sqhd,skhd->shqk", query_block, keys_all, preferred_element_type=jnp.float32)
            * factor
        )
        scores = jnp.where(visible[:, None], scores, -1e30)
        maximum = jnp.max(scores, axis=-1, keepdims=True)
        expo_vals = jnp.exp(scores - maximum)
        total_sum = jnp.sum(expo_vals, axis=-1, keepdims=True)
        soft_weights = (expo_vals / total_sum).astype(jnp.bfloat16)
        outcome = jnp.einsum(
            "shqk,skhd->sqhd", soft_weights, values_all, preferred_element_type=jnp.float32
        )
        return (outcome.astype(jnp.bfloat16), (maximum + jnp.log(total_sum))[..., 0])

    first_rows = jnp.arange(seq_count // block_rows, dtype=jnp.int32) * block_rows
    return lax.map(one_block, first_rows)


def attend_backward(queries, keys_all, values_all, starts, grad_out, log_sums, factor):
    seq_count = queries.shape[1]
    block_rows = min(512, seq_count)

    def one_block(carry, packed):
        key_sum, value_sum = carry
        first_row, lse_block = packed
        query_block = lax.dynamic_slice_in_dim(queries, first_row, block_rows, 1)
        grad_block = lax.dynamic_slice_in_dim(grad_out, first_row, block_rows, 1)
        visible = visible_mask(first_row, block_rows, starts, seq_count)
        scores = (
            jnp.einsum("sqhd,skhd->shqk", query_block, keys_all, preferred_element_type=jnp.float32)
            * factor
        )
        scores = jnp.where(visible[:, None], scores, -1e30)
        soft_full = jnp.exp(scores - lse_block[..., None])
        soft_low = soft_full.astype(jnp.bfloat16)
        value_sum = value_sum + jnp.einsum(
            "shqk,sqhd->skhd", soft_low, grad_block, preferred_element_type=jnp.float32
        )
        grad_soft = jnp.einsum(
            "sqhd,skhd->shqk", grad_block, values_all, preferred_element_type=jnp.float32
        )
        delta_rows = jnp.sum(grad_soft * soft_full, axis=-1, keepdims=True)
        grad_scores = (soft_full * (grad_soft - delta_rows)).astype(jnp.bfloat16)
        grad_query = (
            jnp.einsum("shqk,skhd->sqhd", grad_scores, keys_all, preferred_element_type=jnp.float32)
            * factor
        )
        key_sum = (
            key_sum
            + jnp.einsum(
                "shqk,sqhd->skhd", grad_scores, query_block, preferred_element_type=jnp.float32
            )
            * factor
        )
        return ((key_sum, value_sum), grad_query.astype(jnp.bfloat16))

    first_rows = jnp.arange(seq_count // block_rows, dtype=jnp.int32) * block_rows
    zero_sums = jnp.zeros(keys_all.shape, jnp.float32)
    (key_sum, value_sum), grad_query = lax.scan(
        one_block, (zero_sums, zero_sums), (first_rows, log_sums)
    )
    return (grad_query, key_sum, value_sum)


def on_device(
    tokens,
    positions,
    out_grad,
    w_query,
    w_key,
    w_value,
    w_output,
    query_gain,
    key_gain,
    attn_gain,
    w_gate,
    w_up,
    w_down,
    mlp_gain,
):
    group_size = lax.axis_size("seq")
    local_heads = HEADS // group_size
    factor = HEAD_DIM ** (-0.5)
    group_count = tokens.shape[0] * tokens.shape[1]
    tok_count = tokens.shape[2]
    width_all = tokens.shape[3]
    row_count = group_count * tok_count
    whole_pos = lax.all_gather(positions, "seq", axis=2, tiled=True)
    seq_count = whole_pos.shape[2]
    head_shape = (group_count, seq_count, local_heads, HEAD_DIM)
    local_width = local_heads * HEAD_DIM

    def join_blocks(blocked):
        return jnp.moveaxis(blocked, 0, 1).reshape(group_count, seq_count, local_width)

    inputs = tokens.reshape(row_count, width_all)
    cosine, sine_table = rope_tables(positions.reshape(row_count), HEAD_DIM)
    cosine = cosine[:, None, :]
    sine_table = sine_table[:, None, :]
    starts = jnp.arange(seq_count, dtype=jnp.int32)[None, :] - whole_pos.reshape(
        group_count, seq_count
    )
    q_weight, k_weight, v_weight, o_weight, q_gain, k_gain, a_gain = (
        lax.all_gather(w_query, ("fsdp", "seq"), axis=0, tiled=True),
        lax.all_gather(w_key, ("fsdp", "seq"), axis=0, tiled=True),
        lax.all_gather(w_value, ("fsdp", "seq"), axis=0, tiled=True),
        lax.all_gather(w_output, ("fsdp", "seq"), axis=0, tiled=True),
        lax.all_gather(query_gain, ("fsdp", "seq"), axis=0, tiled=True),
        lax.all_gather(key_gain, ("fsdp", "seq"), axis=0, tiled=True),
        lax.all_gather(attn_gain, ("fsdp", "seq"), axis=0, tiled=True),
    )
    q_proj = project(inputs, q_weight)
    k_proj = project(inputs, k_weight)
    v_proj = project(inputs, v_weight)
    q_scale = inv_rms(q_proj)
    k_scale = inv_rms(k_proj)
    q_norm = (q_proj * q_scale * q_gain.astype(jnp.float32)).reshape(row_count, HEADS, HEAD_DIM)
    k_norm = (k_proj * k_scale * k_gain.astype(jnp.float32)).reshape(row_count, HEADS, HEAD_DIM)
    q_rot = (
        (q_norm * cosine + rotate_half(q_norm) * sine_table)
        .astype(jnp.bfloat16)
        .reshape(group_count, tok_count, width_all)
    )
    k_rot = (
        (k_norm * cosine + rotate_half(k_norm) * sine_table)
        .astype(jnp.bfloat16)
        .reshape(group_count, tok_count, width_all)
    )
    v_low = v_proj.astype(jnp.bfloat16).reshape(group_count, tok_count, width_all)
    by_heads = lax.all_to_all(
        jnp.stack([q_rot, k_rot, v_low]), "seq", split_axis=3, concat_axis=2, tiled=True
    )
    q_heads = by_heads[0].reshape(head_shape)
    k_heads = by_heads[1].reshape(head_shape)
    v_heads = by_heads[2].reshape(head_shape)
    blocked_out, log_sums = attend_forward(q_heads, k_heads, v_heads, starts, factor)
    attn_rows = lax.all_to_all(
        join_blocks(blocked_out), "seq", split_axis=1, concat_axis=2, tiled=True
    ).reshape(row_count, width_all)
    a_proj = project(attn_rows, o_weight)
    a_scale = inv_rms(a_proj)
    hidden = inputs.astype(jnp.float32) + a_proj * a_scale * a_gain.astype(jnp.float32)
    hidden_low = hidden.astype(jnp.bfloat16)
    g_weight, u_weight, d_weight, m_gain = (
        lax.all_gather(w_gate, ("fsdp", "seq"), axis=0, tiled=True),
        lax.all_gather(w_up, ("fsdp", "seq"), axis=0, tiled=True),
        lax.all_gather(w_down, ("fsdp", "seq"), axis=0, tiled=True),
        lax.all_gather(mlp_gain, ("fsdp", "seq"), axis=0, tiled=True),
    )
    gate_proj = project(hidden_low, g_weight)
    up_proj = project(hidden_low, u_weight)
    sigmoid_gate = jax.nn.sigmoid(gate_proj)
    activated = (gate_proj * sigmoid_gate * up_proj).astype(jnp.bfloat16)
    m_proj = project(activated, d_weight)
    m_scale = inv_rms(m_proj)
    result_rows = hidden + m_proj * m_scale * m_gain.astype(jnp.float32)
    g_weight, u_weight, d_weight, m_gain = (
        lax.all_gather(w_gate, ("fsdp", "seq"), axis=0, tiled=True),
        lax.all_gather(w_up, ("fsdp", "seq"), axis=0, tiled=True),
        lax.all_gather(w_down, ("fsdp", "seq"), axis=0, tiled=True),
        lax.all_gather(mlp_gain, ("fsdp", "seq"), axis=0, tiled=True),
    )
    grad_rows = out_grad.reshape(row_count, width_all).astype(jnp.float32)
    grad_mproj, grad_mgain = norm_back(grad_rows, m_proj, m_scale, m_gain.astype(jnp.float32))
    grad_mproj = grad_mproj.astype(jnp.bfloat16)
    share_down = lax.psum_scatter(
        project_tn(activated, grad_mproj), ("fsdp", "seq"), scatter_dimension=0, tiled=True
    )
    grad_act = project_nt(grad_mproj, d_weight)
    grad_gate = (
        grad_act * up_proj * sigmoid_gate * (1.0 + gate_proj * (1.0 - sigmoid_gate))
    ).astype(jnp.bfloat16)
    grad_upper = (grad_act * gate_proj * sigmoid_gate).astype(jnp.bfloat16)
    grad_hidden = grad_rows + project_nt(grad_gate, g_weight) + project_nt(grad_upper, u_weight)
    q_weight, k_weight, v_weight, o_weight, q_gain, k_gain, a_gain = (
        lax.all_gather(w_query, ("fsdp", "seq"), axis=0, tiled=True),
        lax.all_gather(w_key, ("fsdp", "seq"), axis=0, tiled=True),
        lax.all_gather(w_value, ("fsdp", "seq"), axis=0, tiled=True),
        lax.all_gather(w_output, ("fsdp", "seq"), axis=0, tiled=True),
        lax.all_gather(query_gain, ("fsdp", "seq"), axis=0, tiled=True),
        lax.all_gather(key_gain, ("fsdp", "seq"), axis=0, tiled=True),
        lax.all_gather(attn_gain, ("fsdp", "seq"), axis=0, tiled=True),
    )
    grad_aproj, grad_again = norm_back(grad_hidden, a_proj, a_scale, a_gain.astype(jnp.float32))
    grad_aproj = grad_aproj.astype(jnp.bfloat16)
    grad_attn = (
        project_nt(grad_aproj, o_weight)
        .astype(jnp.bfloat16)
        .reshape(group_count, tok_count, width_all)
    )
    grad_heads = lax.all_to_all(grad_attn, "seq", split_axis=2, concat_axis=1, tiled=True).reshape(
        head_shape
    )
    grad_query, key_sum, value_sum = attend_backward(
        q_heads, k_heads, v_heads, starts, grad_heads, log_sums, factor
    )
    grad_stack = jnp.stack(
        [
            join_blocks(grad_query),
            key_sum.astype(jnp.bfloat16).reshape(group_count, seq_count, local_width),
            value_sum.astype(jnp.bfloat16).reshape(group_count, seq_count, local_width),
        ]
    )
    by_tokens = lax.all_to_all(grad_stack, "seq", split_axis=2, concat_axis=3, tiled=True)
    grad_qrot = by_tokens[0].reshape(row_count, HEADS, HEAD_DIM).astype(jnp.float32)
    grad_krot = by_tokens[1].reshape(row_count, HEADS, HEAD_DIM).astype(jnp.float32)
    grad_vproj = by_tokens[2].reshape(row_count, width_all)
    grad_qnorm = (grad_qrot * cosine - rotate_half(grad_qrot) * sine_table).reshape(
        row_count, width_all
    )
    grad_knorm = (grad_krot * cosine - rotate_half(grad_krot) * sine_table).reshape(
        row_count, width_all
    )
    grad_qproj, grad_qgain = norm_back(grad_qnorm, q_proj, q_scale, q_gain.astype(jnp.float32))
    grad_kproj, grad_kgain = norm_back(grad_knorm, k_proj, k_scale, k_gain.astype(jnp.float32))
    grad_qproj = grad_qproj.astype(jnp.bfloat16)
    grad_kproj = grad_kproj.astype(jnp.bfloat16)
    grad_inputs = (
        grad_hidden
        + project_nt(grad_qproj, q_weight)
        + project_nt(grad_kproj, k_weight)
        + project_nt(grad_vproj, v_weight)
    )
    shares = lax.psum_scatter(
        (
            project_tn(inputs, grad_qproj),
            project_tn(inputs, grad_kproj),
            project_tn(inputs, grad_vproj),
            project_tn(attn_rows, grad_aproj),
            grad_qgain,
            grad_kgain,
            grad_again,
            project_tn(hidden_low, grad_gate),
            project_tn(hidden_low, grad_upper),
            grad_mgain,
        ),
        ("fsdp", "seq"),
        scatter_dimension=0,
        tiled=True,
    )
    mixed = result_rows.astype(jnp.bfloat16).reshape(tokens.shape)
    input_grad = grad_inputs.astype(jnp.bfloat16).reshape(tokens.shape)
    return (
        mixed,
        input_grad,
        shares[0],
        shares[1],
        shares[2],
        shares[3],
        shares[4],
        shares[5],
        shares[6],
        shares[7],
        shares[8],
        share_down,
        shares[9],
    )


def solution(mesh):
    placed = (
        P(None, "fsdp", "seq", None),
        P(None, "fsdp", "seq"),
        P(None, "fsdp", "seq", None),
        P(("fsdp", "seq"), None),
        P(("fsdp", "seq"), None),
        P(("fsdp", "seq"), None),
        P(("fsdp", "seq"), None),
        P(("fsdp", "seq")),
        P(("fsdp", "seq")),
        P(("fsdp", "seq")),
        P(("fsdp", "seq"), None),
        P(("fsdp", "seq"), None),
        P(("fsdp", "seq"), None),
        P(("fsdp", "seq")),
    )
    return jax.shard_map(
        on_device,
        mesh=mesh,
        in_specs=placed,
        out_specs=(
            P(None, "fsdp", "seq", None),
            P(None, "fsdp", "seq", None),
            P(("fsdp", "seq"), None),
            P(("fsdp", "seq"), None),
            P(("fsdp", "seq"), None),
            P(("fsdp", "seq"), None),
            P(("fsdp", "seq")),
            P(("fsdp", "seq")),
            P(("fsdp", "seq")),
            P(("fsdp", "seq"), None),
            P(("fsdp", "seq"), None),
            P(("fsdp", "seq"), None),
            P(("fsdp", "seq")),
        ),
        check_vma=False,
    )
```

profile of v0, /device:TPU:0, one launch (start us, length us, event | category | flops | bytes accessed | tf_op | source)
XLA Modules:
  0.0 4538.4 jit_solution(10873708557796416278)
XLA Ops:
  13.0 42.6 all-reduce.9
  64.7 27.0 all-gather.8.cloned.1.call-done
  103.6 67.1 %all-gather.10.cloned.1.call-done = bf16[2048,2048]{1,0:T(8,128)(2,1)} async-done(((bf16[64,2048]{1,0:T(8,128)(2,1)}), bf16[2048,2048]{1,0:T(8,128)(2,1)}) %all-gather.10.cloned.1.call-update) | async-done | bytes 8388624 | tf_op jit(solution)/shard_map/all_gather | solution.py:174
  209.5 12.0 add_convert_fusion.3
  221.6 28.1 all-gather.12.cloned.1.call-done
  261.1 16.1 copy.124
  282.1 232.0 %all_gather.47 = s32[2,1,2048]{2,0,1:T(2,128)S(1)} all-gather(s32[2,1,256]{2,0,1:T(2,128)S(1)} %copy.123), channel_id=1, replica_groups=mesh['fsdp'=4,'seq'=8] {'seq'}, dimensions={2}, use_global_device_ids=true | all-gather | bytes 18432 | tf_op jit(solution)/shard_map/all_gather | solution.py:157
  550.1 93.5 %while.27 = (s32[]{:T(128)}, bf16[4,2,512,2,128]{4,2,3,1,0:T(8,128)(2,1)}, f32[4,2,2,512]{3,2,1,0:T(2,128)}, s32[4]{0:T(128)S(1)}, s32[2,2048]{1,0:T(2,128)S(1)}...) while((s32[]{:T(128)}, ...), condition=%wide.region_5.6_spmd, body=%wide.region_2.5_spmd.sunk | while | flops 2203318784 | bytes 74548416 | solution.py:85
  661.2 93.4 %all-to-all-done.1 = bf16[2,2048,256]{2,0,1:T(2,128)(2,1)S(1)} async-done(((bf16[2,2048,256]{2,0,1:T(2,128)(2,1)}), bf16[2,2048,256]{2,0,1:T(2,128)(2,1)S(1)}, u32[]{:S(2)}, u32[]{:S(2)}) %all-to-all-start.1) | async-done | bytes 2097184 | tf_op jit(solution)/shard_map/all_to_all | solution.py:206
  767.6 27.5 fusion.45
  795.1 64.0 %all-gather.18.cloned.1.call-done = bf16[2048,8192]{1,0:T(8,128)(2,1)} async-done(((bf16[64,8192]{1,0:T(8,128)(2,1)}), bf16[2048,8192]{1,0:T(8,128)(2,1)}) %all-gather.18.cloned.1.call-update) | async-done | bytes 33554448 | tf_op jit(solution)/shard_map/all_gather | solution.py:215
  859.2 36.2 multiply_convert_fusion.3
  895.3 159.8 %all-gather.20.cloned.1.call-done = bf16[8192,2048]{1,0:T(8,128)(2,1)} async-done(((bf16[256,2048]{1,0:T(8,128)(2,1)}), bf16[8192,2048]{1,0:T(8,128)(2,1)}) %all-gather.20.cloned.1.call-update) | async-done | bytes 33554448 | tf_op jit(solution)/shard_map/all_gather | solution.py:216
  1055.1 24.2 multiply_reduce_fusion.7
  1083.7 34.5 multiply_convert_fusion.1
  1118.2 24.9 fusion.46
  1143.2 27.7 multiply_reduce_fusion.1
  1193.9 12.6 fusion.49
  1206.6 58.1 %all-to-all-done.2 = bf16[2,256,2048]{1,0,2:T(2,128)(2,1)S(1)} async-done(((bf16[2,256,2048]{1,0,2:T(2,128)(2,1)}), bf16[2,256,2048]{1,0,2:T(2,128)(2,1)S(1)}, u32[]{:S(2)}, u32[]{:S(2)}) %all-to-all-start.2) | async-done | bytes 2097184 | tf_op jit(solution)/shard_map/all_to_all | solution.py:260
  1270.2 270.9 %while.28 = (s32[]{:T(128)}, f32[2,2048,2,128]{1,3,2,0:T(8,128)}, f32[2,2048,2,128]{1,3,2,0:T(8,128)}, bf16[4,2,512,2,128]{4,2,3,1,0:T(8,128)(2,1)}, s32[4]{0:T(...) while((s32[]{:T(128)}, f32[2,2048,2,128]{1,3,2,0:T(8,128)}, ...), condition=%wide.region_12.13_spmd.clone, body=%wide.region_10.12_spmd.clone.sunk | while | flops 5442632192 | bytes 220816192 | solution.py:128
  1286.2 13.6 multiply_reduce_fusion.12
  1299.9 15.4 multiply_convert_fusion.8
  1326.2 10.7 bitcast_add_fusion.5
  1352.8 13.6 multiply_reduce_fusion.12
  1366.4 15.5 multiply_convert_fusion.8
  1394.0 11.6 bitcast_add_fusion.5
  1421.5 13.5 multiply_reduce_fusion.12
  1435.0 14.9 multiply_convert_fusion.8
  1462.0 11.4 bitcast_add_fusion.5
  1489.2 13.5 multiply_reduce_fusion.12
  1502.7 14.9 multiply_convert_fusion.8
  1529.6 11.3 bitcast_add_fusion.5
  1561.2 40.6 copy.145
  1601.8 142.0 %all_to_all.60 = bf16[3,2,2048,256]{3,1,0,2:T(2,128)(2,1)S(1)} all-to-all(bf16[3,2,2048,256]{3,1,0,2:T(2,128)(2,1)S(1)} %copy.145), channel_id=1, replica_groups=mesh['fsdp'=4,'seq'=8] {'seq'}, dimensions={2} | all-to-all | bytes 12582912 | tf_op jit(solution)/shard_map/all_to_all | solution.py:273
  1799.5 14.3 multiply_reduce_fusion.3
  1826.8 17.6 copy.162
  1858.7 17.7 copy.164
  1889.9 17.7 copy.166
  1909.2 29.6 fusion.52
  1940.4 29.6 fusion.50
  1970.1 29.6 fusion.51
  2000.5 39.8 all-reduce.8
  2062.2 10.9 add_convert_fusion
  2073.0 143.9 %reduce-scatter.24.cloned.1.call-done = f32[64,2048]{1,0:T(8,128)} async-done(((f32[2048,2048]{1,0:T(8,128)}), f32[64,2048]{1,0:T(8,128)}) %reduce-scatter.24.cloned.1.call-update) | async-done | bytes 524304
  2216.9 187.3 %reduce-scatter.26.cloned.1.call-done = f32[64,2048]{1,0:T(8,128)} async-done(((f32[2048,2048]{1,0:T(8,128)}), f32[64,2048]{1,0:T(8,128)}) %reduce-scatter.26.cloned.1.call-update) | async-done | bytes 524304
  2404.2 709.9 %reduce-scatter.20.cloned.1.call-done = f32[256,2048]{1,0:T(8,128)} async-done(((f32[8192,2048]{1,0:T(8,128)}), f32[256,2048]{1,0:T(8,128)}) %reduce-scatter.20.cloned.1.call-update) | async-done | bytes 2097168 | tf_op jit(solution)/shard_map/reduce_scatter | solution.py:235
  3114.2 708.9 %reduce-scatter.16.cloned.1.call-done = f32[64,8192]{1,0:T(8,128)} async-done(((f32[2048,8192]{1,0:T(8,128)}), f32[64,8192]{1,0:T(8,128)}) %reduce-scatter.16.cloned.1.call-update) | async-done | bytes 2097168 | tf_op jit(solution)/shard_map/reduce_scatter | solution.py:293
  3823.0 708.7 %reduce-scatter.18.cloned.1.call-done = f32[64,8192]{1,0:T(8,128)} async-done(((f32[2048,8192]{1,0:T(8,128)}), f32[64,8192]{1,0:T(8,128)}) %reduce-scatter.18.cloned.1.call-update) | async-done | bytes 2097168 | tf_op jit(solution)/shard_map/reduce_scatter | solution.py:293
  (376 shorter events, 511.2 us)
Async XLA Ops:
  7.2 48.4 %copy-start.57 = (s32[2,1,256]{2,1,0:T(1,128)S(1)}, s32[2,1,256]{2,1,0:T(1,128)}, u32[]{:S(2)}) copy-start(s32[2,1,256]{2,1,0:T(1,128)} %param.19) | copy-start | bytes 6148
  7.2 84.4 %all-gather.8.cloned.1.call-start = ((), (), s32[]{:S(2)}) async-start(), calls=%async_computation.11 | async-start | bytes 8650752 | tf_op jit(solution)/shard_map/all_gather | solution.py:173
  8.0 162.7 %all-gather.10.cloned.1.call-start = ((), (), s32[]{:S(2)}) async-start(), calls=%async_computation.12 | async-start | bytes 8650752 | tf_op jit(solution)/shard_map/all_gather | solution.py:174
  8.7 241.0 %all-gather.12.cloned.1.call-start = ((), (), s32[]{:S(2)}) async-start(), calls=%async_computation.13 | async-start | bytes 8650752 | tf_op jit(solution)/shard_map/all_gather | solution.py:175
  9.4 747.0 %all-gather.14.cloned.1.call-start = ((), (), s32[]{:S(2)}) async-start(), calls=%async_computation.14 | async-start | bytes 8650752 | tf_op jit(solution)/shard_map/all_gather | solution.py:176
  10.0 757.6 %all-gather.16.cloned.1.call-start = ((), (), s32[]{:S(2)}) async-start(), calls=%async_computation.15 | async-start | bytes 34603008 | tf_op jit(solution)/shard_map/all_gather | solution.py:214
  10.6 848.5 %all-gather.18.cloned.1.call-start = ((), (), s32[]{:S(2)}) async-start(), calls=%async_computation.16 | async-start | bytes 34603008 | tf_op jit(solution)/shard_map/all_gather | solution.py:215
  11.2 1044.0 %all-gather.20.cloned.1.call-start = ((), (), s32[]{:S(2)}) async-start(), calls=%async_computation.17 | async-start | bytes 34603008 | tf_op jit(solution)/shard_map/all_gather | solution.py:216
  55.6 146.8 %copy-start.44 = (f32[2048]{0:T(1024)}, f32[2048]{0:T(1024)S(1)}, u32[]{:S(2)}) copy-start(f32[2048]{0:T(1024)S(1)} %convert_element_type.143) | copy-start | bytes 24580
  55.6 151.6 %copy-start.42 = (f32[2048]{0:T(1024)}, f32[2048]{0:T(1024)S(1)}, u32[]{:S(2)}) copy-start(f32[2048]{0:T(1024)S(1)} %convert_element_type.147) | copy-start | bytes 24580
  56.9 129.2 %copy-start.31 = (f32[512,128]{1,0:T(8,128)}, f32[512,128]{1,0:T(8,128)S(1)}, u32[]{:S(2)}) copy-start(f32[512,128]{1,0:T(8,128)S(1)} %get-tuple-element.385) | copy-start | bytes 786436
  59.2 32.4 copy-start.22
  98.7 103.7 %copy-start.50 = (f32[512]{0:T(512)}, f32[512]{0:T(512)S(1)}, u32[]{:S(2)}) copy-start(f32[512]{0:T(512)S(1)} %add_rsqrt_fusion.3) | copy-start | bytes 6148
  177.7 29.5 copy-start.48
  209.5 40.1 copy-start.23
  277.3 236.8 %all-to-all-start = ((bf16[3,2,256,2048]{2,1,0,3:T(2,128)(2,1)}), bf16[3,2,256,2048]{2,1,0,3:T(2,128)(2,1)}, u32[]{:S(2)}, u32[]{:S(2)}) async-start(bf16[3,2,256,2048]{2,1,0,3:T(2,128)(2,1)} %copy.124), calls=%async_computation | async-start | bytes 12582912 | tf_op jit(solution)/shard_map/all_to_all | solution.py:199
  643.7 12.6 copy-start.1
  643.7 12.6 copy-start.29
  643.7 12.6 copy-start.65
  649.5 11.6 copy-start.60
  649.5 11.7 copy-start.59
  656.3 98.2 %all-to-all-start.1 = ((bf16[2,2048,256]{2,0,1:T(2,128)(2,1)}), bf16[2,2048,256]{2,0,1:T(2,128)(2,1)S(1)}, u32[]{:S(2)}, u32[]{:S(2)}) async-start(bf16[2,2048,256]{2,0,1:T(2,128)(2,1)} %reshape.415), calls=%async_computation.1 | async-start | bytes 4194304 | tf_op jit(solution)/shard_map/all_to_all | solution.py:206
  661.2 103.2 %copy-start.46 = (f32[2048]{0:T(1024)}, f32[2048]{0:T(1024)S(1)}, u32[]{:S(2)}) copy-start(f32[2048]{0:T(1024)S(1)} %convert_element_type.150) | copy-start | bytes 24580
  756.5 10.0 copy-start.24
  767.6 91.6 %copy-start.18 = (bf16[512,2048]{1,0:T(8,128)(2,1)}, bf16[512,2048]{1,0:T(8,128)(2,1)S(1)}, u32[]{:S(2)}) copy-start(bf16[512,2048]{1,0:T(8,128)(2,1)S(1)} %fusion.40) | copy-start | bytes 6291460
  1055.1 24.2 copy-start.21
  1118.2 25.0 copy-start.47
  1118.2 25.0 copy-start.56
  1143.2 27.7 copy-start.16
  1190.2 74.5 %all-to-all-start.2 = ((bf16[2,256,2048]{1,0,2:T(2,128)(2,1)}), bf16[2,256,2048]{1,0,2:T(2,128)(2,1)S(1)}, u32[]{:S(2)}, u32[]{:S(2)}) async-start(bf16[2,256,2048]{1,0,2:T(2,128)(2,1)} %copy.135), calls=%async_computation.2 | async-start | bytes 4194304 | tf_op jit(solution)/shard_map/all_to_all | solution.py:260
  1193.8 879.3 %reduce-scatter.14.cloned.1.call-start = ((), (), s32[]{:S(2)}) async-start(), calls=%async_computation.18 | async-start | bytes 17301504 | tf_op jit(solution)/shard_map/reduce_scatter | solution.py:293
  1206.5 866.5 %reduce-scatter.22.cloned.1.call-start = ((), (), s32[]{:S(2)}) async-start(), calls=%async_computation.22 | async-start | bytes 17301504
  1276.2 10.1 copy-start.5
  1342.7 10.1 copy-start.5
  1411.4 10.1 copy-start.5
  1479.2 10.1 copy-start.5
  1788.5 9.8 copy-start.10
  1788.5 11.0 copy-start.11
  1788.5 11.0 copy-start.43
  1788.5 11.0 copy-start.45
  1788.5 11.0 copy-start.49
  1788.5 11.0 copy-start.51
  1844.5 372.5 %reduce-scatter.24.cloned.1.call-start = ((), (), s32[]{:S(2)}) async-start(), calls=%async_computation.23 | async-start | bytes 17301504
  1876.4 527.8 %reduce-scatter.26.cloned.1.call-start = ((), (), s32[]{:S(2)}) async-start(), calls=%async_computation.24 | async-start | bytes 17301504
  1907.6 1206.5 %reduce-scatter.20.cloned.1.call-start = ((), (), s32[]{:S(2)}) async-start(), calls=%async_computation.21 | async-start | bytes 69206016 | tf_op jit(solution)/shard_map/reduce_scatter | solution.py:235
  1938.8 1884.2 %reduce-scatter.16.cloned.1.call-start = ((), (), s32[]{:S(2)}) async-start(), calls=%async_computation.19 | async-start | bytes 69206016 | tf_op jit(solution)/shard_map/reduce_scatter | solution.py:293
  1970.1 2561.6 %reduce-scatter.18.cloned.1.call-start = ((), (), s32[]{:S(2)}) async-start(), calls=%async_computation.20 | async-start | bytes 69206016 | tf_op jit(solution)/shard_map/reduce_scatter | solution.py:293
  1999.8 42.9 copy-start.39
  (51 other events, 260.9 us)
Sparse Core Ops, SparseCore 0:
  11.1 80.5 all-gather.7
  94.6 75.9 all-gather.9
  173.6 75.9 all-gather.11
  252.5 119.5 all-gather.13
  374.9 246.6 all-gather.15
  624.5 234.6 all-gather.17
  862.1 192.9 all-gather.19
  1206.6 209.3 reduce-scatter.13
  1844.6 185.5 reduce-scatter.21
  2032.9 183.9 reduce-scatter.23
  2219.8 184.3 reduce-scatter.25
  2407.0 707.0 reduce-scatter.19
  3117.1 705.8 reduce-scatter.15
  3825.8 705.8 reduce-scatter.17
where the time goes:
time: 4550 us; the launch traced here: 4540 us
  waiting for transfers between devices  2960 us (65%)
  matrix products  602 us (13%)
  blocking collectives  456 us (10%)
  local copies, waits for them, and re-layouts  266 us (6%)
  other arithmetic  207 us (5%)
    reduce_scatter x3, waiting for transfers between devices, on_device(): lax.psum_scatter((project_tn(inputs, grad_qproj), project_tn(inputs, grad...  1420 us
    reduce_scatter x1, waiting for transfers between devices, on_device(): lax.psum_scatter(project_tn(activated, grad_mproj), ('fsdp', 'seq'), scat...  710 us
    unnamed x17, waiting for transfers between devices  336 us
    all_gather x1, blocking collectives, on_device(): whole_pos = lax.all_gather(positions, 'seq', axis=2, tiled=True)  232 us
    all_gather x1, waiting for transfers between devices, on_device(): lax.all_gather(w_down, ('fsdp', 'seq'), axis=0, tiled=True)  160 us
    all_to_all x1, blocking collectives, on_device(): lax.all_to_all(grad_stack, 'seq', split_axis=2, concat_axis=3, tiled=True)  142 us
    dot_general x7, matrix products, project_tn(): lax.dot_general(former, latter, (((0,), (0,)), ((), ())), preferred_eleme...  126 us
    dot_general x7, matrix products, project_nt(): lax.dot_general(former, latter, (((1,), (1,)), ((), ())), preferred_eleme...  126 us
  transfers between devices with their start and end apart: 17, of which 12 were waited for; matrix products, arithmetic and copies ran while one was open for 20% of the time, Pallas kernels for 0%

commit v1 on v0

v1 whole, which is shorter than its diff:
```python
import functools

import jax
import jax.numpy as jnp
from jax import lax
from jax.experimental import pallas as pl
from jax.experimental.pallas import tpu as pltpu
from jax.sharding import PartitionSpec as P

HEADS = 16
HEAD_DIM = 128

EPSILON = 1e-06
THETA = 500000.0

BF16 = jnp.bfloat16
F32 = jnp.float32
BOTH = ("fsdp", "seq")

GROUP = 4

UNREAD = pl.BlockSpec(memory_space=pl.ANY)
NO_COST = pl.CostEstimate(flops=0, bytes_accessed=0, transcendentals=0)


def cost(flops):
    return pl.CostEstimate(flops=int(flops * 1), bytes_accessed=0, transcendentals=0)


def dot_nn(former, latter):
    return jnp.dot(former, latter, preferred_element_type=F32)


def dot_tn(former, latter):
    return lax.dot_general(former, latter, (((0,), (0,)), ((), ())), preferred_element_type=F32)


def dot_nt(former, latter):
    return lax.dot_general(former, latter, (((1,), (1,)), ((), ())), preferred_element_type=F32)


def inv_rms(values):
    return lax.rsqrt(jnp.mean(values * values, axis=-1, keepdims=True) + EPSILON)


def norm_back(incoming, values, factor, gain_row):
    weighted = incoming * gain_row
    inner_mean = jnp.mean(weighted * values, axis=-1, keepdims=True)
    result_grad = factor * (weighted - values * factor * factor * inner_mean)
    return (result_grad, jnp.sum(incoming * values * factor, axis=0))


def rope_tables(places_pos):
    half = HEAD_DIM // 2
    exponent = jnp.arange(0, half, dtype=F32) * (2.0 / HEAD_DIM)
    frequency = THETA ** (-exponent)
    angles = places_pos.astype(F32)[:, None] * frequency[None, :]
    cosine, sine = jnp.cos(angles), jnp.sin(angles)
    return (
        jnp.concatenate([cosine, cosine], axis=-1),
        jnp.concatenate([-sine, sine], axis=-1),
    )


def bits_of(size):
    return [1 << i for i in range(size.bit_length() - 1)]


def exchange(values, axis, bit):
    return lax.ppermute(values, axis, [(i, i ^ bit) for i in range(lax.axis_size(axis))])


def sum_small(values, axis):
    for bit in bits_of(lax.axis_size(axis)):
        values = values + exchange(values, axis, bit)
    return values


def after(values, *earlier):
    return pl.pallas_call(
        lambda *refs: None,
        in_specs=[UNREAD] * (1 + len(earlier)),
        out_specs=UNREAD,
        out_shape=jax.ShapeDtypeStruct(values.shape, values.dtype),
        input_output_aliases={0: 0},
        cost_estimate=NO_COST,
    )(values, *earlier)


def gather_group(values):
    near, far = 1, 2
    other = exchange(values, "seq", far)
    return jnp.concatenate(
        [values, other, exchange(values, "seq", near), exchange(other, "seq", near)]
    )


def halve(held, bits, axis, stride=1):
    for i, bit in enumerate(bits):
        sent = {m: exchange(v, axis, bit * stride) for m, v in held.items() if m & bit}
        held = {m: held[m].astype(F32) + sent[m ^ bit].astype(F32) for m in held if not m & bit}
        if i < len(bits) - 1:
            held = {m: v.astype(BF16) for m, v in held.items()}
    return held[0]


def scatter_near(values):
    rows = values.shape[0] // 2
    return values[:rows].astype(F32) + exchange(values[rows:], "seq", 1).astype(F32)


def scatter_far(half, *earlier):
    rows = half.shape[0] // 2
    return half[:rows] + after(exchange(half[rows:].astype(BF16), "seq", 2), *earlier).astype(F32)


def gather_outer(values):
    groups = lax.axis_size("seq") // GROUP
    own = lax.axis_index("seq") // GROUP
    found = {0: values}
    for bit in bits_of(groups):
        found |= {m ^ bit: exchange(v, "seq", bit * GROUP) for m, v in found.items()}
    blocks = []
    for i in range(groups):
        block = found[0]
        for m in range(1, groups):
            block = jnp.where((own ^ i) == m, found[m], block)
        blocks.append(block)
    return jnp.concatenate(blocks)


def scatter_outer(values):
    groups = lax.axis_size("seq") // GROUP
    own = lax.axis_index("seq") // GROUP
    rows = values.shape[0] // groups
    held = {
        m: lax.dynamic_slice_in_dim(values, (own ^ m) * rows, rows, 0) for m in range(groups)
    }
    return halve(held, bits_of(groups)[::-1], "seq", GROUP)


def shift(values, step):
    size = lax.axis_size("seq")
    pairs = [(i, i + 2 * step) for i in range(size) if 0 <= i + 2 * step < size]
    return lax.ppermute(values, "seq", pairs)


def scatter_line(values, *earlier):
    size, place = lax.axis_size("seq"), lax.axis_index("seq")
    pairs, pair, core = size // 2, place // 2, place % 2
    rows = values.shape[0] // size
    blocks = values.reshape(pairs, 2, rows, values.shape[1])
    sent = exchange(lax.dynamic_index_in_dim(blocks, 1 - core, 1, keepdims=False), "seq", 1)
    kept = lax.dynamic_index_in_dim(blocks, core, 1, keepdims=False)
    blocks = (kept.astype(F32) + sent.astype(F32)).astype(BF16)
    total = lax.dynamic_index_in_dim(blocks, pair, 0, keepdims=False).astype(F32)
    for step in (1, -1):
        moving = None
        for far in range(pairs - 1, 0, -1):
            target = jnp.clip(pair + step * far, 0, pairs - 1)
            block = lax.dynamic_index_in_dim(blocks, target, 0, keepdims=False)
            if moving is not None:
                block = (block.astype(F32) + moving.astype(F32)).astype(BF16)
            moving = shift(block, step)
        total = total + after(moving, *earlier).astype(F32)
    return total


def gather_placed(values, axis):
    size, own = lax.axis_size(axis), lax.axis_index(axis)
    bits, rows = bits_of(size), values.shape[0]
    parts = [(0, values, bits[::-1])]
    if axis == "fsdp":
        half = rows // 2
        parts = [(0, values[:half], bits), (half, values[half:], bits[::-1])]
    out = jnp.zeros((size * rows, values.shape[1]), values.dtype)
    for first, part, order in parts:
        found = {0: part}
        for bit in order:
            found |= {m ^ bit: exchange(v, axis, bit) for m, v in found.items()}
        for m, v in found.items():
            out = lax.dynamic_update_slice_in_dim(out, v, (own ^ m) * rows + first, 0)
    return out


def ordered(kernel, count, earlier):
    return lambda *refs: kernel(*refs[:count], *refs[count + len(earlier) :])


def gate_up_kernel(rows_ref, gate_ref, up_ref, gate_out, up_out, act_out):
    gate = dot_nn(rows_ref[...], gate_ref[...])
    up = dot_nn(rows_ref[...], up_ref[...])
    gate_out[...] = gate.astype(BF16)
    up_out[...] = up.astype(BF16)
    act_out[...] = (gate * jax.nn.sigmoid(gate) * up).astype(BF16)


def down_kernel(act_ref, down_ref, out_ref):
    out_ref[...] = dot_nn(act_ref[...], down_ref[...]).astype(BF16)


def act_back_kernel(grad_ref, down_ref, gate_ref, up_ref, dgate_ref, dup_ref):
    dact = dot_nt(grad_ref[...], down_ref[...])
    gate, up = gate_ref[...].astype(F32), up_ref[...].astype(F32)
    sigmoid = jax.nn.sigmoid(gate)
    dgate_ref[...] = (dact * up * sigmoid * (1.0 + gate * (1.0 - sigmoid))).astype(BF16)
    dup_ref[...] = (dact * gate * sigmoid).astype(BF16)


def hidden_back_kernel(dgate_ref, gate_ref, dup_ref, up_ref, out_ref):
    total = dot_nt(dgate_ref[...], gate_ref[...]) + dot_nt(dup_ref[...], up_ref[...])
    out_ref[...] = total.astype(BF16)


def weight_kernel(former_ref, latter_ref, out_ref):
    out_ref[...] = dot_tn(former_ref[...], latter_ref[...]).astype(BF16)


def held_rows(values):
    return pl.BlockSpec((min(1024, values.shape[0]), values.shape[1]), lambda j, i: (i, 0))


def cols_of(values, block):
    return pl.BlockSpec((values.shape[0], block), lambda j, i: (0, j))


def rows_of(values, block):
    return pl.BlockSpec((block, values.shape[1]), lambda j, i: (j, 0))


def tiles_of(values, block):
    return pl.BlockSpec((min(1024, values.shape[0]), block), lambda j, i: (i, j))


def by_columns(kernel, operands, specs, outs, cols, earlier, products=1):
    rows = operands[0].shape[0]
    high = min(1024, rows)
    return pl.pallas_call(
        ordered(kernel, len(operands), earlier),
        grid=(cols // 512, rows // high),
        in_specs=specs + [UNREAD] * len(earlier),
        out_specs=[pl.BlockSpec((high, 512), lambda j, i: (i, j))] * outs,
        out_shape=[jax.ShapeDtypeStruct((rows, cols), BF16)] * outs,
        compiler_params=pltpu.CompilerParams(vmem_limit_bytes=56 << 20),
        cost_estimate=cost(products * rows * cols * operands[0].shape[1] * 2),
    )(*operands, *earlier)


def gate_up(rows, gate, up, *earlier):
    specs = [held_rows(rows), cols_of(gate, 512), cols_of(up, 512)]
    return by_columns(gate_up_kernel, (rows, gate, up), specs, 3, gate.shape[1], earlier, 2)


def down(act, weight, *earlier):
    specs = [held_rows(act), cols_of(weight, 512)]
    return by_columns(down_kernel, (act, weight), specs, 1, weight.shape[1], earlier)[0]


def act_back(grads, weight, gate, up, *earlier):
    specs = [held_rows(grads), rows_of(weight, 512), tiles_of(gate, 512), tiles_of(up, 512)]
    return by_columns(act_back_kernel, (grads, weight, gate, up), specs, 2, gate.shape[1], earlier)


def hidden_back(dgate, gate, dup, up, *earlier):
    specs = [held_rows(dgate), rows_of(gate, 512), held_rows(dup), rows_of(up, 512)]
    return by_columns(hidden_back_kernel, (dgate, gate, dup, up), specs, 1, gate.shape[0], earlier, 2)[0]


def weight_grad(former, latter, *earlier):
    rows, cols = former.shape[1], latter.shape[1]
    block = min(512, rows)
    specs = [
        pl.BlockSpec((former.shape[0], block), lambda j: (0, j)),
        pl.BlockSpec(latter.shape, lambda j: (0, 0)),
    ]
    return pl.pallas_call(
        ordered(weight_kernel, 2, earlier),
        grid=(rows // block,),
        in_specs=specs + [UNREAD] * len(earlier),
        out_specs=pl.BlockSpec((block, cols), lambda j: (j, 0)),
        out_shape=jax.ShapeDtypeStruct((rows, cols), BF16),
        compiler_params=pltpu.CompilerParams(vmem_limit_bytes=56 << 20),
        cost_estimate=cost(former.shape[0] * rows * cols * 2),
    )(former, latter, *earlier)


def project_kernel(rows_ref, weight_ref, out_ref, squares_ref):
    width = weight_ref.shape[1] // 3
    proj = dot_nn(rows_ref[...], weight_ref[...])
    out_ref[...] = proj
    squares = (proj[:, : 2 * width] * proj[:, : 2 * width]).astype(BF16)
    part = lax.broadcasted_iota(jnp.int32, (8, 2 * width), 1) // width
    chosen = part == lax.broadcasted_iota(jnp.int32, (8, 2 * width), 0)
    squares_ref[...] = dot_nt(chosen.astype(BF16), squares)


def project(rows, weight):
    count, depth = rows.shape
    block = min(512, count)
    cols = weight.shape[1]
    return pl.pallas_call(
        project_kernel,
        grid=(count // block,),
        in_specs=[
            pl.BlockSpec((block, depth), lambda i: (i, 0)),
            pl.BlockSpec(weight.shape, lambda i: (0, 0)),
        ],
        out_specs=[
            pl.BlockSpec((block, cols), lambda i: (i, 0)),
            pl.BlockSpec((8, block), lambda i: (0, i)),
        ],
        out_shape=[
            jax.ShapeDtypeStruct((count, cols), F32),
            jax.ShapeDtypeStruct((8, count), F32),
        ],
        compiler_params=pltpu.CompilerParams(vmem_limit_bytes=48 << 20),
        cost_estimate=cost(count * depth * cols * 2),
    )(rows, weight)


def prepare_kernel(proj_ref, scale_ref, gain_ref, cos_ref, sin_ref, q_ref, k_ref, v_ref):
    width = q_ref.shape[1]
    cosine, sine = cos_ref[...], sin_ref[...]
    for part, out_ref in ((0, q_ref), (1, k_ref)):
        scale = scale_ref[:, part : part + 1]
        for low in range(0, width, HEAD_DIM):
            cols = slice(part * width + low, part * width + low + HEAD_DIM)
            normed = proj_ref[:, cols] * scale * gain_ref[:, cols]
            turned = normed * cosine + pltpu.roll(normed, HEAD_DIM // 2, 1) * sine
            out_ref[:, low : low + HEAD_DIM] = turned.astype(BF16)
    v_ref[...] = proj_ref[:, 2 * width :].astype(BF16)


def prepare(proj, scales, gains, cosine, sine):
    rows, width3 = proj.shape
    width = width3 // 3
    block = min(512, rows)
    by_rows = lambda cols: pl.BlockSpec((block, cols), lambda i: (i, 0))
    return pl.pallas_call(
        prepare_kernel,
        grid=(rows // block,),
        in_specs=[
            by_rows(width3),
            by_rows(2),
            pl.BlockSpec((1, 2 * width), lambda i: (0, 0)),
            by_rows(HEAD_DIM),
            by_rows(HEAD_DIM),
        ],
        out_specs=[by_rows(width)] * 3,
        out_shape=[jax.ShapeDtypeStruct((rows, width), BF16)] * 3,
        cost_estimate=cost(rows * width3 * 3600),
    )(proj, scales, gains, cosine, sine)


def unprepare_kernel(
    dq_ref, dk_ref, dv_ref, proj_ref, scale_ref, inner_ref, gain_ref, cos_ref, sin_ref, out_ref, sum_ref
):
    width = dq_ref.shape[1]

    @pl.when(pl.program_id(0) == 0)
    def _():
        sum_ref[...] = jnp.zeros_like(sum_ref)

    cosine, sine = cos_ref[...], sin_ref[...]
    for part, in_ref in ((0, dq_ref), (1, dk_ref)):
        scale = scale_ref[:, part : part + 1]
        inner = inner_ref[:, part : part + 1]
        for low in range(0, width, HEAD_DIM):
            cols = slice(part * width + low, part * width + low + HEAD_DIM)
            turned = in_ref[:, low : low + HEAD_DIM].astype(F32)
            normed = turned * cosine - pltpu.roll(turned, HEAD_DIM // 2, 1) * sine
            scaled = proj_ref[:, cols] * scale
            sum_ref[:, cols] += jnp.sum(normed * scaled, axis=0, keepdims=True)
            result = scale * (normed * gain_ref[:, cols] - scaled * inner)
            out_ref[:, cols] = result.astype(BF16)
    out_ref[:, 2 * width :] = dv_ref[...]


def unprepare(dq, dk, dv, proj, scales, inner, gains, cosine, sine):
    rows, width3 = proj.shape
    width = width3 // 3
    block = min(512, rows)
    by_rows = lambda cols: pl.BlockSpec((block, cols), lambda i: (i, 0))
    fixed = pl.BlockSpec((1, 2 * width), lambda i: (0, 0))
    return pl.pallas_call(
        unprepare_kernel,
        grid=(rows // block,),
        in_specs=[by_rows(width)] * 3
        + [by_rows(width3), by_rows(2), by_rows(2), fixed, by_rows(HEAD_DIM), by_rows(HEAD_DIM)],
        out_specs=[by_rows(width3), fixed],
        out_shape=[
            jax.ShapeDtypeStruct((rows, width3), BF16),
            jax.ShapeDtypeStruct((1, 2 * width), F32),
        ],
        cost_estimate=cost(rows * width3 * 4700),
    )(dq, dk, dv, proj, scales, inner, gains, cosine, sine)


def visible_mask(first, keys, rows, starts):
    key_ids = lax.broadcasted_iota(jnp.int32, (keys, rows), 0)
    query_ids = first + lax.broadcasted_iota(jnp.int32, (keys, rows), 1)
    return (key_ids <= query_ids) & (key_ids >= starts)


def forward_kernel(q_ref, k_ref, v_ref, start_ref, o_ref, lse_ref, *, factor, blocks):
    block = lse_ref.shape[-1]
    whole = blocks * block
    for turn in range(blocks):

        @pl.when(pl.program_id(2) == turn)
        def _():
            keys = (turn + 1) * block
            queries = q_ref[...].reshape(block, HEAD_DIM)
            keys_all = k_ref[...].reshape(whole, HEAD_DIM)[:keys]
            values = v_ref[...].reshape(whole, HEAD_DIM)[:keys]
            scores = dot_nt(keys_all, queries) * factor
            visible = visible_mask(turn * block, keys, block, start_ref[0])
            scores = jnp.where(visible, scores, -1e30)
            top = jnp.max(scores, axis=0, keepdims=True)
            expo = jnp.exp(scores - top)
            total = jnp.sum(expo, axis=0, keepdims=True)
            outcome = dot_tn(values, expo.astype(BF16)) / total
            o_ref[...] = outcome.T.astype(BF16).reshape(o_ref.shape)
            lse_ref[0, 0] = top + jnp.log(total)


def backward_kernel(
    q_ref, k_ref, v_ref, start_ref, do_ref, lse_ref, dq_ref, dk_ref, dv_ref, dk_sum, dv_sum, *, factor, blocks
):
    block = lse_ref.shape[-1]
    whole = blocks * block

    @pl.when(pl.program_id(2) == 0)
    def _():
        dk_sum[...] = jnp.zeros_like(dk_sum)
        dv_sum[...] = jnp.zeros_like(dv_sum)

    for turn in range(blocks):

        @pl.when(pl.program_id(2) == turn)
        def _():
            keys = (turn + 1) * block
            queries = q_ref[...].reshape(block, HEAD_DIM)
            grads = do_ref[...].reshape(block, HEAD_DIM)
            keys_all = k_ref[...].reshape(whole, HEAD_DIM)[:keys]
            values = v_ref[...].reshape(whole, HEAD_DIM)[:keys]
            scores = dot_nt(keys_all, queries) * factor
            visible = visible_mask(turn * block, keys, block, start_ref[0])
            soft = jnp.where(visible, jnp.exp(scores - lse_ref[0, 0]), 0.0)
            dv_sum[:keys] += dot_nn(soft.astype(BF16), grads)
            dsoft = dot_nt(values, grads)
            delta = jnp.sum(dsoft * soft, axis=0, keepdims=True)
            dscores = (soft * (dsoft - delta)).astype(BF16)
            dk_sum[:keys] += dot_nn(dscores, queries)
            dq = dot_tn(keys_all, dscores) * factor
            dq_ref[...] = dq.T.astype(BF16).reshape(dq_ref.shape)

    @pl.when(pl.program_id(2) == blocks - 1)
    def _():
        dk_ref[...] = (dk_sum[...] * factor).astype(BF16).reshape(dk_ref.shape)
        dv_ref[...] = dv_sum[...].astype(BF16).reshape(dv_ref.shape)


def attention_specs(shape):
    groups, count, rows, width = shape
    whole = groups * rows
    block = min(512, whole)
    per = block // rows
    some = pl.BlockSpec((per, 1, rows, HEAD_DIM), lambda b, h, i: (i, b, 0, h))
    every = pl.BlockSpec((groups, 1, rows, HEAD_DIM), lambda b, h, i: (0, b, 0, h))
    starts = pl.BlockSpec((1, 1, block), lambda b, h, i: (b, 0, i))
    sums = pl.BlockSpec((1, 1, 1, block), lambda b, h, i: (b, h, 0, i))
    heads = width // HEAD_DIM
    pairs = count * heads * whole * whole
    return some, every, starts, sums, (count, heads, whole // block), whole, pairs


def attend_forward(queries, keys, values, starts, factor, *earlier):
    some, every, start_spec, sums, grid, whole, pairs = attention_specs(queries.shape)
    return pl.pallas_call(
        ordered(functools.partial(forward_kernel, factor=factor, blocks=grid[2]), 4, earlier),
        grid=grid,
        in_specs=[some, every, every, start_spec] + [UNREAD] * len(earlier),
        out_specs=[some, sums],
        out_shape=[
            jax.ShapeDtypeStruct(queries.shape, BF16),
            jax.ShapeDtypeStruct((grid[0], grid[1], 1, whole), F32),
        ],
        compiler_params=pltpu.CompilerParams(vmem_limit_bytes=48 << 20),
        cost_estimate=cost(pairs * HEAD_DIM * 11),
    )(queries, keys, values, starts, *earlier)


def attend_backward(queries, keys, values, starts, grads, log_sums, factor, *earlier):
    some, every, start_spec, sums, grid, whole, pairs = attention_specs(queries.shape)
    return pl.pallas_call(
        ordered(functools.partial(backward_kernel, factor=factor, blocks=grid[2]), 6, earlier),
        grid=grid,
        in_specs=[some, every, every, start_spec, some, sums] + [UNREAD] * len(earlier),
        out_specs=[some, every, every],
        out_shape=[jax.ShapeDtypeStruct(queries.shape, BF16)] * 3,
        scratch_shapes=[pltpu.VMEM((whole, HEAD_DIM), F32)] * 2,
        compiler_params=pltpu.CompilerParams(vmem_limit_bytes=52 << 20),
        cost_estimate=cost(pairs * HEAD_DIM * 20),
    )(queries, keys, values, starts, grads, log_sums, *earlier)


def on_device(
    tokens,
    positions,
    out_grad,
    w_query,
    w_key,
    w_value,
    w_output,
    query_gain,
    key_gain,
    attn_gain,
    w_gate,
    w_up,
    w_down,
    mlp_gain,
):
    fsdp, seq = lax.axis_size("fsdp"), lax.axis_size("seq")
    row, place = lax.axis_index("fsdp"), lax.axis_index("seq")
    groups = seq // GROUP
    factor = HEAD_DIM ** (-0.5)
    count = tokens.shape[0] * tokens.shape[1]
    tok_count, width = tokens.shape[2], tokens.shape[3]
    own_rows = count * tok_count
    local_width = width // seq
    hidden_width = w_gate.shape[1] // GROUP
    share = w_query.shape[0]
    down_share = w_down.shape[0]
    head_shape = (seq, count, tok_count, local_width)

    inputs = tokens.reshape(own_rows, width)
    grad_rows = out_grad.reshape(own_rows, width).astype(F32)
    inputs_all = lax.all_gather(inputs, "seq", axis=0, tiled=True)

    qkv_weight = lax.all_to_all(
        jnp.stack([w_query, w_key, w_value]), "seq", split_axis=2, concat_axis=1, tiled=True
    )
    qkv_weight = jnp.moveaxis(qkv_weight, 0, 1).reshape(seq * share, 3 * local_width)
    qkv_weight = gather_placed(qkv_weight, "fsdp")

    own_gains = jnp.stack([query_gain, key_gain, attn_gain, mlp_gain]).astype(F32)
    small = jnp.concatenate([own_gains.reshape(-1), positions.reshape(-1).astype(F32)])
    small = lax.dynamic_update_index_in_dim(jnp.zeros((seq, small.shape[0]), F32), small, place, 0)
    small = sum_small(small, "seq")
    gains = small[:, : 4 * share].reshape(seq, 4, share)
    gains = lax.dynamic_update_index_in_dim(jnp.zeros((fsdp, seq, 4, share), F32), gains, row, 0)
    gains = jnp.moveaxis(sum_small(gains, "fsdp"), 2, 0).reshape(4, 1, width)
    a_gain, m_gain = gains[2], gains[3]
    qk_gain = lax.dynamic_slice_in_dim(gains[:2], place * local_width, local_width, 2)
    qk_gain = qk_gain.reshape(1, 2 * local_width)
    places = small[:, 4 * share :].reshape(seq, count, tok_count)
    cosine, sine = rope_tables(places.reshape(-1))
    order = jnp.arange(seq * tok_count, dtype=jnp.int32).reshape(seq, 1, tok_count)
    starts = jnp.moveaxis(order - places.astype(jnp.int32), 0, 1).reshape(count, 1, seq * tok_count)

    def columns(weight):
        part = weight.reshape(share, fsdp * groups, GROUP, down_share)
        part = jnp.moveaxis(part, 2, 0).reshape(1, GROUP, share, hidden_width)
        part = jnp.broadcast_to(part, (groups, GROUP, share, hidden_width))
        part = part.reshape(seq * share, hidden_width)
        return lax.all_to_all(part, "seq", split_axis=0, concat_axis=0, tiled=True)

    inputs_all = after(inputs_all, qkv_weight, cosine, sine, starts, gains)
    g_part = columns(after(w_gate, inputs_all))
    o_weight = lax.all_gather(w_output, BOTH, axis=0, tiled=True)
    proj, squares = project(inputs_all, qkv_weight)
    scales = lax.rsqrt(sum_small(squares[:2], "seq") / width + EPSILON).T
    rotated = prepare(proj, scales, qk_gain, cosine, sine)
    g_part = after(g_part, *rotated)
    u_part = columns(after(w_up, g_part))
    g_weight = lax.all_gather(g_part, "fsdp", axis=0, tiled=True)
    rotated = [v.reshape(head_shape) for v in rotated]
    attended, log_sums = attend_forward(*rotated, starts, factor)
    attended = after(attended, u_part)
    attn_rows = lax.all_to_all(
        attended.reshape(seq, own_rows, local_width), "seq", split_axis=0, concat_axis=0, tiled=True
    )
    attn_rows = jnp.moveaxis(attn_rows, 0, 1).reshape(own_rows, width)

    a_proj = dot_nn(attn_rows, o_weight)
    a_scale = inv_rms(a_proj)
    hidden = inputs.astype(F32) + a_proj * a_scale * a_gain
    d_part = gather_outer(after(w_down, u_part))
    u_weight, d_weight = (lax.all_gather(v, "fsdp", axis=0, tiled=True) for v in (u_part, d_part))
    hidden_low = gather_group(hidden.astype(BF16))
    gate, up, act = gate_up(hidden_low, g_weight, u_weight)
    m_proj = scatter_far(scatter_near(down(act, d_weight)))
    m_scale = inv_rms(m_proj)
    mixed = (hidden + m_proj * m_scale * m_gain).astype(BF16)

    grad_mproj, grad_mgain = norm_back(grad_rows, m_proj, m_scale, m_gain)
    grad_mproj = gather_group(grad_mproj.astype(BF16))

    def over_rows(part):
        return lax.psum_scatter(part, "fsdp", scatter_dimension=0, tiled=True)

    def columns_back(part):
        part = lax.all_to_all(part, "seq", split_axis=0, concat_axis=0, tiled=True).astype(F32)
        part = part.reshape(groups, GROUP, share, fsdp * groups, down_share).sum(axis=0)
        return jnp.moveaxis(part, 0, 2).reshape(share, -1)

    dgate, dup = act_back(grad_mproj, d_weight, gate, up)
    down_grad = weight_grad(act, grad_mproj, dgate)
    share_down = over_rows(down_grad)
    grads = hidden_back(dgate, g_weight, dup, u_weight, down_grad)
    gate_grad = weight_grad(hidden_low, dgate, grads)
    share_gate = over_rows(gate_grad)
    grads = scatter_near(grads)
    up_grad = weight_grad(hidden_low, dup, gate_grad, grads)
    share_up = over_rows(up_grad)
    grad_hidden = grad_rows + scatter_far(grads, up_grad)

    grad_aproj, grad_again = norm_back(grad_hidden, a_proj, a_scale, a_gain)
    grad_aproj = grad_aproj.astype(BF16)
    grad_attn = dot_nt(grad_aproj, o_weight).astype(BF16)
    grad_attn = jnp.moveaxis(grad_attn.reshape(own_rows, seq, local_width), 1, 0)
    grad_heads = lax.all_to_all(grad_attn, "seq", split_axis=0, concat_axis=0, tiled=True)
    o_grad = weight_grad(attn_rows, grad_aproj, grad_attn)
    share_output = over_rows(o_grad)
    grad_heads = after(grad_heads, o_grad)
    share_down = scatter_outer(after(share_down, grad_heads))
    dq, dk, dv = attend_backward(
        *rotated, starts, grad_heads.reshape(head_shape), log_sums, factor
    )
    dq = after(dq, share_down)
    dq, dk, dv = (v.reshape(seq * own_rows, local_width) for v in (dq, dk, dv))
    q_rot, k_rot = (v.reshape(seq * own_rows, local_width) for v in rotated[:2])
    inner = jnp.stack(
        [
            jnp.sum(dq.astype(F32) * q_rot.astype(F32), axis=1),
            jnp.sum(dk.astype(F32) * k_rot.astype(F32), axis=1),
        ]
    )
    inner = sum_small(inner, "seq") / width
    grad_qkv, gain_sums = unprepare(
        dq, dk, dv, proj, scales, inner.T, qk_gain, cosine, sine
    )
    partial = dot_nt(grad_qkv, qkv_weight).astype(BF16)
    qkv_grad = weight_grad(inputs_all, grad_qkv, partial)
    share_output = lax.psum_scatter(share_output, "seq", scatter_dimension=0, tiled=True).astype(F32)
    qkv_grad = after(qkv_grad, share_output)
    share_gate = columns_back(after(share_gate, grad_qkv))
    share_up = columns_back(after(share_up, grad_qkv))
    share_qkv = over_rows(qkv_grad)
    share_qkv = lax.all_to_all(
        share_qkv.reshape(seq, share, 3 * local_width), "seq", split_axis=0, concat_axis=0, tiled=True
    )
    share_qkv = share_qkv.reshape(seq, share, 3, local_width).transpose(2, 1, 0, 3)
    share_qkv = share_qkv.reshape(3, share, width).astype(F32)
    slots = lax.dynamic_update_slice_in_dim(
        jnp.zeros((2, width), F32), gain_sums.reshape(2, local_width), place * local_width, 1
    )
    slots = jnp.concatenate([slots, grad_again[None], grad_mgain[None]])
    slots = sum_small(sum_small(slots, "fsdp"), "seq")
    gain_grads = lax.dynamic_slice_in_dim(slots, (row * seq + place) * share, share, 1)
    grad_inputs = scatter_line(partial, share_gate, share_up, share_qkv, gain_grads)
    input_grad = (grad_hidden + grad_inputs).astype(BF16)
    return (
        mixed.reshape(tokens.shape),
        input_grad.reshape(tokens.shape),
        share_qkv[0],
        share_qkv[1],
        share_qkv[2],
        share_output,
        gain_grads[0],
        gain_grads[1],
        gain_grads[2],
        share_gate,
        share_up,
        share_down,
        gain_grads[3],
    )


def solution(mesh):
    rows = P(BOTH, None)
    flat = P(BOTH)
    acts = P(None, "fsdp", "seq", None)
    return jax.shard_map(
        on_device,
        mesh=mesh,
        in_specs=(acts, P(None, "fsdp", "seq"), acts, rows, rows, rows, rows, flat, flat, flat)
        + (rows, rows, rows, flat),
        out_specs=(acts, acts, rows, rows, rows, rows, flat, flat, flat, rows, rows, rows, flat),
        check_vma=False,
    )
```

time: 4550 us -> 1490 us (0.33)
  waiting for transfers between devices: 2960 us -> 654 us
  matrix products: 602 us -> 36.5 us
  blocking collectives: 456 us -> 52.2 us
  Pallas kernels: 0 us -> 357 us
  local copies, waits for them, and re-layouts: 266 us -> 134 us
  starting transfers between devices: 14.4 us -> 113 us
  other arithmetic: 207 us -> 117 us
    reduce_scatter x4 -> x6, waiting for transfers between devices: 2130 us -> 42.7 us  [the longest x5 42.7 us: over_rows(): return lax.psum_scatter(part, 'fsdp', scatter_dimension=0, tiled=True)]
    dot_general x49 -> x3, matrix products: 602 us -> 36.5 us  [the longest x2 28.2 us: dot_nt(): lax.dot_general(former, latter, (((1,), (1,)), ((), ())), preferred_eleme...]
    ppermute x0 -> x41, waiting for transfers between devices: none -> 462 us  [the longest x35 342 us: exchange(): lax.ppermute(values, axis, [(i, i ^ bit) for i in range(lax.axis_size(axi...]
    pallas_call x0 -> x30, Pallas kernels: none -> 357 us  [the longest x4 146 us: by_columns(): pl.pallas_call(ordered(kernel, len(operands), earlier), grid=(cols // 512...]
    unnamed x17 -> x11, waiting for transfers between devices: 336 us -> 1.54 us
    all_gather x7 -> x5, waiting for transfers between devices: 346 us -> 75.6 us  [the longest x1 68.9 us: on_device(): inputs_all = lax.all_gather(inputs, 'seq', axis=0, tiled=True)]
    all_gather x1 -> x0, blocking collectives: 232 us -> none  [on_device(): whole_pos = lax.all_gather(positions, 'seq', axis=2, tiled=True)]
    all_to_all x1, blocking collectives: 142 us -> 52.2 us  [columns(): return lax.all_to_all(part, 'seq', split_axis=0, concat_axis=0, tiled=True)]
  transfers between devices with their start and end apart: 17 -> 59, of which waited for: 12 -> 36; matrix products, arithmetic and copies ran while one was open for 20% -> 16% of each run, Pallas kernels for 0% -> 19%
where the time goes in v1:
time: 1490 us; the launch traced here: 1480 us
  waiting for transfers between devices  654 us (44%)
  Pallas kernels  357 us (24%)
  local copies, waits for them, and re-layouts  134 us (9%)
  other arithmetic  117 us (8%)
  starting transfers between devices  113 us (8%)
  blocking collectives  52.2 us (4%)
  matrix products  36.5 us (2%)
  between operations  15.4 us (1%)
    ppermute x35, waiting for transfers between devices, exchange(): lax.ppermute(values, axis, [(i, i ^ bit) for i in range(lax.axis_size(axi...  342 us
    pallas_call x4, Pallas kernels, by_columns(): pl.pallas_call(ordered(kernel, len(operands), earlier), grid=(cols // 512...  146 us
    ppermute x6, waiting for transfers between devices, shift(): return lax.ppermute(values, 'seq', pairs)  120 us
    pallas_call x5, Pallas kernels, weight_grad(): pl.pallas_call(ordered(weight_kernel, 2, earlier), grid=(rows // block,),...  98.7 us
    all_gather x1, waiting for transfers between devices, on_device(): inputs_all = lax.all_gather(inputs, 'seq', axis=0, tiled=True)  68.9 us
    all_to_all x1, blocking collectives, columns(): return lax.all_to_all(part, 'seq', split_axis=0, concat_axis=0, tiled=True)  52.2 us
    all_to_all x1, waiting for transfers between devices, on_device(): lax.all_to_all(grad_attn, 'seq', split_axis=0, concat_axis=0, tiled=True)  49 us
    pallas_call x1, Pallas kernels, attend_backward(): pl.pallas_call(ordered(functools.partial(backward_kernel, factor=factor,...  43.5 us
  transfers between devices with their start and end apart: 59, of which 36 were waited for; matrix products, arithmetic and copies ran while one was open for 16% of the time, Pallas kernels for 19%

profile of v1, /device:TPU:0, one launch (start us, length us, event | category | flops | bytes accessed | tf_op | source)
XLA Modules:
  0.0 1479.4 jit_solution(5819622573449172467)
XLA Ops:
  26.8 25.2 %collective-permute-done.7 = f32[8,768]{1,0:T(8,128)S(1)} collective-permute-done((f32[8,768]{1,0:T(8,128)S(1)}, f32[8,768]{1,0:T(8,128)S(1)}, u32[]{:S(2)}, u32[]{:S(2)}) %collective-permute-start.7) | collective-permute-done | bytes 24608 | tf_op jit(solution)/shard_map/ppermute | solution.py:70
  56.5 15.5 %collective-permute-done.8 = f32[8,768]{1,0:T(8,128)S(1)} collective-permute-done((f32[8,768]{1,0:T(8,128)S(1)}, f32[8,768]{1,0:T(8,128)S(1)}, u32[]{:S(2)}, u32[]{:S(2)}) %collective-permute-start.8) | collective-permute-done | bytes 24608 | tf_op jit(solution)/shard_map/ppermute | solution.py:70
  73.7 7.5 fusion.16
  114.8 68.9 %all-gather.6.cloned.1.call-done.refs_0_ = bf16[4096,2048]{1,0:T(8,128)(2,1)} async-done(((bf16[512,2048]{1,0:T(8,128)(2,1)}), bf16[4096,2048]{1,0:T(8,128)(2,1)}) %all-gather.6.cloned.1.call-update) | async-done | bytes 16777232 | tf_op jit(solution)/shard_map/all_gather | solution.py:539
  194.6 19.2 %shard_map.238 = (f32[4096,768]{1,0:T(8,128)}, f32[8,4096]{1,0:T(8,128)S(1)}) custom-call(bf16[4096,2048]{1,0:T(8,128)(2,1)} %shard_map.237.rows_ref.refs_1_.refs_0_, bf16[2048,768]{1,0:T(8,128)(2,1)S(1)} %copy-done.1), custom_call_target="tpu_custom_call" | custom-call | flops 12884901888 | tf_op jit(solution)/shard_map/pallas_call | solution.py:301
  219.1 26.5 %collective-permute-done.12 = f32[2,4096]{1,0:T(2,128)S(1)} collective-permute-done((f32[2,4096]{1,0:T(2,128)S(1)}, f32[2,4096]{1,0:T(2,128)S(1)}, u32[]{:S(2)}, u32[]{:S(2)}) %collective-permute-start.12) | collective-permute-done | bytes 32800 | tf_op jit(solution)/shard_map/ppermute | solution.py:70
  269.9 11.5 shard_map.239
  290.4 52.2 %all_to_all.73 = bf16[8,64,2048]{2,1,0:T(8,128)(2,1)} all-to-all(bf16[8,64,2048]{2,1,0:T(8,128)(2,1)S(1)} %bitcast.182), channel_id=1, replica_groups=mesh['fsdp'=4,'seq'=8] {'seq'}, dimensions={0} | all-to-all | bytes 4194304 | tf_op jit(solution)/shard_map/all_to_all | solution.py:567
  344.9 23.0 %shard_map.240 = (bf16[8,2,256,256]{3,2,1,0:T(8,128)(2,1)S(1)}, f32[2,2,1,2048]{3,2,1,0:T(1,128)S(1)}) custom-call(bf16[8,2,256,256]{3,2,1,0:T(8,128)(2,1)S(1)} %bitcast.157, bf16[8,2,256,256]{3,2,1,0:T(8,128)(2,1)} %bitcast.169, bf16[8,2,256,256]{3,2,1,0:T(8,128)(2,1)} %bitcast.188, s32[2,1,2048]{2,1,0:T(1,128)S(1)} %copy-done.4), custom_call_target="tpu_custom_call" | custom-call | flops 23622320128 | tf_op jit(solution)/shard_map/pallas_call | solution.py:480
  373.7 39.1 %collective-permute-done.17 = bf16[256,2048]{1,0:T(8,128)(2,1)} collective-permute-done((bf16[256,2048]{1,0:T(8,128)(2,1)}, bf16[256,2048]{1,0:T(8,128)(2,1)}, u32[]{:S(2)}, u32[]{:S(2)}) %collective-permute-start.17) | collective-permute-done | bytes 1048608 | tf_op jit(solution)/shard_map/ppermute | solution.py:70
  416.4 18.8 %all-to-all-done.3 = bf16[8,512,256]{2,1,0:T(8,128)(2,1)} async-done(((bf16[8,512,256]{2,1,0:T(8,128)(2,1)}), bf16[8,512,256]{2,1,0:T(8,128)(2,1)}, u32[]{:S(2)}, u32[]{:S(2)}) %all-to-all-start.3) | async-done | bytes 2097184 | tf_op jit(solution)/shard_map/all_to_all | solution.py:581
  438.3 8.3 multiply_reduce_fusion.5
  448.6 47.5 %collective-permute-done.14 = bf16[512,2048]{1,0:T(8,128)(2,1)S(1)} collective-permute-done((bf16[512,2048]{1,0:T(8,128)(2,1)S(1)}, bf16[512,2048]{1,0:T(8,128)(2,1)S(1)}, u32[]{:S(2)}, u32[]{:S(2)}) %collective-permute-start.14) | collective-permute-done | bytes 2097184 | tf_op jit(solution)/shard_map/ppermute | solution.py:70
  504.5 42.6 %shard_map.245 = (bf16[2048,2048]{1,0:T(8,128)(2,1)}, bf16[2048,2048]{1,0:T(8,128)(2,1)}, bf16[2048,2048]{1,0:T(8,128)(2,1)}) custom-call(bf16[2048,2048]{1,0:T(8,128)(2,1)} %pad_maximum_fusion.refs_0_, bf16[2048,2048]{1,0:T(8,128)(2,1)} %all-gather.10.cloned.1.call-done.refs_1_, bf16[2048,2048]{1,0:T(8,128)(2,1)} %all-gather.12.cloned.1.call-done.refs_2_.refs_3_), custom_call_target="tpu_custom_call" | custom-call | flops 34359738368 | tf_op jit(solution)/shard_map/pallas_call | solution.py:238
  547.1 6.6 all-gather.14.cloned.1.call-done.refs_1_
  553.7 25.3 %shard_map.247 = bf16[2048,2048]{1,0:T(8,128)(2,1)} custom-call(bf16[2048,2048]{1,0:T(8,128)(2,1)} %get-tuple-element.36.refs_0_, bf16[2048,2048]{1,0:T(8,128)(2,1)} %all-gather.14.cloned.1.call-done.refs_1_), custom_call_target="tpu_custom_call" | custom-call | flops 17179869184 | tf_op jit(solution)/shard_map/pallas_call | solution.py:238
  581.7 7.3 collective-permute-done.18
  599.6 46.4 %collective-permute-done.19.refs_0_ = bf16[512,2048]{1,0:T(8,128)(2,1)} collective-permute-done((bf16[512,2048]{1,0:T(8,128)(2,1)}, bf16[512,2048]{1,0:T(8,128)(2,1)}, u32[]{:S(2)}, u32[]{:S(2)}) %collective-permute-start.19) | collective-permute-done | bytes 2097184 | tf_op jit(solution)/shard_map/ppermute | solution.py:70
  649.7 6.2 fusion.7
  662.7 45.3 %collective-permute-done.20 = bf16[512,2048]{1,0:T(8,128)(2,1)S(1)} collective-permute-done((bf16[512,2048]{1,0:T(8,128)(2,1)S(1)}, bf16[512,2048]{1,0:T(8,128)(2,1)S(1)}, u32[]{:S(2)}, u32[]{:S(2)}) %collective-permute-start.20) | collective-permute-done | bytes 2097184 | tf_op jit(solution)/shard_map/ppermute | solution.py:70
  716.1 33.6 %shard_map.249 = (bf16[2048,2048]{1,0:T(8,128)(2,1)}, bf16[2048,2048]{1,0:T(8,128)(2,1)}) custom-call(bf16[2048,2048]{1,0:T(8,128)(2,1)} %pad_maximum_fusion.1.refs_0_.refs_1_, bf16[2048,2048]{1,0:T(8,128)(2,1)} %all-gather.14.cloned.1.call-done.refs_1_, bf16[2048,2048]{1,0:T(8,128)(2,1)} %get-tuple-element.37.refs_2_, ...), custom_call_target="tpu_custom_call" | custom-call | flops 17179869184 | tf_op jit(solution)/shard_map/pallas_call | solution.py:238
  749.7 23.5 %shard_map.250.refs_4_ = bf16[2048,2048]{1,0:T(8,128)(2,1)} custom-call(bf16[2048,2048]{1,0:T(8,128)(2,1)} %get-tuple-element.36.refs_0_, bf16[2048,2048]{1,0:T(8,128)(2,1)} %pad_maximum_fusion.1.refs_0_.refs_1_, bf16[2048,2048]{1,0:T(8,128)(2,1)} %get-tuple-element.39.refs_2_.refs_0_.refs_1_), custom_call_target="tpu_custom_call" | custom-call | flops 17179869184 | tf_op jit(solution)/shard_map/pallas_call | solution.py:276
  773.3 44.6 %shard_map.251.refs_2_ = bf16[2048,2048]{1,0:T(8,128)(2,1)} custom-call(bf16[2048,2048]{1,0:T(8,128)(2,1)} %get-tuple-element.39.refs_2_.refs_0_.refs_1_, bf16[2048,2048]{1,0:T(8,128)(2,1)} %all-gather.10.cloned.1.call-done.refs_1_, bf16[2048,2048]{1,0:T(8,128)(2,1)} %get-tuple-element.40.refs_2_.refs_1_, ...), custom_call_target="tpu_custom_call" | custom-call | flops 34359738368 | tf_op jit(solution)/shard_map/pallas_call | solution.py:238
  820.9 7.0 collective-permute-done.23
  838.5 23.7 %shard_map.252.refs_2_ = bf16[2048,2048]{1,0:T(8,128)(2,1)} custom-call(bf16[2048,2048]{1,0:T(8,128)(2,1)} %pad_maximum_fusion.refs_0_, bf16[2048,2048]{1,0:T(8,128)(2,1)} %get-tuple-element.39.refs_2_.refs_0_.refs_1_, bf16[2048,2048]{1,0:T(8,128)(2,1)} %shard_map.251.refs_2_), custom_call_target="tpu_custom_call" | custom-call | flops 17179869184 | tf_op jit(solution)/shard_map/pallas_call | solution.py:276
  862.3 23.5 %shard_map.253.refs_1_ = bf16[2048,2048]{1,0:T(8,128)(2,1)} custom-call(bf16[2048,2048]{1,0:T(8,128)(2,1)} %pad_maximum_fusion.refs_0_, bf16[2048,2048]{1,0:T(8,128)(2,1)} %get-tuple-element.40.refs_2_.refs_1_, bf16[2048,2048]{1,0:T(8,128)(2,1)} %shard_map.252.refs_2_, f32[1024,2048]{1,0:T(8,128)} %copy-done.12), custom_call_target="tpu_custom_call" | custom-call | flops 17179869184 | tf_op jit(solution)/shard_map/pallas_call | solution.py:276
  885.8 6.7 multiply_reduce_fusion
  896.9 9.4 convolution_convert_fusion.1
  914.1 8.5 shard_map.255.refs_1_
  927.8 49.0 %all-to-all-done.4.refs_0_ = bf16[8,512,256]{2,1,0:T(8,128)(2,1)} async-done(((bf16[8,512,256]{2,1,0:T(8,128)(2,1)}), bf16[8,512,256]{2,1,0:T(8,128)(2,1)}, u32[]{:S(2)}, u32[]{:S(2)}) %all-to-all-start.4) | async-done | bytes 2097184 | tf_op jit(solution)/shard_map/all_to_all | solution.py:623
  979.2 29.3 %reduce-scatter.13.cloned.1.call-done = bf16[512,2048]{1,0:T(8,128)(2,1)} async-done(((bf16[2048,2048]{1,0:T(8,128)(2,1)}), bf16[512,2048]{1,0:T(8,128)(2,1)}) %reduce-scatter.13.cloned.1.call-update) | async-done | bytes 2097168 | tf_op jit(solution)/shard_map/reduce_scatter | solution.py:601
  1008.6 43.5 %shard_map.257 = (bf16[8,2,256,256]{3,2,1,0:T(8,128)(2,1)}, bf16[8,2,256,256]{3,2,1,0:T(8,128)(2,1)}, bf16[8,2,256,256]{3,2,1,0:T(8,128)(2,1)}) custom-call(bf16[8,2,256,256]{3,2,1,0:T(8,128)(2,1)} %bitcast.156, bf16[8,2,256,256]{3,2,1,0:T(8,128)(2,1)} %bitcast.170, bf16[8,2,256,256]{3,2,1,0:T(8,128)(2,1)} %bitcast.189, s32[2,1,2048]{2,1,0:T(1,128)S(1)} %copy-done.4, ...), custom_call_target="tpu_custom_call" | custom-call | flops 42949672960 | tf_op jit(solution)/shard_map/pallas_call | solution.py:496
  1084.8 15.0 %shard_map.260 = (bf16[4096,768]{1,0:T(8,128)(2,1)}, f32[1,512]{1,0:T(1,128)}) custom-call(bf16[4096,256]{1,0:T(8,128)(2,1)} %bitcast.174, bf16[4096,256]{1,0:T(8,128)(2,1)} %bitcast.193, bf16[4096,256]{1,0:T(8,128)(2,1)} %bitcast.223, f32[4096,768]{1,0:T(8,128)} %get-tuple-element.30.proj_ref, f32[4096,2]{1,0:T(8,128)} %rsqrt_bitcast_fusion.scale_ref, ...), custom_call_target="tpu_custom_call" | custom-call | flops 14784921600 | tf_op jit(solution)/shard_map/pallas_call | solution.py:385
  1099.8 18.8 %convolution_convert_fusion.refs_2_ = bf16[4096,2048]{1,0:T(8,128)(2,1)} fusion(bf16[4096,768]{1,0:T(8,128)(2,1)} %get-tuple-element.45.refs_1_, bf16[2048,768]{1,0:T(8,128)(2,1)S(1)} %copy-done.1), kind=kOutput, calls=%fused_computation.2 | convolution fusion | flops 12893290496 | bytes 26214400 | tf_op jit(solution)/shard_map/dot_general | solution.py:39
  1118.6 8.5 dynamic-slice_bitcast_fusion
  1127.1 13.5 collective-permute-done.29
  1140.6 7.6 fusion
  1161.5 19.4 %shard_map.263.refs_0_ = bf16[2048,768]{1,0:T(8,128)(2,1)} custom-call(bf16[4096,2048]{1,0:T(8,128)(2,1)} %shard_map.237.rows_ref.refs_1_.refs_0_, bf16[4096,768]{1,0:T(8,128)(2,1)} %get-tuple-element.45.refs_1_, bf16[4096,2048]{1,0:T(8,128)(2,1)} %convolution_convert_fusion.refs_2_), custom_call_target="tpu_custom_call" | custom-call | flops 12884901888 | tf_op jit(solution)/shard_map/pallas_call | solution.py:276
  1184.0 18.8 %collective-permute-done.30 = bf16[512,2048]{1,0:T(8,128)(2,1)} collective-permute-done((bf16[512,2048]{1,0:T(8,128)(2,1)}, bf16[512,2048]{1,0:T(8,128)(2,1)}, u32[]{:S(2)}, u32[]{:S(2)}) %collective-permute-start.30) | collective-permute-done | bytes 2097184 | tf_op jit(solution)/shard_map/ppermute | solution.py:145
  1207.2 11.5 collective-permute-start.31
  1218.7 13.3 reduce-scatter.11.cloned.1.call-done.refs_0_
  1236.6 16.7 %all-to-all-start.6 = ((bf16[8,64,2048]{2,1,0:T(8,128)(2,1)}), bf16[8,64,2048]{2,1,0:T(8,128)(2,1)}, u32[]{:S(2)}, u32[]{:S(2)}) async-start(bf16[8,64,2048]{2,1,0:T(8,128)(2,1)} %bitcast.173), calls=%async_computation.9 | async-start | bytes 4194304 | tf_op jit(solution)/shard_map/all_to_all | solution.py:604
  1253.3 28.2 %collective-permute-done.31 = bf16[512,2048]{1,0:T(8,128)(2,1)} collective-permute-done((bf16[512,2048]{1,0:T(8,128)(2,1)}, bf16[512,2048]{1,0:T(8,128)(2,1)}, u32[]{:S(2)}, u32[]{:S(2)}) %collective-permute-start.31) | collective-permute-done | bytes 2097184 | tf_op jit(solution)/shard_map/ppermute | solution.py:145
  1281.5 7.8 fusion.11
  1290.6 73.0 %collective-permute-done.39 = bf16[512,2048]{1,0:T(8,128)(2,1)} collective-permute-done((bf16[512,2048]{1,0:T(8,128)(2,1)}, bf16[512,2048]{1,0:T(8,128)(2,1)}, u32[]{:S(2)}, u32[]{:S(2)}) %collective-permute-start.39) | collective-permute-done | bytes 2097184 | tf_op jit(solution)/shard_map/ppermute | solution.py:145
  1369.4 6.9 collective-permute-start.32
  1393.7 31.3 %collective-permute-done.36 = f32[4,2048]{1,0:T(4,128)S(1)} collective-permute-done((f32[4,2048]{1,0:T(4,128)S(1)}, f32[4,2048]{1,0:T(4,128)S(1)}, u32[]{:S(2)}, u32[]{:S(2)}) %collective-permute-start.36) | collective-permute-done | bytes 32800 | tf_op jit(solution)/shard_map/ppermute | solution.py:70
  1465.4 7.0 fusion.14
  (332 shorter events, 321.6 us)
Async XLA Ops:
  7.2 176.5 %all-gather.6.cloned.1.call-start = ((), (), s32[]{:S(2)}) async-start(), calls=%async_computation.14 | async-start | bytes 18874368 | tf_op jit(solution)/shard_map/all_gather | solution.py:539
  13.1 425.2 %all-gather.8.cloned.1.call-start = ((), (), s32[]{:S(2)}) async-start(), calls=%async_computation.15 | async-start | bytes 8650752 | tf_op jit(solution)/shard_map/all_gather | solution.py:571
  14.2 10.4 collective-permute-start.6
  18.6 65.8 %all-to-all-start = ((bf16[8,2,24576]{2,1,0:T(2,128)(2,1)}), bf16[8,2,24576]{2,1,0:T(2,128)(2,1)S(1)}, u32[]{:S(2)}, u32[]{:S(2)}) async-start(bf16[8,2,24576]{2,1,0:T(2,128)(2,1)} %reshape.275), calls=%async_computation | async-start | bytes 1572864 | tf_op jit(solution)/shard_map/all_to_all | solution.py:541
  24.7 27.3 %collective-permute-start.7 = (f32[8,768]{1,0:T(8,128)S(1)}, f32[8,768]{1,0:T(8,128)S(1)}, u32[]{:S(2)}, u32[]{:S(2)}) collective-permute-start(f32[8,768]{1,0:T(8,128)S(1)} %add.264), channel_id=1, source_target_pairs={{0,2},{1,3},{2,0},{3,1},{4,6},{5,7},{6,4},{7,5},{8,10},{9,11},{10,... | collective-permute-start | bytes 73736 | tf_op jit(solution)/shard_map/ppermute | solution.py:70
  52.0 20.0 %collective-permute-start.8 = (f32[8,768]{1,0:T(8,128)S(1)}, f32[8,768]{1,0:T(8,128)S(1)}, u32[]{:S(2)}, u32[]{:S(2)}) collective-permute-start(f32[8,768]{1,0:T(8,128)S(1)} %add.265), channel_id=1, source_target_pairs={{0,4},{1,5},{2,6},{3,7},{4,0},{5,1},{6,2},{7,3},{8,12},{9,13},{10,... | collective-permute-start | bytes 73736 | tf_op jit(solution)/shard_map/ppermute | solution.py:70
  72.2 16.3 %collective-permute-start.9 = (f32[4,8,4,64]{3,2,1,0:T(4,128)S(1)}, f32[4,8,4,64]{3,2,1,0:T(4,128)S(1)}, u32[]{:S(2)}, u32[]{:S(2)}) collective-permute-start(f32[4,8,4,64]{3,2,1,0:T(4,128)S(1)} %constant_dynamic-update-slice_fusion.1), channel_id=1, source_target_pairs={{0,8},{8,0},{16,24},{24,16},{1,9},{9,1},{17,25},{25,17},{2,10},{10... | collective-permute-start | bytes 98312 | tf_op jit(solution)/shard_map/ppermute | solution.py:70
  87.9 10.8 collective-permute-start
  88.4 12.9 collective-permute-start.10
  90.4 14.1 collective-permute-start.3
  91.6 15.6 %collective-permute-start.1 = (bf16[256,768]{1,0:T(8,128)(2,1)}, bf16[256,768]{1,0:T(8,128)(2,1)}, u32[]{:S(2)}, u32[]{:S(2)}) collective-permute-start(bf16[256,768]{1,0:T(8,128)(2,1)} %copy.207), channel_id=1, source_target_pairs={{0,16},{8,24},{16,0},{24,8},{1,17},{9,25},{17,1},{25,9},{2,18},{10... | collective-permute-start | bytes 1179656 | tf_op jit(solution)/shard_map/ppermute | solution.py:70
  98.7 12.7 collective-permute-start.2
  102.7 10.8 collective-permute-start.4
  104.5 10.2 collective-permute-start.5
  190.0 91.4 %all-to-all-start.1 = ((bf16[8,64,2048]{2,1,0:T(8,128)(2,1)}), bf16[8,64,2048]{2,1,0:T(8,128)(2,1)}, u32[]{:S(2)}, u32[]{:S(2)}) async-start(bf16[8,64,2048]{2,1,0:T(8,128)(2,1)} %bitcast.177), calls=%async_computation.1 | async-start | bytes 4194304 | tf_op jit(solution)/shard_map/all_to_all | solution.py:567
  194.3 310.2 %all-gather.10.cloned.1.call-start = ((), (), s32[]{:S(2)}) async-start(), calls=%async_computation.16 | async-start | bytes 10485760 | tf_op jit(solution)/shard_map/all_gather | solution.py:577
  215.1 30.5 %collective-permute-start.12 = (f32[2,4096]{1,0:T(2,128)S(1)}, f32[2,4096]{1,0:T(2,128)S(1)}, u32[]{:S(2)}, u32[]{:S(2)}) collective-permute-start(f32[2,4096]{1,0:T(2,128)S(1)} %slice_add_fusion.2), channel_id=1, source_target_pairs={{0,2},{1,3},{2,0},{3,1},{4,6},{5,7},{6,4},{7,5},{8,10},{9,11},{10,... | collective-permute-start | bytes 98312 | tf_op jit(solution)/shard_map/ppermute | solution.py:70
  253.5 10.5 collective-permute-start.13
  281.4 223.1 %all-gather.12.cloned.1.call-start = ((), (), s32[]{:S(2)}) async-start(), calls=%async_computation.17 | async-start | bytes 10485760 | tf_op jit(solution)/shard_map/all_gather | solution.py:590
  342.6 70.1 %collective-permute-start.17 = (bf16[256,2048]{1,0:T(8,128)(2,1)}, bf16[256,2048]{1,0:T(8,128)(2,1)}, u32[]{:S(2)}, u32[]{:S(2)}) collective-permute-start(bf16[256,2048]{1,0:T(8,128)(2,1)} %shard_map.246), channel_id=1, source_target_pairs={{0,4},{1,5},{2,6},{3,7},{4,0},{5,1},{6,2},{7,3},{8,12},{9,13},{10,... | collective-permute-start | bytes 3145736 | tf_op jit(solution)/shard_map/ppermute | solution.py:70
  369.2 65.9 %all-to-all-start.3 = ((bf16[8,512,256]{2,1,0:T(8,128)(2,1)}), bf16[8,512,256]{2,1,0:T(8,128)(2,1)}, u32[]{:S(2)}, u32[]{:S(2)}) async-start(bf16[8,512,256]{2,1,0:T(8,128)(2,1)} %bitcast.158), calls=%async_computation.3 | async-start | bytes 4194304 | tf_op jit(solution)/shard_map/all_to_all | solution.py:581
  373.6 180.1 %all-gather.14.cloned.1.call-start = ((), (), s32[]{:S(2)}) async-start(), calls=%async_computation.18 | async-start | bytes 10485760 | tf_op jit(solution)/shard_map/all_gather | solution.py:590
  416.1 560.7 %reduce-scatter.7.cloned.1.call-start = ((), (), s32[]{:S(2)}) async-start(), calls=%async_computation.19 | async-start | bytes 10485760 | tf_op jit(solution)/shard_map/reduce_scatter | solution.py:601
  448.6 47.6 %collective-permute-start.14 = (bf16[512,2048]{1,0:T(8,128)(2,1)S(1)}, bf16[512,2048]{1,0:T(8,128)(2,1)S(1)}, u32[]{:S(2)}, u32[]{:S(2)}) collective-permute-start(bf16[512,2048]{1,0:T(8,128)(2,1)S(1)} %fusion.15), channel_id=1, source_target_pairs={{0,2},{1,3},{2,0},{3,1},{4,6},{5,7},{6,4},{7,5},{8,10},{9,11},{10,... | collective-permute-start | bytes 6291464 | tf_op jit(solution)/shard_map/ppermute | solution.py:70
  448.6 47.6 %collective-permute-start.15 = (bf16[512,2048]{1,0:T(8,128)(2,1)S(1)}, bf16[512,2048]{1,0:T(8,128)(2,1)S(1)}, u32[]{:S(2)}, u32[]{:S(2)}) collective-permute-start(bf16[512,2048]{1,0:T(8,128)(2,1)S(1)} %fusion.15), channel_id=1, source_target_pairs={{0,1},{1,0},{2,3},{3,2},{4,5},{5,4},{6,7},{7,6},{8,9},{9,8},{10,11... | collective-permute-start | bytes 6291464 | tf_op jit(solution)/shard_map/ppermute | solution.py:70
  581.7 7.4 collective-permute-start.18
  598.0 48.0 %collective-permute-start.19 = (bf16[512,2048]{1,0:T(8,128)(2,1)}, bf16[512,2048]{1,0:T(8,128)(2,1)}, u32[]{:S(2)}, u32[]{:S(2)}) collective-permute-start(bf16[512,2048]{1,0:T(8,128)(2,1)} %slice.157), channel_id=1, source_target_pairs={{0,2},{1,3},{2,0},{3,1},{4,6},{5,7},{6,4},{7,5},{8,10},{9,11},{10,... | collective-permute-start | bytes 6291464 | tf_op jit(solution)/shard_map/ppermute | solution.py:70
  661.2 46.8 %collective-permute-start.20 = (bf16[512,2048]{1,0:T(8,128)(2,1)S(1)}, bf16[512,2048]{1,0:T(8,128)(2,1)S(1)}, u32[]{:S(2)}, u32[]{:S(2)}) collective-permute-start(bf16[512,2048]{1,0:T(8,128)(2,1)S(1)} %get-tuple-element.145), channel_id=1, source_target_pairs={{0,2},{1,3},{2,0},{3,1},{4,6},{5,7},{6,4},{7,5},{8,10},{9,11},{10,... | collective-permute-start | bytes 6291464 | tf_op jit(solution)/shard_map/ppermute | solution.py:70
  662.7 45.4 %collective-permute-start.21 = (bf16[512,2048]{1,0:T(8,128)(2,1)S(1)}, bf16[512,2048]{1,0:T(8,128)(2,1)S(1)}, u32[]{:S(2)}, u32[]{:S(2)}) collective-permute-start(bf16[512,2048]{1,0:T(8,128)(2,1)S(1)} %get-tuple-element.145), channel_id=1, source_target_pairs={{0,1},{1,0},{2,3},{3,2},{4,5},{5,4},{6,7},{7,6},{8,9},{9,8},{10,11... | collective-permute-start | bytes 6291464 | tf_op jit(solution)/shard_map/ppermute | solution.py:70
  773.3 235.2 %reduce-scatter.13.cloned.1.call-start = ((), (), s32[]{:S(2)}) async-start(), calls=%async_computation.22 | async-start | bytes 10485760 | tf_op jit(solution)/shard_map/reduce_scatter | solution.py:601
  837.0 48.8 %collective-permute-start.24 = (bf16[512,2048]{1,0:T(8,128)(2,1)}, bf16[512,2048]{1,0:T(8,128)(2,1)}, u32[]{:S(2)}, u32[]{:S(2)}) collective-permute-start(bf16[512,2048]{1,0:T(8,128)(2,1)} %slice.156), channel_id=1, source_target_pairs={{0,2},{1,3},{2,0},{3,1},{4,6},{5,7},{6,4},{7,5},{8,10},{9,11},{10,... | collective-permute-start | bytes 6291464 | tf_op jit(solution)/shard_map/ppermute | solution.py:70
  922.6 235.2 %reduce-scatter.9.cloned.1.call-start = ((), (), s32[]{:S(2)}) async-start(), calls=%async_computation.20 | async-start | bytes 10485760 | tf_op jit(solution)/shard_map/reduce_scatter | solution.py:601
  923.4 53.4 %all-to-all-start.4 = ((bf16[8,512,256]{2,1,0:T(8,128)(2,1)}), bf16[8,512,256]{2,1,0:T(8,128)(2,1)}, u32[]{:S(2)}, u32[]{:S(2)}) async-start(bf16[8,512,256]{2,1,0:T(8,128)(2,1)} %bitcast.179), calls=%async_computation.4 | async-start | bytes 4194304 | tf_op jit(solution)/shard_map/all_to_all | solution.py:623
  927.7 254.4 %reduce-scatter.15.cloned.1.call-start = ((), (), s32[]{:S(2)}) async-start(), calls=%async_computation.23 | async-start | bytes 2359296 | tf_op jit(solution)/shard_map/reduce_scatter | solution.py:646
  979.2 75.5 %collective-permute-start.25 = (bf16[256,2048]{1,0:T(8,128)(2,1)}, bf16[256,2048]{1,0:T(8,128)(2,1)}, u32[]{:S(2)}, u32[]{:S(2)}) collective-permute-start(bf16[256,2048]{1,0:T(8,128)(2,1)} %constant_dynamic-slice_fusion.1), channel_id=1, source_target_pairs={{0,4},{1,5},{2,6},{3,7},{4,0},{5,1},{6,2},{7,3},{8,12},{9,13},{10,... | collective-permute-start | bytes 3145736 | tf_op jit(solution)/shard_map/ppermute | solution.py:70
  1008.5 223.5 %reduce-scatter.11.cloned.1.call-start = ((), (), s32[]{:S(2)}) async-start(), calls=%async_computation.21 | async-start | bytes 10485760 | tf_op jit(solution)/shard_map/reduce_scatter | solution.py:601
  1127.1 13.5 collective-permute-start.29
  1153.0 49.8 %collective-permute-start.30 = (bf16[512,2048]{1,0:T(8,128)(2,1)}, bf16[512,2048]{1,0:T(8,128)(2,1)}, u32[]{:S(2)}, u32[]{:S(2)}) collective-permute-start(bf16[512,2048]{1,0:T(8,128)(2,1)} %get-tuple-element.149), channel_id=1, source_target_pairs={{0,2},{1,3},{2,4},{3,5},{4,6},{5,7},{8,10},{9,11},{10,12},{11,13},... | collective-permute-start | bytes 6291464 | tf_op jit(solution)/shard_map/ppermute | solution.py:145
  1157.8 78.8 %all-to-all-start.5 = ((bf16[8,64,2048]{2,1,0:T(8,128)(2,1)}), bf16[8,64,2048]{2,1,0:T(8,128)(2,1)S(1)}, u32[]{:S(2)}, u32[]{:S(2)}) async-start(bf16[8,64,2048]{2,1,0:T(8,128)(2,1)} %bitcast.171), calls=%async_computation.7 | async-start | bytes 4194304 | tf_op jit(solution)/shard_map/all_to_all | solution.py:604
  1161.4 214.8 %reduce-scatter.17.cloned.1.call-start = ((), (), s32[]{:S(2)}) async-start(), calls=%async_computation.24 | async-start | bytes 3932160 | tf_op jit(solution)/shard_map/reduce_scatter | solution.py:601
  1180.8 72.5 %collective-permute-start.38 = (bf16[512,2048]{1,0:T(8,128)(2,1)}, bf16[512,2048]{1,0:T(8,128)(2,1)}, u32[]{:S(2)}, u32[]{:S(2)}) collective-permute-start(bf16[512,2048]{1,0:T(8,128)(2,1)} %get-tuple-element.150), channel_id=1, source_target_pairs={{2,0},{3,1},{4,2},{5,3},{6,4},{7,5},{10,8},{11,9},{12,10},{13,11},... | collective-permute-start | bytes 6291464 | tf_op jit(solution)/shard_map/ppermute | solution.py:145
  1207.2 74.3 %collective-permute-start.31 = (bf16[512,2048]{1,0:T(8,128)(2,1)}, bf16[512,2048]{1,0:T(8,128)(2,1)}, u32[]{:S(2)}, u32[]{:S(2)}) collective-permute-start(bf16[512,2048]{1,0:T(8,128)(2,1)} %fusion.10), channel_id=1, source_target_pairs={{0,2},{1,3},{2,4},{3,5},{4,6},{5,7},{8,10},{9,11},{10,12},{11,13},... | collective-permute-start | bytes 6291464 | tf_op jit(solution)/shard_map/ppermute | solution.py:145
  1236.6 139.7 %all-to-all-start.6 = ((bf16[8,64,2048]{2,1,0:T(8,128)(2,1)}), bf16[8,64,2048]{2,1,0:T(8,128)(2,1)}, u32[]{:S(2)}, u32[]{:S(2)}) async-start(bf16[8,64,2048]{2,1,0:T(8,128)(2,1)} %bitcast.173), calls=%async_computation.9 | async-start | bytes 4194304 | tf_op jit(solution)/shard_map/all_to_all | solution.py:604
  1289.3 74.3 %collective-permute-start.39 = (bf16[512,2048]{1,0:T(8,128)(2,1)}, bf16[512,2048]{1,0:T(8,128)(2,1)}, u32[]{:S(2)}, u32[]{:S(2)}) collective-permute-start(bf16[512,2048]{1,0:T(8,128)(2,1)} %get-tuple-element.148), channel_id=1, source_target_pairs={{2,0},{3,1},{4,2},{5,3},{6,4},{7,5},{10,8},{11,9},{12,10},{13,11},... | collective-permute-start | bytes 6291464 | tf_op jit(solution)/shard_map/ppermute | solution.py:145
  1368.1 97.3 %collective-permute-start.40 = (bf16[512,2048]{1,0:T(8,128)(2,1)}, bf16[512,2048]{1,0:T(8,128)(2,1)}, u32[]{:S(2)}, u32[]{:S(2)}) collective-permute-start(bf16[512,2048]{1,0:T(8,128)(2,1)} %fusion.9), channel_id=1, source_target_pairs={{2,0},{3,1},{4,2},{5,3},{6,4},{7,5},{10,8},{11,9},{12,10},{13,11},... | collective-permute-start | bytes 6291464 | tf_op jit(solution)/shard_map/ppermute | solution.py:145
  1369.4 96.0 %collective-permute-start.32 = (bf16[512,2048]{1,0:T(8,128)(2,1)}, bf16[512,2048]{1,0:T(8,128)(2,1)}, u32[]{:S(2)}, u32[]{:S(2)}) collective-permute-start(bf16[512,2048]{1,0:T(8,128)(2,1)} %get-tuple-element.147), channel_id=1, source_target_pairs={{0,2},{1,3},{2,4},{3,5},{4,6},{5,7},{8,10},{9,11},{10,12},{11,13},... | collective-permute-start | bytes 6291464 | tf_op jit(solution)/shard_map/ppermute | solution.py:145
  1376.3 78.2 %all-to-all-start.7 = ((bf16[8,64,768]{2,1,0:T(8,128)(2,1)}), bf16[8,64,768]{2,1,0:T(8,128)(2,1)S(1)}, u32[]{:S(2)}, u32[]{:S(2)}) async-start(bf16[8,64,768]{2,1,0:T(8,128)(2,1)} %bitcast.199), calls=%async_computation.13 | async-start | bytes 1572864 | tf_op jit(solution)/shard_map/all_to_all | solution.py:651
  1391.6 33.4 %collective-permute-start.36 = (f32[4,2048]{1,0:T(4,128)S(1)}, f32[4,2048]{1,0:T(4,128)S(1)}, u32[]{:S(2)}, u32[]{:S(2)}) collective-permute-start(f32[4,2048]{1,0:T(4,128)S(1)} %add.303), channel_id=1, source_target_pairs={{0,2},{1,3},{2,0},{3,1},{4,6},{5,7},{6,4},{7,5},{8,10},{9,11},{10,... | collective-permute-start | bytes 98312 | tf_op jit(solution)/shard_map/ppermute | solution.py:70
  (47 other events, 587.9 us)
Sparse Core Ops, SparseCore 0:
  13.2 170.4 all-gather.5
  186.7 100.1 all-gather.7
  288.8 86.1 all-gather.9
  376.7 87.5 all-gather.11
  466.0 87.5 all-gather.13
  773.4 86.3 reduce-scatter.6
  922.7 85.7 reduce-scatter.12
  1011.6 86.4 reduce-scatter.8
  1100.4 41.1 reduce-scatter.14
  1144.8 87.1 reduce-scatter.10
  1235.0 43.9 reduce-scatter.16

commit v2 on v1

--- a/solution.py
+++ b/solution.py
@@ -143,27 +143,6 @@
     size = lax.axis_size("seq")
     pairs = [(i, i + 2 * step) for i in range(size) if 0 <= i + 2 * step < size]
     return lax.ppermute(values, "seq", pairs)
-
-
-def scatter_line(values, *earlier):
-    size, place = lax.axis_size("seq"), lax.axis_index("seq")
-    pairs, pair, core = size // 2, place // 2, place % 2
-    rows = values.shape[0] // size
-    blocks = values.reshape(pairs, 2, rows, values.shape[1])
-    sent = exchange(lax.dynamic_index_in_dim(blocks, 1 - core, 1, keepdims=False), "seq", 1)
-    kept = lax.dynamic_index_in_dim(blocks, core, 1, keepdims=False)
-    blocks = (kept.astype(F32) + sent.astype(F32)).astype(BF16)
-    total = lax.dynamic_index_in_dim(blocks, pair, 0, keepdims=False).astype(F32)
-    for step in (1, -1):
-        moving = None
-        for far in range(pairs - 1, 0, -1):
-            target = jnp.clip(pair + step * far, 0, pairs - 1)
-            block = lax.dynamic_index_in_dim(blocks, target, 0, keepdims=False)
-            if moving is not None:
-                block = (block.astype(F32) + moving.astype(F32)).astype(BF16)
-            moving = shift(block, step)
-        total = total + after(moving, *earlier).astype(F32)
-    return total
 
 
 def gather_placed(values, axis):
@@ -181,6 +160,30 @@
         for m, v in found.items():
             out = lax.dynamic_update_slice_in_dim(out, v, (own ^ m) * rows + first, 0)
     return out
+
+
+def scatter_line(values, earlier):
+    size, place = lax.axis_size("seq"), lax.axis_index("seq")
+    pairs, pair, core = size // 2, place // 2, place % 2
+    rows = values.shape[0] // size
+    blocks = values.reshape(pairs, 2, rows, values.shape[1])
+    sent = exchange(lax.dynamic_index_in_dim(blocks, 1 - core, 1, keepdims=False), "seq", 1)
+    kept = lax.dynamic_index_in_dim(blocks, core, 1, keepdims=False)
+    blocks = (kept.astype(F32) + sent.astype(F32)).astype(BF16)
+
+    def block_at(place):
+        place = jnp.clip(place, 0, pairs - 1)
+        return lax.dynamic_index_in_dim(blocks, place, 0, keepdims=False)
+
+    up = down = None
+    for far in range(pairs - 1, 0, -1):
+        next_up, next_down = block_at(pair + far), block_at(pair - far)
+        if up is not None:
+            next_up = (next_up.astype(F32) + up.astype(F32)).astype(BF16)
+            next_down = (next_down.astype(F32) + down.astype(F32)).astype(BF16)
+        up, down = shift(next_up, 1), shift(next_down, -1)
+        up = after(up, down, *earlier.get(pairs - far, ()))
+    return block_at(pair).astype(F32) + up.astype(F32) + down.astype(F32)
 
 
 def ordered(kernel, count, earlier):
@@ -600,35 +603,38 @@
     def over_rows(part):
         return lax.psum_scatter(part, "fsdp", scatter_dimension=0, tiled=True)
 
-    def columns_back(part):
-        part = lax.all_to_all(part, "seq", split_axis=0, concat_axis=0, tiled=True).astype(F32)
-        part = part.reshape(groups, GROUP, share, fsdp * groups, down_share).sum(axis=0)
-        return jnp.moveaxis(part, 0, 2).reshape(share, -1)
+    def columns_sent(part):
+        return lax.all_to_all(part, "seq", split_axis=0, concat_axis=0, tiled=True)
+
+    def columns_joined(part):
+        part = part.reshape(groups, GROUP, share, fsdp * groups, down_share)
+        return jnp.moveaxis(part.astype(F32).sum(axis=0), 0, 2).reshape(share, -1)
 
     dgate, dup = act_back(grad_mproj, d_weight, gate, up)
     down_grad = weight_grad(act, grad_mproj, dgate)
     share_down = over_rows(down_grad)
     grads = hidden_back(dgate, g_weight, dup, u_weight, down_grad)
+    grads = scatter_near(grads)
     gate_grad = weight_grad(hidden_low, dgate, grads)
     share_gate = over_rows(gate_grad)
-    grads = scatter_near(grads)
-    up_grad = weight_grad(hidden_low, dup, gate_grad, grads)
-    share_up = over_rows(up_grad)
-    grad_hidden = grad_rows + scatter_far(grads, up_grad)
+    grad_hidden = grad_rows + scatter_far(grads, gate_grad)
 
     grad_aproj, grad_again = norm_back(grad_hidden, a_proj, a_scale, a_gain)
-    grad_aproj = grad_aproj.astype(BF16)
+    grad_aproj = after(grad_aproj.astype(BF16), share_down)
     grad_attn = dot_nt(grad_aproj, o_weight).astype(BF16)
     grad_attn = jnp.moveaxis(grad_attn.reshape(own_rows, seq, local_width), 1, 0)
     grad_heads = lax.all_to_all(grad_attn, "seq", split_axis=0, concat_axis=0, tiled=True)
-    o_grad = weight_grad(attn_rows, grad_aproj, grad_attn)
+    up_grad = weight_grad(hidden_low, dup, gate_grad, grad_attn)
+    share_up = over_rows(up_grad)
+    o_grad = weight_grad(attn_rows, grad_aproj, up_grad)
     share_output = over_rows(o_grad)
-    grad_heads = after(grad_heads, o_grad)
+    grad_heads = after(grad_heads, o_grad, share_gate)
     share_down = scatter_outer(after(share_down, grad_heads))
     dq, dk, dv = attend_backward(
         *rotated, starts, grad_heads.reshape(head_shape), log_sums, factor
     )
     dq = after(dq, share_down)
+    share_gate = columns_sent(after(share_gate, dq))
     dq, dk, dv = (v.reshape(seq * own_rows, local_width) for v in (dq, dk, dv))
     q_rot, k_rot = (v.reshape(seq * own_rows, local_width) for v in rotated[:2])
     inner = jnp.stack(
@@ -639,14 +645,19 @@
     )
     inner = sum_small(inner, "seq") / width
     grad_qkv, gain_sums = unprepare(
-        dq, dk, dv, proj, scales, inner.T, qk_gain, cosine, sine
+        dq, dk, after(dv, share_up), proj, scales, inner.T, qk_gain, cosine, sine
     )
     partial = dot_nt(grad_qkv, qkv_weight).astype(BF16)
+    partial = after(partial, share_gate)
     qkv_grad = weight_grad(inputs_all, grad_qkv, partial)
-    share_output = lax.psum_scatter(share_output, "seq", scatter_dimension=0, tiled=True).astype(F32)
     qkv_grad = after(qkv_grad, share_output)
-    share_gate = columns_back(after(share_gate, grad_qkv))
-    share_up = columns_back(after(share_up, grad_qkv))
+    share_output = lax.all_to_all(share_output, "seq", split_axis=0, concat_axis=0, tiled=True)
+    middle = (share_output,)
+    share_output = share_output.astype(F32).reshape(seq, share, width).sum(axis=0)
+    share_gate = columns_joined(share_gate)
+    share_up = columns_sent(after(share_up, partial))
+    early = (share_up,)
+    share_up = columns_joined(share_up)
     share_qkv = over_rows(qkv_grad)
     share_qkv = lax.all_to_all(
         share_qkv.reshape(seq, share, 3 * local_width), "seq", split_axis=0, concat_axis=0, tiled=True
@@ -659,7 +670,8 @@
     slots = jnp.concatenate([slots, grad_again[None], grad_mgain[None]])
     slots = sum_small(sum_small(slots, "fsdp"), "seq")
     gain_grads = lax.dynamic_slice_in_dim(slots, (row * seq + place) * share, share, 1)
-    grad_inputs = scatter_line(partial, share_gate, share_up, share_qkv, gain_grads)
+    late = (share_gate, share_up, share_output, share_qkv, gain_grads)
+    grad_inputs = scatter_line(partial, {1: early, 2: middle, seq // 2 - 1: late})
     input_grad = (grad_hidden + grad_inputs).astype(BF16)
     return (
         mixed.reshape(tokens.shape),

time: 1490 us -> 1470 us (0.987)
  waiting for transfers between devices: 654 us -> 634 us
    ppermute x6, waiting for transfers between devices: 120 us -> 76.3 us  [shift(): return lax.ppermute(values, 'seq', pairs)]
    reduce_scatter x5, waiting for transfers between devices: 42.7 us -> 0.03 us  [over_rows(): return lax.psum_scatter(part, 'fsdp', scatter_dimension=0, tiled=True)]
    ppermute x35, waiting for transfers between devices: 342 us -> 380 us  [exchange(): lax.ppermute(values, axis, [(i, i ^ bit) for i in range(lax.axis_size(axi...]
    all_to_all x2 -> x3, waiting for transfers between devices: 4.61 us -> 42.1 us  [the longest x1 21.1 us: on_device(): lax.all_to_all(share_output, 'seq', split_axis=0, concat_axis=0, tiled=True)]
    unnamed x83 -> x85, local copies, waits for them, and re-layouts: 36.8 us -> 31.9 us
where the time goes in v2:
time: 1470 us; the launch traced here: 1460 us
  waiting for transfers between devices  634 us (43%)
  Pallas kernels  358 us (24%)
  local copies, waits for them, and re-layouts  129 us (9%)
  other arithmetic  118 us (8%)
  starting transfers between devices  113 us (8%)
  blocking collectives  52.2 us (4%)
  matrix products  37 us (3%)
  between operations  15.7 us (1%)
    ppermute x35, waiting for transfers between devices, exchange(): lax.ppermute(values, axis, [(i, i ^ bit) for i in range(lax.axis_size(axi...  380 us
    pallas_call x4, Pallas kernels, by_columns(): pl.pallas_call(ordered(kernel, len(operands), earlier), grid=(cols // 512...  146 us
    pallas_call x5, Pallas kernels, weight_grad(): pl.pallas_call(ordered(weight_kernel, 2, earlier), grid=(rows // block,),...  99.7 us
    ppermute x6, waiting for transfers between devices, shift(): return lax.ppermute(values, 'seq', pairs)  76.3 us
    all_gather x1, waiting for transfers between devices, on_device(): inputs_all = lax.all_gather(inputs, 'seq', axis=0, tiled=True)  68.9 us
    all_to_all x1, blocking collectives, columns(): return lax.all_to_all(part, 'seq', split_axis=0, concat_axis=0, tiled=True)  52.2 us
    pallas_call x1, Pallas kernels, attend_backward(): pl.pallas_call(ordered(functools.partial(backward_kernel, factor=factor,...  43.1 us
    all_to_all x1, waiting for transfers between devices, on_device(): lax.all_to_all(grad_attn, 'seq', split_axis=0, concat_axis=0, tiled=True)  40 us
  transfers between devices with their start and end apart: 59, of which 36 were waited for; matrix products, arithmetic and copies ran while one was open for 16% of the time, Pallas kernels for 19%

profile of v2, /device:TPU:0, one launch (start us, length us, event | category | flops | bytes accessed | tf_op | source)
XLA Modules:
  0.0 1457.5 jit_solution(2720372610612513143)
XLA Ops:
  26.7 25.2 %collective-permute-done.7 = f32[8,768]{1,0:T(8,128)S(1)} collective-permute-done((f32[8,768]{1,0:T(8,128)S(1)}, f32[8,768]{1,0:T(8,128)S(1)}, u32[]{:S(2)}, u32[]{:S(2)}) %collective-permute-start.7) | collective-permute-done | bytes 24608 | tf_op jit(solution)/shard_map/ppermute | solution.py:70
  56.4 15.5 %collective-permute-done.8 = f32[8,768]{1,0:T(8,128)S(1)} collective-permute-done((f32[8,768]{1,0:T(8,128)S(1)}, f32[8,768]{1,0:T(8,128)S(1)}, u32[]{:S(2)}, u32[]{:S(2)}) %collective-permute-start.8) | collective-permute-done | bytes 24608 | tf_op jit(solution)/shard_map/ppermute | solution.py:70
  73.6 7.5 fusion.16
  114.6 68.9 %all-gather.6.cloned.1.call-done.refs_0_ = bf16[4096,2048]{1,0:T(8,128)(2,1)} async-done(((bf16[512,2048]{1,0:T(8,128)(2,1)}), bf16[4096,2048]{1,0:T(8,128)(2,1)}) %all-gather.6.cloned.1.call-update) | async-done | bytes 16777232 | tf_op jit(solution)/shard_map/all_gather | solution.py:542
  194.5 19.2 %shard_map.238 = (f32[4096,768]{1,0:T(8,128)}, f32[8,4096]{1,0:T(8,128)S(1)}) custom-call(bf16[4096,2048]{1,0:T(8,128)(2,1)} %shard_map.237.rows_ref.refs_1_.refs_0_, bf16[2048,768]{1,0:T(8,128)(2,1)S(1)} %copy-done.1), custom_call_target="tpu_custom_call" | custom-call | flops 12884901888 | tf_op jit(solution)/shard_map/pallas_call | solution.py:304
  218.9 26.6 %collective-permute-done.12 = f32[2,4096]{1,0:T(2,128)S(1)} collective-permute-done((f32[2,4096]{1,0:T(2,128)S(1)}, f32[2,4096]{1,0:T(2,128)S(1)}, u32[]{:S(2)}, u32[]{:S(2)}) %collective-permute-start.12) | collective-permute-done | bytes 32800 | tf_op jit(solution)/shard_map/ppermute | solution.py:70
  269.7 11.5 shard_map.239
  290.2 52.2 %all_to_all.88 = bf16[8,64,2048]{2,1,0:T(8,128)(2,1)} all-to-all(bf16[8,64,2048]{2,1,0:T(8,128)(2,1)S(1)} %bitcast.189), channel_id=1, replica_groups=mesh['fsdp'=4,'seq'=8] {'seq'}, dimensions={0} | all-to-all | bytes 4194304 | tf_op jit(solution)/shard_map/all_to_all | solution.py:570
  344.8 23.0 %shard_map.240 = (bf16[8,2,256,256]{3,2,1,0:T(8,128)(2,1)S(1)}, f32[2,2,1,2048]{3,2,1,0:T(1,128)S(1)}) custom-call(bf16[8,2,256,256]{3,2,1,0:T(8,128)(2,1)S(1)} %bitcast.161, bf16[8,2,256,256]{3,2,1,0:T(8,128)(2,1)} %bitcast.178, bf16[8,2,256,256]{3,2,1,0:T(8,128)(2,1)} %bitcast.196, s32[2,1,2048]{2,1,0:T(1,128)S(1)} %copy-done.4), custom_call_target="tpu_custom_call" | custom-call | flops 23622320128 | tf_op jit(solution)/shard_map/pallas_call | solution.py:483
  373.6 39.1 %collective-permute-done.17 = bf16[256,2048]{1,0:T(8,128)(2,1)} collective-permute-done((bf16[256,2048]{1,0:T(8,128)(2,1)}, bf16[256,2048]{1,0:T(8,128)(2,1)}, u32[]{:S(2)}, u32[]{:S(2)}) %collective-permute-start.17) | collective-permute-done | bytes 1048608 | tf_op jit(solution)/shard_map/ppermute | solution.py:70
  416.2 18.8 %all-to-all-done.3 = bf16[8,512,256]{2,1,0:T(8,128)(2,1)} async-done(((bf16[8,512,256]{2,1,0:T(8,128)(2,1)}), bf16[8,512,256]{2,1,0:T(8,128)(2,1)}, u32[]{:S(2)}, u32[]{:S(2)}) %all-to-all-start.3) | async-done | bytes 2097184 | tf_op jit(solution)/shard_map/all_to_all | solution.py:584
  438.2 8.3 multiply_reduce_fusion.5
  448.5 47.5 %collective-permute-done.14 = bf16[512,2048]{1,0:T(8,128)(2,1)S(1)} collective-permute-done((bf16[512,2048]{1,0:T(8,128)(2,1)S(1)}, bf16[512,2048]{1,0:T(8,128)(2,1)S(1)}, u32[]{:S(2)}, u32[]{:S(2)}) %collective-permute-start.14) | collective-permute-done | bytes 2097184 | tf_op jit(solution)/shard_map/ppermute | solution.py:70
  504.2 42.5 %shard_map.245 = (bf16[2048,2048]{1,0:T(8,128)(2,1)}, bf16[2048,2048]{1,0:T(8,128)(2,1)}, bf16[2048,2048]{1,0:T(8,128)(2,1)}) custom-call(bf16[2048,2048]{1,0:T(8,128)(2,1)} %pad_maximum_fusion.refs_0_, bf16[2048,2048]{1,0:T(8,128)(2,1)} %all-gather.10.cloned.1.call-done.refs_1_, bf16[2048,2048]{1,0:T(8,128)(2,1)} %all-gather.12.cloned.1.call-done.refs_2_.refs_3_), custom_call_target="tpu_custom_call" | custom-call | flops 34359738368 | tf_op jit(solution)/shard_map/pallas_call | solution.py:241
  546.7 6.9 all-gather.14.cloned.1.call-done.refs_1_
  553.6 25.3 %shard_map.247 = bf16[2048,2048]{1,0:T(8,128)(2,1)} custom-call(bf16[2048,2048]{1,0:T(8,128)(2,1)} %get-tuple-element.36.refs_0_, bf16[2048,2048]{1,0:T(8,128)(2,1)} %all-gather.14.cloned.1.call-done.refs_1_), custom_call_target="tpu_custom_call" | custom-call | flops 17179869184 | tf_op jit(solution)/shard_map/pallas_call | solution.py:241
  581.6 7.3 collective-permute-done.18
  599.3 46.4 %collective-permute-done.19.refs_0_ = bf16[512,2048]{1,0:T(8,128)(2,1)} collective-permute-done((bf16[512,2048]{1,0:T(8,128)(2,1)}, bf16[512,2048]{1,0:T(8,128)(2,1)}, u32[]{:S(2)}, u32[]{:S(2)}) %collective-permute-start.19) | collective-permute-done | bytes 2097184 | tf_op jit(solution)/shard_map/ppermute | solution.py:70
  662.4 45.4 %collective-permute-done.20 = bf16[512,2048]{1,0:T(8,128)(2,1)S(1)} collective-permute-done((bf16[512,2048]{1,0:T(8,128)(2,1)S(1)}, bf16[512,2048]{1,0:T(8,128)(2,1)S(1)}, u32[]{:S(2)}, u32[]{:S(2)}) %collective-permute-start.20) | collective-permute-done | bytes 2097184 | tf_op jit(solution)/shard_map/ppermute | solution.py:70
  715.8 33.7 %shard_map.249 = (bf16[2048,2048]{1,0:T(8,128)(2,1)}, bf16[2048,2048]{1,0:T(8,128)(2,1)}) custom-call(bf16[2048,2048]{1,0:T(8,128)(2,1)} %pad_maximum_fusion.1.refs_0_.refs_1_, bf16[2048,2048]{1,0:T(8,128)(2,1)} %all-gather.14.cloned.1.call-done.refs_1_, bf16[2048,2048]{1,0:T(8,128)(2,1)} %get-tuple-element.37.refs_2_, ...), custom_call_target="tpu_custom_call" | custom-call | flops 17179869184 | tf_op jit(solution)/shard_map/pallas_call | solution.py:241
  749.5 23.7 %shard_map.250.refs_4_ = bf16[2048,2048]{1,0:T(8,128)(2,1)} custom-call(bf16[2048,2048]{1,0:T(8,128)(2,1)} %get-tuple-element.36.refs_0_, bf16[2048,2048]{1,0:T(8,128)(2,1)} %pad_maximum_fusion.1.refs_0_.refs_1_, bf16[2048,2048]{1,0:T(8,128)(2,1)} %get-tuple-element.39.refs_2_.refs_0_.refs_1_), custom_call_target="tpu_custom_call" | custom-call | flops 17179869184 | tf_op jit(solution)/shard_map/pallas_call | solution.py:279
  773.3 44.6 %shard_map.251 = bf16[2048,2048]{1,0:T(8,128)(2,1)} custom-call(bf16[2048,2048]{1,0:T(8,128)(2,1)} %get-tuple-element.39.refs_2_.refs_0_.refs_1_, bf16[2048,2048]{1,0:T(8,128)(2,1)} %all-gather.10.cloned.1.call-done.refs_1_, bf16[2048,2048]{1,0:T(8,128)(2,1)} %get-tuple-element.40.refs_2_.refs_1_, ...), custom_call_target="tpu_custom_call" | custom-call | flops 34359738368 | tf_op jit(solution)/shard_map/pallas_call | solution.py:241
  820.9 6.9 collective-permute-done.23
  833.0 24.1 %shard_map.252.refs_1_.refs_2_ = bf16[2048,2048]{1,0:T(8,128)(2,1)} custom-call(bf16[2048,2048]{1,0:T(8,128)(2,1)} %pad_maximum_fusion.refs_0_, bf16[2048,2048]{1,0:T(8,128)(2,1)} %get-tuple-element.39.refs_2_.refs_0_.refs_1_, f32[1024,2048]{1,0:T(8,128)} %convert_add_fusion.1.refs_2_), custom_call_target="tpu_custom_call" | custom-call | flops 17179869184 | tf_op jit(solution)/shard_map/pallas_call | solution.py:279
  861.4 46.4 %collective-permute-done.24.refs_0_ = bf16[512,2048]{1,0:T(8,128)(2,1)} collective-permute-done((bf16[512,2048]{1,0:T(8,128)(2,1)S(1)}, bf16[512,2048]{1,0:T(8,128)(2,1)}, u32[]{:S(2)}, u32[]{:S(2)}) %collective-permute-start.24) | collective-permute-done | bytes 2097184 | tf_op jit(solution)/shard_map/ppermute | solution.py:70
  918.8 9.9 convolution_convert_fusion.1
  936.6 23.8 %shard_map.255.refs_2_ = bf16[2048,2048]{1,0:T(8,128)(2,1)} custom-call(bf16[2048,2048]{1,0:T(8,128)(2,1)} %pad_maximum_fusion.refs_0_, bf16[2048,2048]{1,0:T(8,128)(2,1)} %get-tuple-element.40.refs_2_.refs_1_, bf16[2048,2048]{1,0:T(8,128)(2,1)} %shard_map.252.refs_1_.refs_2_, bf16[8,512,256]{2,1,0:T(8,128)(2,1)} %bitcast.185), custom_call_target="tpu_custom_call" | custom-call | flops 17179869184 | tf_op jit(solution)/shard_map/pallas_call | solution.py:279
  965.1 9.1 shard_map.256.refs_1_
  974.3 40.0 %all-to-all-done.4.refs_0_ = bf16[8,512,256]{2,1,0:T(8,128)(2,1)} async-done(((bf16[8,512,256]{2,1,0:T(8,128)(2,1)}), bf16[8,512,256]{2,1,0:T(8,128)(2,1)}, u32[]{:S(2)}, u32[]{:S(2)}) %all-to-all-start.4) | async-done | bytes 2097184 | tf_op jit(solution)/shard_map/all_to_all | solution.py:626
  1015.7 43.1 %shard_map.258 = (bf16[8,2,256,256]{3,2,1,0:T(8,128)(2,1)}, bf16[8,2,256,256]{3,2,1,0:T(8,128)(2,1)}, bf16[8,2,256,256]{3,2,1,0:T(8,128)(2,1)}) custom-call(bf16[8,2,256,256]{3,2,1,0:T(8,128)(2,1)} %bitcast.160, bf16[8,2,256,256]{3,2,1,0:T(8,128)(2,1)} %bitcast.179, bf16[8,2,256,256]{3,2,1,0:T(8,128)(2,1)} %bitcast.197, s32[2,1,2048]{2,1,0:T(1,128)S(1)} %copy-done.4, ...), custom_call_target="tpu_custom_call" | custom-call | flops 42949672960 | tf_op jit(solution)/shard_map/pallas_call | solution.py:499
  1092.5 15.0 %shard_map.262 = (bf16[4096,768]{1,0:T(8,128)(2,1)}, f32[1,512]{1,0:T(1,128)}) custom-call(bf16[4096,256]{1,0:T(8,128)(2,1)} %bitcast.170, bf16[4096,256]{1,0:T(8,128)(2,1)} %bitcast.200, bf16[4096,256]{1,0:T(8,128)(2,1)} %shard_map.261.dv_ref, f32[4096,768]{1,0:T(8,128)} %get-tuple-element.30.proj_ref, f32[4096,2]{1,0:T(8,128)} %rsqrt_bitcast_fusion.scale_ref, ...), custom_call_target="tpu_custom_call" | custom-call | flops 14784921600 | tf_op jit(solution)/shard_map/pallas_call | solution.py:388
  1107.5 18.8 %convolution_convert_fusion.refs_0_ = bf16[4096,2048]{1,0:T(8,128)(2,1)} fusion(bf16[4096,768]{1,0:T(8,128)(2,1)} %get-tuple-element.45.refs_1_, bf16[2048,768]{1,0:T(8,128)(2,1)S(1)} %copy-done.1), kind=kOutput, calls=%fused_computation.2 | convolution fusion | flops 12893290496 | bytes 26214400 | tf_op jit(solution)/shard_map/dot_general | solution.py:39
  1126.3 9.4 all-to-all-done.5
  1135.7 8.4 dynamic-slice_bitcast_fusion
  1147.8 19.1 %shard_map.268.refs_0_ = bf16[2048,768]{1,0:T(8,128)(2,1)} custom-call(bf16[4096,2048]{1,0:T(8,128)(2,1)} %shard_map.237.rows_ref.refs_1_.refs_0_, bf16[4096,768]{1,0:T(8,128)(2,1)} %get-tuple-element.45.refs_1_, bf16[4096,2048]{1,0:T(8,128)(2,1)} %shard_map.264.refs_1_.refs_2_), custom_call_target="tpu_custom_call" | custom-call | flops 12884901888 | tf_op jit(solution)/shard_map/pallas_call | solution.py:279
  1166.9 7.5 fusion
  1185.6 11.6 all-to-all-done.6
  1201.7 27.6 %collective-permute-done.30.refs_0_ = bf16[512,2048]{1,0:T(8,128)(2,1)} collective-permute-done((bf16[512,2048]{1,0:T(8,128)(2,1)}, bf16[512,2048]{1,0:T(8,128)(2,1)}, u32[]{:S(2)}, u32[]{:S(2)}) %collective-permute-start.30) | collective-permute-done | bytes 2097184 | tf_op jit(solution)/shard_map/ppermute | solution.py:145
  1229.3 12.4 collective-permute-done.31.refs_1_
  1241.7 7.8 fusion.10
  1249.5 15.4 %collective-permute-start.32 = (bf16[512,2048]{1,0:T(8,128)(2,1)}, bf16[512,2048]{1,0:T(8,128)(2,1)S(1)}, u32[]{:S(2)}, u32[]{:S(2)}) collective-permute-start(bf16[512,2048]{1,0:T(8,128)(2,1)} %get-tuple-element.149), channel_id=1, source_target_pairs={{0,2},{1,3},{2,4},{3,5},{4,6},{5,7},{8,10},{9,11},{10,12},{11,13},... | collective-permute-start | bytes 6291464 | tf_op jit(solution)/shard_map/ppermute | solution.py:145
  1266.2 21.1 %all-to-all-done.7 = bf16[8,64,2048]{2,1,0:T(8,128)(2,1)} async-done(((bf16[8,64,2048]{2,1,0:T(8,128)(2,1)}), bf16[8,64,2048]{2,1,0:T(8,128)(2,1)}, u32[]{:S(2)}, u32[]{:S(2)}) %all-to-all-start.7) | async-done | bytes 2097184 | tf_op jit(solution)/shard_map/all_to_all | solution.py:654
  1287.3 22.5 %collective-permute-done.32.refs_0_ = bf16[512,2048]{1,0:T(8,128)(2,1)S(1)} collective-permute-done((bf16[512,2048]{1,0:T(8,128)(2,1)}, bf16[512,2048]{1,0:T(8,128)(2,1)S(1)}, u32[]{:S(2)}, u32[]{:S(2)}) %collective-permute-start.32) | collective-permute-done | bytes 2097184 | tf_op jit(solution)/shard_map/ppermute | solution.py:145
  1309.8 13.8 collective-permute-done.33.refs_1_
  1323.6 7.8 fusion.11
  1332.7 12.6 collective-permute-start.34
  1362.6 39.7 %collective-permute-done.39 = f32[4,2048]{1,0:T(4,128)S(1)} collective-permute-done((f32[4,2048]{1,0:T(4,128)S(1)}, f32[4,2048]{1,0:T(4,128)S(1)}, u32[]{:S(2)}, u32[]{:S(2)}) %collective-permute-start.39) | collective-permute-done | bytes 32800 | tf_op jit(solution)/shard_map/ppermute | solution.py:70
  1443.2 7.0 fusion.14
  (336 shorter events, 322.0 us)
Async XLA Ops:
  7.2 176.4 %all-gather.6.cloned.1.call-start = ((), (), s32[]{:S(2)}) async-start(), calls=%async_computation.14 | async-start | bytes 18874368 | tf_op jit(solution)/shard_map/all_gather | solution.py:542
  13.0 425.2 %all-gather.8.cloned.1.call-start = ((), (), s32[]{:S(2)}) async-start(), calls=%async_computation.15 | async-start | bytes 8650752 | tf_op jit(solution)/shard_map/all_gather | solution.py:574
  14.0 10.4 collective-permute-start.6
  18.5 65.8 %all-to-all-start = ((bf16[8,2,24576]{2,1,0:T(2,128)(2,1)}), bf16[8,2,24576]{2,1,0:T(2,128)(2,1)S(1)}, u32[]{:S(2)}, u32[]{:S(2)}) async-start(bf16[8,2,24576]{2,1,0:T(2,128)(2,1)} %reshape.278), calls=%async_computation | async-start | bytes 1572864 | tf_op jit(solution)/shard_map/all_to_all | solution.py:544
  24.6 27.3 %collective-permute-start.7 = (f32[8,768]{1,0:T(8,128)S(1)}, f32[8,768]{1,0:T(8,128)S(1)}, u32[]{:S(2)}, u32[]{:S(2)}) collective-permute-start(f32[8,768]{1,0:T(8,128)S(1)} %add.254), channel_id=1, source_target_pairs={{0,2},{1,3},{2,0},{3,1},{4,6},{5,7},{6,4},{7,5},{8,10},{9,11},{10,... | collective-permute-start | bytes 73736 | tf_op jit(solution)/shard_map/ppermute | solution.py:70
  51.9 20.0 %collective-permute-start.8 = (f32[8,768]{1,0:T(8,128)S(1)}, f32[8,768]{1,0:T(8,128)S(1)}, u32[]{:S(2)}, u32[]{:S(2)}) collective-permute-start(f32[8,768]{1,0:T(8,128)S(1)} %add.255), channel_id=1, source_target_pairs={{0,4},{1,5},{2,6},{3,7},{4,0},{5,1},{6,2},{7,3},{8,12},{9,13},{10,... | collective-permute-start | bytes 73736 | tf_op jit(solution)/shard_map/ppermute | solution.py:70
  72.1 16.3 %collective-permute-start.9 = (f32[4,8,4,64]{3,2,1,0:T(4,128)S(1)}, f32[4,8,4,64]{3,2,1,0:T(4,128)S(1)}, u32[]{:S(2)}, u32[]{:S(2)}) collective-permute-start(f32[4,8,4,64]{3,2,1,0:T(4,128)S(1)} %constant_dynamic-update-slice_fusion.1), channel_id=1, source_target_pairs={{0,8},{8,0},{16,24},{24,16},{1,9},{9,1},{17,25},{25,17},{2,10},{10... | collective-permute-start | bytes 98312 | tf_op jit(solution)/shard_map/ppermute | solution.py:70
  87.8 10.8 collective-permute-start
  88.3 12.9 collective-permute-start.10
  90.3 14.1 collective-permute-start.3
  91.5 15.6 %collective-permute-start.1 = (bf16[256,768]{1,0:T(8,128)(2,1)}, bf16[256,768]{1,0:T(8,128)(2,1)}, u32[]{:S(2)}, u32[]{:S(2)}) collective-permute-start(bf16[256,768]{1,0:T(8,128)(2,1)} %copy.211), channel_id=1, source_target_pairs={{0,16},{8,24},{16,0},{24,8},{1,17},{9,25},{17,1},{25,9},{2,18},{10... | collective-permute-start | bytes 1179656 | tf_op jit(solution)/shard_map/ppermute | solution.py:70
  98.6 12.7 collective-permute-start.2
  102.6 10.8 collective-permute-start.4
  104.4 10.2 collective-permute-start.5
  189.8 91.4 %all-to-all-start.1 = ((bf16[8,64,2048]{2,1,0:T(8,128)(2,1)}), bf16[8,64,2048]{2,1,0:T(8,128)(2,1)}, u32[]{:S(2)}, u32[]{:S(2)}) async-start(bf16[8,64,2048]{2,1,0:T(8,128)(2,1)} %bitcast.184), calls=%async_computation.1 | async-start | bytes 4194304 | tf_op jit(solution)/shard_map/all_to_all | solution.py:570
  194.2 310.0 %all-gather.10.cloned.1.call-start = ((), (), s32[]{:S(2)}) async-start(), calls=%async_computation.16 | async-start | bytes 10485760 | tf_op jit(solution)/shard_map/all_gather | solution.py:580
  215.0 30.5 %collective-permute-start.12 = (f32[2,4096]{1,0:T(2,128)S(1)}, f32[2,4096]{1,0:T(2,128)S(1)}, u32[]{:S(2)}, u32[]{:S(2)}) collective-permute-start(f32[2,4096]{1,0:T(2,128)S(1)} %slice_add_fusion.2), channel_id=1, source_target_pairs={{0,2},{1,3},{2,0},{3,1},{4,6},{5,7},{6,4},{7,5},{8,10},{9,11},{10,... | collective-permute-start | bytes 98312 | tf_op jit(solution)/shard_map/ppermute | solution.py:70
  253.4 10.5 collective-permute-start.13
  281.3 222.9 %all-gather.12.cloned.1.call-start = ((), (), s32[]{:S(2)}) async-start(), calls=%async_computation.17 | async-start | bytes 10485760 | tf_op jit(solution)/shard_map/all_gather | solution.py:593
  342.5 70.1 %collective-permute-start.17 = (bf16[256,2048]{1,0:T(8,128)(2,1)}, bf16[256,2048]{1,0:T(8,128)(2,1)}, u32[]{:S(2)}, u32[]{:S(2)}) collective-permute-start(bf16[256,2048]{1,0:T(8,128)(2,1)} %shard_map.246), channel_id=1, source_target_pairs={{0,4},{1,5},{2,6},{3,7},{4,0},{5,1},{6,2},{7,3},{8,12},{9,13},{10,... | collective-permute-start | bytes 3145736 | tf_op jit(solution)/shard_map/ppermute | solution.py:70
  369.1 65.9 %all-to-all-start.3 = ((bf16[8,512,256]{2,1,0:T(8,128)(2,1)}), bf16[8,512,256]{2,1,0:T(8,128)(2,1)}, u32[]{:S(2)}, u32[]{:S(2)}) async-start(bf16[8,512,256]{2,1,0:T(8,128)(2,1)} %bitcast.162), calls=%async_computation.3 | async-start | bytes 4194304 | tf_op jit(solution)/shard_map/all_to_all | solution.py:584
  373.5 180.1 %all-gather.14.cloned.1.call-start = ((), (), s32[]{:S(2)}) async-start(), calls=%async_computation.18 | async-start | bytes 10485760 | tf_op jit(solution)/shard_map/all_gather | solution.py:593
  415.9 502.9 %reduce-scatter.6.cloned.1.call-start = ((), (), s32[]{:S(2)}) async-start(), calls=%async_computation.19 | async-start | bytes 10485760 | tf_op jit(solution)/shard_map/reduce_scatter | solution.py:604
  448.5 47.6 %collective-permute-start.14 = (bf16[512,2048]{1,0:T(8,128)(2,1)S(1)}, bf16[512,2048]{1,0:T(8,128)(2,1)S(1)}, u32[]{:S(2)}, u32[]{:S(2)}) collective-permute-start(bf16[512,2048]{1,0:T(8,128)(2,1)S(1)} %fusion.15), channel_id=1, source_target_pairs={{0,2},{1,3},{2,0},{3,1},{4,6},{5,7},{6,4},{7,5},{8,10},{9,11},{10,... | collective-permute-start | bytes 6291464 | tf_op jit(solution)/shard_map/ppermute | solution.py:70
  448.5 47.6 %collective-permute-start.15 = (bf16[512,2048]{1,0:T(8,128)(2,1)S(1)}, bf16[512,2048]{1,0:T(8,128)(2,1)S(1)}, u32[]{:S(2)}, u32[]{:S(2)}) collective-permute-start(bf16[512,2048]{1,0:T(8,128)(2,1)S(1)} %fusion.15), channel_id=1, source_target_pairs={{0,1},{1,0},{2,3},{3,2},{4,5},{5,4},{6,7},{7,6},{8,9},{9,8},{10,11... | collective-permute-start | bytes 6291464 | tf_op jit(solution)/shard_map/ppermute | solution.py:70
  597.8 48.0 %collective-permute-start.19 = (bf16[512,2048]{1,0:T(8,128)(2,1)}, bf16[512,2048]{1,0:T(8,128)(2,1)}, u32[]{:S(2)}, u32[]{:S(2)}) collective-permute-start(bf16[512,2048]{1,0:T(8,128)(2,1)} %slice.157), channel_id=1, source_target_pairs={{0,2},{1,3},{2,0},{3,1},{4,6},{5,7},{6,4},{7,5},{8,10},{9,11},{10,... | collective-permute-start | bytes 6291464 | tf_op jit(solution)/shard_map/ppermute | solution.py:70
  660.9 46.8 %collective-permute-start.20 = (bf16[512,2048]{1,0:T(8,128)(2,1)S(1)}, bf16[512,2048]{1,0:T(8,128)(2,1)S(1)}, u32[]{:S(2)}, u32[]{:S(2)}) collective-permute-start(bf16[512,2048]{1,0:T(8,128)(2,1)S(1)} %get-tuple-element.145), channel_id=1, source_target_pairs={{0,2},{1,3},{2,0},{3,1},{4,6},{5,7},{6,4},{7,5},{8,10},{9,11},{10,... | collective-permute-start | bytes 6291464 | tf_op jit(solution)/shard_map/ppermute | solution.py:70
  662.4 45.4 %collective-permute-start.21 = (bf16[512,2048]{1,0:T(8,128)(2,1)S(1)}, bf16[512,2048]{1,0:T(8,128)(2,1)S(1)}, u32[]{:S(2)}, u32[]{:S(2)}) collective-permute-start(bf16[512,2048]{1,0:T(8,128)(2,1)S(1)} %get-tuple-element.145), channel_id=1, source_target_pairs={{0,1},{1,0},{2,3},{3,2},{4,5},{5,4},{6,7},{7,6},{8,9},{9,8},{10,11... | collective-permute-start | bytes 6291464 | tf_op jit(solution)/shard_map/ppermute | solution.py:70
  773.2 241.0 %reduce-scatter.8.cloned.1.call-start = ((), (), s32[]{:S(2)}) async-start(), calls=%async_computation.20 | async-start | bytes 10485760 | tf_op jit(solution)/shard_map/reduce_scatter | solution.py:604
  857.1 235.3 %reduce-scatter.10.cloned.1.call-start = ((), (), s32[]{:S(2)}) async-start(), calls=%async_computation.21 | async-start | bytes 10485760 | tf_op jit(solution)/shard_map/reduce_scatter | solution.py:604
  859.7 48.0 %collective-permute-start.24 = (bf16[512,2048]{1,0:T(8,128)(2,1)S(1)}, bf16[512,2048]{1,0:T(8,128)(2,1)}, u32[]{:S(2)}, u32[]{:S(2)}) collective-permute-start(bf16[512,2048]{1,0:T(8,128)(2,1)S(1)} %slice.156), channel_id=1, source_target_pairs={{0,2},{1,3},{2,0},{3,1},{4,6},{5,7},{6,4},{7,5},{8,10},{9,11},{10,... | collective-permute-start | bytes 6291464 | tf_op jit(solution)/shard_map/ppermute | solution.py:70
  960.4 53.8 %all-to-all-start.4 = ((bf16[8,512,256]{2,1,0:T(8,128)(2,1)}), bf16[8,512,256]{2,1,0:T(8,128)(2,1)}, u32[]{:S(2)}, u32[]{:S(2)}) async-start(bf16[8,512,256]{2,1,0:T(8,128)(2,1)} %bitcast.186), calls=%async_computation.5 | async-start | bytes 4194304 | tf_op jit(solution)/shard_map/all_to_all | solution.py:626
  965.1 201.8 %reduce-scatter.12.cloned.1.call-start = ((), (), s32[]{:S(2)}) async-start(), calls=%async_computation.22 | async-start | bytes 10485760 | tf_op jit(solution)/shard_map/reduce_scatter | solution.py:604
  1015.6 47.2 %collective-permute-start.25 = (bf16[256,2048]{1,0:T(8,128)(2,1)S(1)}, bf16[256,2048]{1,0:T(8,128)(2,1)S(1)}, u32[]{:S(2)}, u32[]{:S(2)}) collective-permute-start(bf16[256,2048]{1,0:T(8,128)(2,1)S(1)} %constant_dynamic-slice_fusion.1), channel_id=1, source_target_pairs={{0,4},{1,5},{2,6},{3,7},{4,0},{5,1},{6,2},{7,3},{8,12},{9,13},{10,... | collective-permute-start | bytes 3145736 | tf_op jit(solution)/shard_map/ppermute | solution.py:70
  1082.2 53.4 %all-to-all-start.5 = ((bf16[8,64,2048]{2,1,0:T(8,128)(2,1)}), bf16[8,64,2048]{2,1,0:T(8,128)(2,1)}, u32[]{:S(2)}, u32[]{:S(2)}) async-start(bf16[8,64,2048]{2,1,0:T(8,128)(2,1)} %bitcast.169), calls=%async_computation.8 | async-start | bytes 4194304 | tf_op jit(solution)/shard_map/all_to_all | solution.py:607
  1144.1 22.8 %collective-permute-start.29 = (bf16[4,512,2048]{2,1,0:T(8,128)(2,1)}, bf16[4,512,2048]{2,1,0:T(8,128)(2,1)}, u32[]{:S(2)}, u32[]{:S(2)}) collective-permute-start(bf16[4,512,2048]{2,1,0:T(8,128)(2,1)} %dynamic-slice_bitcast_fusion), channel_id=1, source_target_pairs={{0,1},{1,0},{2,3},{3,2},{4,5},{5,4},{6,7},{7,6},{8,9},{9,8},{10,11... | collective-permute-start | bytes 25165832 | tf_op jit(solution)/shard_map/ppermute | solution.py:70
  1144.1 53.1 %all-to-all-start.6 = ((bf16[8,64,2048]{2,1,0:T(8,128)(2,1)}), bf16[8,64,2048]{2,1,0:T(8,128)(2,1)S(1)}, u32[]{:S(2)}, u32[]{:S(2)}) async-start(bf16[8,64,2048]{2,1,0:T(8,128)(2,1)} %bitcast.168), calls=%async_computation.9 | async-start | bytes 4194304 | tf_op jit(solution)/shard_map/all_to_all | solution.py:607
  1147.7 198.8 %reduce-scatter.14.cloned.1.call-start = ((), (), s32[]{:S(2)}) async-start(), calls=%async_computation.23 | async-start | bytes 3932160 | tf_op jit(solution)/shard_map/reduce_scatter | solution.py:604
  1179.2 50.0 %collective-permute-start.30 = (bf16[512,2048]{1,0:T(8,128)(2,1)}, bf16[512,2048]{1,0:T(8,128)(2,1)}, u32[]{:S(2)}, u32[]{:S(2)}) collective-permute-start(bf16[512,2048]{1,0:T(8,128)(2,1)} %get-tuple-element.151), channel_id=1, source_target_pairs={{0,2},{1,3},{2,4},{3,5},{4,6},{5,7},{8,10},{9,11},{10,12},{11,13},... | collective-permute-start | bytes 6291464 | tf_op jit(solution)/shard_map/ppermute | solution.py:145
  1184.3 57.4 %collective-permute-start.31 = (bf16[512,2048]{1,0:T(8,128)(2,1)}, bf16[512,2048]{1,0:T(8,128)(2,1)}, u32[]{:S(2)}, u32[]{:S(2)}) collective-permute-start(bf16[512,2048]{1,0:T(8,128)(2,1)} %get-tuple-element.152), channel_id=1, source_target_pairs={{2,0},{3,1},{4,2},{5,3},{6,4},{7,5},{10,8},{11,9},{12,10},{13,11},... | collective-permute-start | bytes 6291464 | tf_op jit(solution)/shard_map/ppermute | solution.py:145
  1197.2 90.0 %all-to-all-start.7 = ((bf16[8,64,2048]{2,1,0:T(8,128)(2,1)}), bf16[8,64,2048]{2,1,0:T(8,128)(2,1)}, u32[]{:S(2)}, u32[]{:S(2)}) async-start(bf16[8,64,2048]{2,1,0:T(8,128)(2,1)} %bitcast.191), calls=%async_computation.11 | async-start | bytes 4194304 | tf_op jit(solution)/shard_map/all_to_all | solution.py:654
  1249.5 60.3 %collective-permute-start.32 = (bf16[512,2048]{1,0:T(8,128)(2,1)}, bf16[512,2048]{1,0:T(8,128)(2,1)S(1)}, u32[]{:S(2)}, u32[]{:S(2)}) collective-permute-start(bf16[512,2048]{1,0:T(8,128)(2,1)} %get-tuple-element.149), channel_id=1, source_target_pairs={{0,2},{1,3},{2,4},{3,5},{4,6},{5,7},{8,10},{9,11},{10,12},{11,13},... | collective-permute-start | bytes 6291464 | tf_op jit(solution)/shard_map/ppermute | solution.py:145
  1264.9 58.7 %collective-permute-start.33 = (bf16[512,2048]{1,0:T(8,128)(2,1)}, bf16[512,2048]{1,0:T(8,128)(2,1)}, u32[]{:S(2)}, u32[]{:S(2)}) collective-permute-start(bf16[512,2048]{1,0:T(8,128)(2,1)} %get-tuple-element.150), channel_id=1, source_target_pairs={{2,0},{3,1},{4,2},{5,3},{6,4},{7,5},{10,8},{11,9},{12,10},{13,11},... | collective-permute-start | bytes 6291464 | tf_op jit(solution)/shard_map/ppermute | solution.py:145
  1331.4 111.8 %collective-permute-start.35 = (bf16[512,2048]{1,0:T(8,128)(2,1)}, bf16[512,2048]{1,0:T(8,128)(2,1)}, u32[]{:S(2)}, u32[]{:S(2)}) collective-permute-start(bf16[512,2048]{1,0:T(8,128)(2,1)} %get-tuple-element.148), channel_id=1, source_target_pairs={{2,0},{3,1},{4,2},{5,3},{6,4},{7,5},{10,8},{11,9},{12,10},{13,11},... | collective-permute-start | bytes 6291464 | tf_op jit(solution)/shard_map/ppermute | solution.py:145
  1332.7 110.5 %collective-permute-start.34 = (bf16[512,2048]{1,0:T(8,128)(2,1)}, bf16[512,2048]{1,0:T(8,128)(2,1)}, u32[]{:S(2)}, u32[]{:S(2)}) collective-permute-start(bf16[512,2048]{1,0:T(8,128)(2,1)} %get-tuple-element.147), channel_id=1, source_target_pairs={{0,2},{1,3},{2,4},{3,5},{4,6},{5,7},{8,10},{9,11},{10,12},{11,13},... | collective-permute-start | bytes 6291464 | tf_op jit(solution)/shard_map/ppermute | solution.py:145
  1346.5 85.6 %all-to-all-start.8 = ((bf16[8,64,768]{2,1,0:T(8,128)(2,1)}), bf16[8,64,768]{2,1,0:T(8,128)(2,1)S(1)}, u32[]{:S(2)}, u32[]{:S(2)}) async-start(bf16[8,64,768]{2,1,0:T(8,128)(2,1)} %bitcast.206), calls=%async_computation.13 | async-start | bytes 1572864 | tf_op jit(solution)/shard_map/all_to_all | solution.py:662
  1360.5 41.8 %collective-permute-start.39 = (f32[4,2048]{1,0:T(4,128)S(1)}, f32[4,2048]{1,0:T(4,128)S(1)}, u32[]{:S(2)}, u32[]{:S(2)}) collective-permute-start(f32[4,2048]{1,0:T(4,128)S(1)} %add.294), channel_id=1, source_target_pairs={{0,2},{1,3},{2,0},{3,1},{4,6},{5,7},{6,4},{7,5},{8,10},{9,11},{10,... | collective-permute-start | bytes 98312 | tf_op jit(solution)/shard_map/ppermute | solution.py:70
  1402.3 15.1 %collective-permute-start.40 = (f32[4,2048]{1,0:T(4,128)S(1)}, f32[4,2048]{1,0:T(4,128)S(1)}, u32[]{:S(2)}, u32[]{:S(2)}) collective-permute-start(f32[4,2048]{1,0:T(4,128)S(1)} %add.295), channel_id=1, source_target_pairs={{0,4},{1,5},{2,6},{3,7},{4,0},{5,1},{6,2},{7,3},{8,12},{9,13},{10,... | collective-permute-start | bytes 98312 | tf_op jit(solution)/shard_map/ppermute | solution.py:70
  (48 other events, 451.7 us)
Sparse Core Ops, SparseCore 0:
  13.1 170.4 all-gather.5
  186.6 100.1 all-gather.7
  288.6 86.1 all-gather.9
  376.6 87.5 all-gather.11
  465.9 87.5 all-gather.13
  773.3 86.4 reduce-scatter.5
  863.1 86.4 reduce-scatter.7
  960.5 86.4 reduce-scatter.9
  1050.4 86.4 reduce-scatter.11
  1167.0 44.3 reduce-scatter.13

commit v3 on v2

--- a/solution.py
+++ b/solution.py
@@ -628,7 +628,7 @@
     share_up = over_rows(up_grad)
     o_grad = weight_grad(attn_rows, grad_aproj, up_grad)
     share_output = over_rows(o_grad)
-    grad_heads = after(grad_heads, o_grad, share_gate)
+    grad_heads = after(grad_heads, o_grad)
     share_down = scatter_outer(after(share_down, grad_heads))
     dq, dk, dv = attend_backward(
         *rotated, starts, grad_heads.reshape(head_shape), log_sums, factor
@@ -662,6 +662,7 @@
     share_qkv = lax.all_to_all(
         share_qkv.reshape(seq, share, 3 * local_width), "seq", split_axis=0, concat_axis=0, tiled=True
     )
+    middle += (share_qkv,)
     share_qkv = share_qkv.reshape(seq, share, 3, local_width).transpose(2, 1, 0, 3)
     share_qkv = share_qkv.reshape(3, share, width).astype(F32)
     slots = lax.dynamic_update_slice_in_dim(

time: 1470 us -> 1500 us (1.020)
  waiting for transfers between devices: 634 us -> 669 us
    all_to_all x1, waiting for transfers between devices: 0.01 us -> 60.3 us  [on_device(): lax.all_to_all(share_qkv.reshape(seq, share, 3 * local_width), 'seq', spl...]
    all_to_all x1, waiting for transfers between devices: 21.1 us -> 0.01 us  [on_device(): lax.all_to_all(share_output, 'seq', split_axis=0, concat_axis=0, tiled=True)]
    unnamed x85 -> x89, local copies, waits for them, and re-layouts: 31.9 us -> 31.5 us
  transfers between devices with their start and end apart: 59 -> 59, of which waited for: 36 -> 34; matrix products, arithmetic and copies ran while one was open for 16% -> 15% of each run, Pallas kernels for 19% -> 18%
where the time goes in v3:
time: 1500 us; the launch traced here: 1490 us
  waiting for transfers between devices  669 us (45%)
  Pallas kernels  358 us (24%)
  local copies, waits for them, and re-layouts  131 us (9%)
  other arithmetic  122 us (8%)
  starting transfers between devices  102 us (7%)
  blocking collectives  52.2 us (3%)
  matrix products  36.9 us (2%)
  between operations  15.6 us (1%)
    ppermute x35, waiting for transfers between devices, exchange(): lax.ppermute(values, axis, [(i, i ^ bit) for i in range(lax.axis_size(axi...  374 us
    pallas_call x4, Pallas kernels, by_columns(): pl.pallas_call(ordered(kernel, len(operands), earlier), grid=(cols // 512...  146 us
    pallas_call x5, Pallas kernels, weight_grad(): pl.pallas_call(ordered(weight_kernel, 2, earlier), grid=(rows // block,),...  99.6 us
    ppermute x6, waiting for transfers between devices, shift(): return lax.ppermute(values, 'seq', pairs)  71.8 us
    all_gather x1, waiting for transfers between devices, on_device(): inputs_all = lax.all_gather(inputs, 'seq', axis=0, tiled=True)  68.9 us
    all_to_all x1, waiting for transfers between devices, on_device(): lax.all_to_all(share_qkv.reshape(seq, share, 3 * local_width), 'seq', spl...  60.3 us
    all_to_all x1, blocking collectives, columns(): return lax.all_to_all(part, 'seq', split_axis=0, concat_axis=0, tiled=True)  52.2 us
    pallas_call x1, Pallas kernels, attend_backward(): pl.pallas_call(ordered(functools.partial(backward_kernel, factor=factor,...  43.1 us
  transfers between devices with their start and end apart: 59, of which 34 were waited for; matrix products, arithmetic and copies ran while one was open for 15% of the time, Pallas kernels for 18%

profile of v3, /device:TPU:0, one launch (start us, length us, event | category | flops | bytes accessed | tf_op | source)
XLA Modules:
  0.0 1486.6 jit_solution(3599116220473353402)
XLA Ops:
  18.5 6.0 all-to-all-start
  26.7 25.2 %collective-permute-done.7 = f32[8,768]{1,0:T(8,128)S(1)} collective-permute-done((f32[8,768]{1,0:T(8,128)S(1)}, f32[8,768]{1,0:T(8,128)S(1)}, u32[]{:S(2)}, u32[]{:S(2)}) %collective-permute-start.7) | collective-permute-done | bytes 24608 | tf_op jit(solution)/shard_map/ppermute | solution.py:70
  56.4 15.5 %collective-permute-done.8 = f32[8,768]{1,0:T(8,128)S(1)} collective-permute-done((f32[8,768]{1,0:T(8,128)S(1)}, f32[8,768]{1,0:T(8,128)S(1)}, u32[]{:S(2)}, u32[]{:S(2)}) %collective-permute-start.8) | collective-permute-done | bytes 24608 | tf_op jit(solution)/shard_map/ppermute | solution.py:70
  73.6 7.5 fusion.16
  114.6 68.9 %all-gather.6.cloned.1.call-done.refs_0_ = bf16[4096,2048]{1,0:T(8,128)(2,1)} async-done(((bf16[512,2048]{1,0:T(8,128)(2,1)}), bf16[4096,2048]{1,0:T(8,128)(2,1)}) %all-gather.6.cloned.1.call-update) | async-done | bytes 16777232 | tf_op jit(solution)/shard_map/all_gather | solution.py:542
  194.5 19.1 %shard_map.238 = (f32[4096,768]{1,0:T(8,128)}, f32[8,4096]{1,0:T(8,128)S(1)}) custom-call(bf16[4096,2048]{1,0:T(8,128)(2,1)} %shard_map.237.rows_ref.refs_1_.refs_0_, bf16[2048,768]{1,0:T(8,128)(2,1)S(1)} %copy-done.1), custom_call_target="tpu_custom_call" | custom-call | flops 12884901888 | tf_op jit(solution)/shard_map/pallas_call | solution.py:304
  218.9 26.5 %collective-permute-done.12 = f32[2,4096]{1,0:T(2,128)S(1)} collective-permute-done((f32[2,4096]{1,0:T(2,128)S(1)}, f32[2,4096]{1,0:T(2,128)S(1)}, u32[]{:S(2)}, u32[]{:S(2)}) %collective-permute-start.12) | collective-permute-done | bytes 32800 | tf_op jit(solution)/shard_map/ppermute | solution.py:70
  269.8 11.5 shard_map.239
  290.3 52.2 %all_to_all.88 = bf16[8,64,2048]{2,1,0:T(8,128)(2,1)} all-to-all(bf16[8,64,2048]{2,1,0:T(8,128)(2,1)S(1)} %bitcast.189), channel_id=1, replica_groups=mesh['fsdp'=4,'seq'=8] {'seq'}, dimensions={0} | all-to-all | bytes 4194304 | tf_op jit(solution)/shard_map/all_to_all | solution.py:570
  344.8 23.0 %shard_map.240 = (bf16[8,2,256,256]{3,2,1,0:T(8,128)(2,1)S(1)}, f32[2,2,1,2048]{3,2,1,0:T(1,128)S(1)}) custom-call(bf16[8,2,256,256]{3,2,1,0:T(8,128)(2,1)S(1)} %bitcast.161, bf16[8,2,256,256]{3,2,1,0:T(8,128)(2,1)} %bitcast.177, bf16[8,2,256,256]{3,2,1,0:T(8,128)(2,1)} %bitcast.196, s32[2,1,2048]{2,1,0:T(1,128)S(1)} %copy-done.4), custom_call_target="tpu_custom_call" | custom-call | flops 23622320128 | tf_op jit(solution)/shard_map/pallas_call | solution.py:483
  373.6 39.1 %collective-permute-done.17 = bf16[256,2048]{1,0:T(8,128)(2,1)} collective-permute-done((bf16[256,2048]{1,0:T(8,128)(2,1)}, bf16[256,2048]{1,0:T(8,128)(2,1)}, u32[]{:S(2)}, u32[]{:S(2)}) %collective-permute-start.17) | collective-permute-done | bytes 1048608 | tf_op jit(solution)/shard_map/ppermute | solution.py:70
  416.2 18.8 %all-to-all-done.3 = bf16[8,512,256]{2,1,0:T(8,128)(2,1)} async-done(((bf16[8,512,256]{2,1,0:T(8,128)(2,1)}), bf16[8,512,256]{2,1,0:T(8,128)(2,1)}, u32[]{:S(2)}, u32[]{:S(2)}) %all-to-all-start.3) | async-done | bytes 2097184 | tf_op jit(solution)/shard_map/all_to_all | solution.py:584
  438.2 8.3 multiply_reduce_fusion.5
  448.5 47.5 %collective-permute-done.14 = bf16[512,2048]{1,0:T(8,128)(2,1)S(1)} collective-permute-done((bf16[512,2048]{1,0:T(8,128)(2,1)S(1)}, bf16[512,2048]{1,0:T(8,128)(2,1)S(1)}, u32[]{:S(2)}, u32[]{:S(2)}) %collective-permute-start.14) | collective-permute-done | bytes 2097184 | tf_op jit(solution)/shard_map/ppermute | solution.py:70
  504.2 42.5 %shard_map.245 = (bf16[2048,2048]{1,0:T(8,128)(2,1)}, bf16[2048,2048]{1,0:T(8,128)(2,1)}, bf16[2048,2048]{1,0:T(8,128)(2,1)}) custom-call(bf16[2048,2048]{1,0:T(8,128)(2,1)} %pad_maximum_fusion.refs_0_, bf16[2048,2048]{1,0:T(8,128)(2,1)} %all-gather.10.cloned.1.call-done.refs_1_, bf16[2048,2048]{1,0:T(8,128)(2,1)} %all-gather.12.cloned.1.call-done.refs_2_.refs_3_), custom_call_target="tpu_custom_call" | custom-call | flops 34359738368 | tf_op jit(solution)/shard_map/pallas_call | solution.py:241
  546.7 6.9 all-gather.14.cloned.1.call-done.refs_1_
  553.6 25.3 %shard_map.247 = bf16[2048,2048]{1,0:T(8,128)(2,1)} custom-call(bf16[2048,2048]{1,0:T(8,128)(2,1)} %get-tuple-element.36.refs_0_, bf16[2048,2048]{1,0:T(8,128)(2,1)} %all-gather.14.cloned.1.call-done.refs_1_), custom_call_target="tpu_custom_call" | custom-call | flops 17179869184 | tf_op jit(solution)/shard_map/pallas_call | solution.py:241
  581.6 7.3 collective-permute-done.18
  599.3 46.4 %collective-permute-done.19.refs_0_ = bf16[512,2048]{1,0:T(8,128)(2,1)} collective-permute-done((bf16[512,2048]{1,0:T(8,128)(2,1)}, bf16[512,2048]{1,0:T(8,128)(2,1)}, u32[]{:S(2)}, u32[]{:S(2)}) %collective-permute-start.19) | collective-permute-done | bytes 2097184 | tf_op jit(solution)/shard_map/ppermute | solution.py:70
  649.4 6.2 fusion.7
  662.4 45.4 %collective-permute-done.20 = bf16[512,2048]{1,0:T(8,128)(2,1)S(1)} collective-permute-done((bf16[512,2048]{1,0:T(8,128)(2,1)S(1)}, bf16[512,2048]{1,0:T(8,128)(2,1)S(1)}, u32[]{:S(2)}, u32[]{:S(2)}) %collective-permute-start.20) | collective-permute-done | bytes 2097184 | tf_op jit(solution)/shard_map/ppermute | solution.py:70
  715.8 33.7 %shard_map.249 = (bf16[2048,2048]{1,0:T(8,128)(2,1)}, bf16[2048,2048]{1,0:T(8,128)(2,1)}) custom-call(bf16[2048,2048]{1,0:T(8,128)(2,1)} %pad_maximum_fusion.1.refs_0_.refs_1_, bf16[2048,2048]{1,0:T(8,128)(2,1)} %all-gather.14.cloned.1.call-done.refs_1_, bf16[2048,2048]{1,0:T(8,128)(2,1)} %get-tuple-element.37.refs_2_, ...), custom_call_target="tpu_custom_call" | custom-call | flops 17179869184 | tf_op jit(solution)/shard_map/pallas_call | solution.py:241
  749.5 23.7 %shard_map.250.refs_4_ = bf16[2048,2048]{1,0:T(8,128)(2,1)} custom-call(bf16[2048,2048]{1,0:T(8,128)(2,1)} %get-tuple-element.36.refs_0_, bf16[2048,2048]{1,0:T(8,128)(2,1)} %pad_maximum_fusion.1.refs_0_.refs_1_, bf16[2048,2048]{1,0:T(8,128)(2,1)} %get-tuple-element.39.refs_2_.refs_0_.refs_1_), custom_call_target="tpu_custom_call" | custom-call | flops 17179869184 | tf_op jit(solution)/shard_map/pallas_call | solution.py:279
  773.2 44.6 %shard_map.251 = bf16[2048,2048]{1,0:T(8,128)(2,1)} custom-call(bf16[2048,2048]{1,0:T(8,128)(2,1)} %get-tuple-element.39.refs_2_.refs_0_.refs_1_, bf16[2048,2048]{1,0:T(8,128)(2,1)} %all-gather.10.cloned.1.call-done.refs_1_, bf16[2048,2048]{1,0:T(8,128)(2,1)} %get-tuple-element.40.refs_2_.refs_1_, ...), custom_call_target="tpu_custom_call" | custom-call | flops 34359738368 | tf_op jit(solution)/shard_map/pallas_call | solution.py:241
  820.9 6.9 collective-permute-done.23
  833.0 24.0 %shard_map.252.refs_1_.refs_2_ = bf16[2048,2048]{1,0:T(8,128)(2,1)} custom-call(bf16[2048,2048]{1,0:T(8,128)(2,1)} %pad_maximum_fusion.refs_0_, bf16[2048,2048]{1,0:T(8,128)(2,1)} %get-tuple-element.39.refs_2_.refs_0_.refs_1_, f32[1024,2048]{1,0:T(8,128)} %convert_add_fusion.1.refs_2_), custom_call_target="tpu_custom_call" | custom-call | flops 17179869184 | tf_op jit(solution)/shard_map/pallas_call | solution.py:279
  861.3 46.3 %collective-permute-done.24.refs_0_ = bf16[512,2048]{1,0:T(8,128)(2,1)} collective-permute-done((bf16[512,2048]{1,0:T(8,128)(2,1)S(1)}, bf16[512,2048]{1,0:T(8,128)(2,1)}, u32[]{:S(2)}, u32[]{:S(2)}) %collective-permute-start.24) | collective-permute-done | bytes 2097184 | tf_op jit(solution)/shard_map/ppermute | solution.py:70
  907.6 6.8 multiply_reduce_fusion
  918.7 9.9 convolution_convert_fusion.1
  936.5 23.8 %shard_map.255.refs_2_ = bf16[2048,2048]{1,0:T(8,128)(2,1)} custom-call(bf16[2048,2048]{1,0:T(8,128)(2,1)} %pad_maximum_fusion.refs_0_, bf16[2048,2048]{1,0:T(8,128)(2,1)} %get-tuple-element.40.refs_2_.refs_1_, bf16[2048,2048]{1,0:T(8,128)(2,1)} %shard_map.252.refs_1_.refs_2_, bf16[8,512,256]{2,1,0:T(8,128)(2,1)} %bitcast.185), custom_call_target="tpu_custom_call" | custom-call | flops 17179869184 | tf_op jit(solution)/shard_map/pallas_call | solution.py:279
  965.1 9.1 shard_map.256.refs_1_
  974.2 40.0 %all-to-all-done.4.refs_0_ = bf16[8,512,256]{2,1,0:T(8,128)(2,1)} async-done(((bf16[8,512,256]{2,1,0:T(8,128)(2,1)}), bf16[8,512,256]{2,1,0:T(8,128)(2,1)}, u32[]{:S(2)}, u32[]{:S(2)}) %all-to-all-start.4) | async-done | bytes 2097184 | tf_op jit(solution)/shard_map/all_to_all | solution.py:626
  1015.6 43.1 %shard_map.258 = (bf16[8,2,256,256]{3,2,1,0:T(8,128)(2,1)}, bf16[8,2,256,256]{3,2,1,0:T(8,128)(2,1)}, bf16[8,2,256,256]{3,2,1,0:T(8,128)(2,1)}) custom-call(bf16[8,2,256,256]{3,2,1,0:T(8,128)(2,1)} %bitcast.160, bf16[8,2,256,256]{3,2,1,0:T(8,128)(2,1)} %bitcast.178, bf16[8,2,256,256]{3,2,1,0:T(8,128)(2,1)} %bitcast.197, s32[2,1,2048]{2,1,0:T(1,128)S(1)} %copy-done.4, ...), custom_call_target="tpu_custom_call" | custom-call | flops 42949672960 | tf_op jit(solution)/shard_map/pallas_call | solution.py:499
  1092.5 15.0 %shard_map.262 = (bf16[4096,768]{1,0:T(8,128)(2,1)}, f32[1,512]{1,0:T(1,128)}) custom-call(bf16[4096,256]{1,0:T(8,128)(2,1)} %bitcast.169, bf16[4096,256]{1,0:T(8,128)(2,1)} %bitcast.200, bf16[4096,256]{1,0:T(8,128)(2,1)} %shard_map.261.dv_ref, f32[4096,768]{1,0:T(8,128)} %get-tuple-element.30.proj_ref, f32[4096,2]{1,0:T(8,128)} %rsqrt_bitcast_fusion.scale_ref, ...), custom_call_target="tpu_custom_call" | custom-call | flops 14784921600 | tf_op jit(solution)/shard_map/pallas_call | solution.py:388
  1107.5 18.8 %convolution_convert_fusion.refs_0_ = bf16[4096,2048]{1,0:T(8,128)(2,1)} fusion(bf16[4096,768]{1,0:T(8,128)(2,1)} %get-tuple-element.45.refs_1_, bf16[2048,768]{1,0:T(8,128)(2,1)S(1)} %copy-done.1), kind=kOutput, calls=%fused_computation.2 | convolution fusion | flops 12893290496 | bytes 26214400 | tf_op jit(solution)/shard_map/dot_general | solution.py:39
  1126.3 9.4 all-to-all-done.5
  1135.7 8.4 dynamic-slice_bitcast_fusion
  1147.8 19.1 %shard_map.267.refs_0_ = bf16[2048,768]{1,0:T(8,128)(2,1)} custom-call(bf16[4096,2048]{1,0:T(8,128)(2,1)} %shard_map.237.rows_ref.refs_1_.refs_0_, bf16[4096,768]{1,0:T(8,128)(2,1)} %get-tuple-element.45.refs_1_, bf16[4096,2048]{1,0:T(8,128)(2,1)} %shard_map.264.refs_1_.refs_2_), custom_call_target="tpu_custom_call" | custom-call | flops 12884901888 | tf_op jit(solution)/shard_map/pallas_call | solution.py:279
  1166.9 11.1 fusion
  1178.0 18.7 %all-to-all-done.6 = bf16[8,64,2048]{2,1,0:T(8,128)(2,1)S(1)} async-done(((bf16[8,64,2048]{2,1,0:T(8,128)(2,1)}), bf16[8,64,2048]{2,1,0:T(8,128)(2,1)S(1)}, u32[]{:S(2)}, u32[]{:S(2)}) %all-to-all-start.6) | async-done | bytes 2097184 | tf_op jit(solution)/shard_map/all_to_all | solution.py:607
  1211.2 69.8 %collective-permute-done.30.refs_0_ = bf16[512,2048]{1,0:T(8,128)(2,1)S(1)} collective-permute-done((bf16[512,2048]{1,0:T(8,128)(2,1)}, bf16[512,2048]{1,0:T(8,128)(2,1)S(1)}, u32[]{:S(2)}, u32[]{:S(2)}) %collective-permute-start.30) | collective-permute-done | bytes 2097184 | tf_op jit(solution)/shard_map/ppermute | solution.py:145
  1283.0 7.8 fusion.10
  1290.7 14.8 collective-permute-start.32
  1312.4 60.3 %all-to-all-done.8.refs_3_ = bf16[8,64,768]{2,1,0:T(8,128)(2,1)S(1)} async-done(((bf16[8,64,768]{2,1,0:T(8,128)(2,1)}), bf16[8,64,768]{2,1,0:T(8,128)(2,1)S(1)}, u32[]{:S(2)}, u32[]{:S(2)}) %all-to-all-start.8) | async-done | bytes 786464 | tf_op jit(solution)/shard_map/all_to_all | solution.py:662
  1374.3 7.8 fusion.11
  1383.4 5.9 collective-permute-start.34
  1399.9 32.8 %collective-permute-done.39 = f32[4,2048]{1,0:T(4,128)S(1)} collective-permute-done((f32[4,2048]{1,0:T(4,128)S(1)}, f32[4,2048]{1,0:T(4,128)S(1)}, u32[]{:S(2)}, u32[]{:S(2)}) %collective-permute-start.39) | collective-permute-done | bytes 32800 | tf_op jit(solution)/shard_map/ppermute | solution.py:70
  1472.4 7.0 fusion.14
  (340 shorter events, 303.4 us)
Async XLA Ops:
  7.2 176.4 %all-gather.6.cloned.1.call-start = ((), (), s32[]{:S(2)}) async-start(), calls=%async_computation.14 | async-start | bytes 18874368 | tf_op jit(solution)/shard_map/all_gather | solution.py:542
  13.0 425.2 %all-gather.8.cloned.1.call-start = ((), (), s32[]{:S(2)}) async-start(), calls=%async_computation.15 | async-start | bytes 8650752 | tf_op jit(solution)/shard_map/all_gather | solution.py:574
  14.0 10.4 collective-permute-start.6
  18.5 65.8 %all-to-all-start = ((bf16[8,2,24576]{2,1,0:T(2,128)(2,1)}), bf16[8,2,24576]{2,1,0:T(2,128)(2,1)S(1)}, u32[]{:S(2)}, u32[]{:S(2)}) async-start(bf16[8,2,24576]{2,1,0:T(2,128)(2,1)} %reshape.278), calls=%async_computation | async-start | bytes 1572864 | tf_op jit(solution)/shard_map/all_to_all | solution.py:544
  24.6 27.3 %collective-permute-start.7 = (f32[8,768]{1,0:T(8,128)S(1)}, f32[8,768]{1,0:T(8,128)S(1)}, u32[]{:S(2)}, u32[]{:S(2)}) collective-permute-start(f32[8,768]{1,0:T(8,128)S(1)} %add.254), channel_id=1, source_target_pairs={{0,2},{1,3},{2,0},{3,1},{4,6},{5,7},{6,4},{7,5},{8,10},{9,11},{10,... | collective-permute-start | bytes 73736 | tf_op jit(solution)/shard_map/ppermute | solution.py:70
  51.9 20.0 %collective-permute-start.8 = (f32[8,768]{1,0:T(8,128)S(1)}, f32[8,768]{1,0:T(8,128)S(1)}, u32[]{:S(2)}, u32[]{:S(2)}) collective-permute-start(f32[8,768]{1,0:T(8,128)S(1)} %add.255), channel_id=1, source_target_pairs={{0,4},{1,5},{2,6},{3,7},{4,0},{5,1},{6,2},{7,3},{8,12},{9,13},{10,... | collective-permute-start | bytes 73736 | tf_op jit(solution)/shard_map/ppermute | solution.py:70
  72.1 16.3 %collective-permute-start.9 = (f32[4,8,4,64]{3,2,1,0:T(4,128)S(1)}, f32[4,8,4,64]{3,2,1,0:T(4,128)S(1)}, u32[]{:S(2)}, u32[]{:S(2)}) collective-permute-start(f32[4,8,4,64]{3,2,1,0:T(4,128)S(1)} %constant_dynamic-update-slice_fusion.1), channel_id=1, source_target_pairs={{0,8},{8,0},{16,24},{24,16},{1,9},{9,1},{17,25},{25,17},{2,10},{10... | collective-permute-start | bytes 98312 | tf_op jit(solution)/shard_map/ppermute | solution.py:70
  87.8 10.8 collective-permute-start
  88.3 12.9 collective-permute-start.10
  90.3 14.1 collective-permute-start.3
  91.5 15.6 %collective-permute-start.1 = (bf16[256,768]{1,0:T(8,128)(2,1)}, bf16[256,768]{1,0:T(8,128)(2,1)}, u32[]{:S(2)}, u32[]{:S(2)}) collective-permute-start(bf16[256,768]{1,0:T(8,128)(2,1)} %copy.212), channel_id=1, source_target_pairs={{0,16},{8,24},{16,0},{24,8},{1,17},{9,25},{17,1},{25,9},{2,18},{10... | collective-permute-start | bytes 1179656 | tf_op jit(solution)/shard_map/ppermute | solution.py:70
  98.5 12.7 collective-permute-start.2
  102.6 10.8 collective-permute-start.4
  104.4 10.2 collective-permute-start.5
  189.8 91.4 %all-to-all-start.1 = ((bf16[8,64,2048]{2,1,0:T(8,128)(2,1)}), bf16[8,64,2048]{2,1,0:T(8,128)(2,1)}, u32[]{:S(2)}, u32[]{:S(2)}) async-start(bf16[8,64,2048]{2,1,0:T(8,128)(2,1)} %bitcast.184), calls=%async_computation.1 | async-start | bytes 4194304 | tf_op jit(solution)/shard_map/all_to_all | solution.py:570
  194.2 310.0 %all-gather.10.cloned.1.call-start = ((), (), s32[]{:S(2)}) async-start(), calls=%async_computation.16 | async-start | bytes 10485760 | tf_op jit(solution)/shard_map/all_gather | solution.py:580
  215.0 30.5 %collective-permute-start.12 = (f32[2,4096]{1,0:T(2,128)S(1)}, f32[2,4096]{1,0:T(2,128)S(1)}, u32[]{:S(2)}, u32[]{:S(2)}) collective-permute-start(f32[2,4096]{1,0:T(2,128)S(1)} %slice_add_fusion.2), channel_id=1, source_target_pairs={{0,2},{1,3},{2,0},{3,1},{4,6},{5,7},{6,4},{7,5},{8,10},{9,11},{10,... | collective-permute-start | bytes 98312 | tf_op jit(solution)/shard_map/ppermute | solution.py:70
  253.4 10.5 collective-permute-start.13
  281.3 222.9 %all-gather.12.cloned.1.call-start = ((), (), s32[]{:S(2)}) async-start(), calls=%async_computation.17 | async-start | bytes 10485760 | tf_op jit(solution)/shard_map/all_gather | solution.py:593
  342.5 70.1 %collective-permute-start.17 = (bf16[256,2048]{1,0:T(8,128)(2,1)}, bf16[256,2048]{1,0:T(8,128)(2,1)}, u32[]{:S(2)}, u32[]{:S(2)}) collective-permute-start(bf16[256,2048]{1,0:T(8,128)(2,1)} %shard_map.246), channel_id=1, source_target_pairs={{0,4},{1,5},{2,6},{3,7},{4,0},{5,1},{6,2},{7,3},{8,12},{9,13},{10,... | collective-permute-start | bytes 3145736 | tf_op jit(solution)/shard_map/ppermute | solution.py:70
  369.2 65.9 %all-to-all-start.3 = ((bf16[8,512,256]{2,1,0:T(8,128)(2,1)}), bf16[8,512,256]{2,1,0:T(8,128)(2,1)}, u32[]{:S(2)}, u32[]{:S(2)}) async-start(bf16[8,512,256]{2,1,0:T(8,128)(2,1)} %bitcast.162), calls=%async_computation.3 | async-start | bytes 4194304 | tf_op jit(solution)/shard_map/all_to_all | solution.py:584
  373.5 180.0 %all-gather.14.cloned.1.call-start = ((), (), s32[]{:S(2)}) async-start(), calls=%async_computation.18 | async-start | bytes 10485760 | tf_op jit(solution)/shard_map/all_gather | solution.py:593
  416.0 502.7 %reduce-scatter.6.cloned.1.call-start = ((), (), s32[]{:S(2)}) async-start(), calls=%async_computation.19 | async-start | bytes 10485760 | tf_op jit(solution)/shard_map/reduce_scatter | solution.py:604
  448.5 47.6 %collective-permute-start.14 = (bf16[512,2048]{1,0:T(8,128)(2,1)S(1)}, bf16[512,2048]{1,0:T(8,128)(2,1)S(1)}, u32[]{:S(2)}, u32[]{:S(2)}) collective-permute-start(bf16[512,2048]{1,0:T(8,128)(2,1)S(1)} %fusion.15), channel_id=1, source_target_pairs={{0,2},{1,3},{2,0},{3,1},{4,6},{5,7},{6,4},{7,5},{8,10},{9,11},{10,... | collective-permute-start | bytes 6291464 | tf_op jit(solution)/shard_map/ppermute | solution.py:70
  448.5 47.6 %collective-permute-start.15 = (bf16[512,2048]{1,0:T(8,128)(2,1)S(1)}, bf16[512,2048]{1,0:T(8,128)(2,1)S(1)}, u32[]{:S(2)}, u32[]{:S(2)}) collective-permute-start(bf16[512,2048]{1,0:T(8,128)(2,1)S(1)} %fusion.15), channel_id=1, source_target_pairs={{0,1},{1,0},{2,3},{3,2},{4,5},{5,4},{6,7},{7,6},{8,9},{9,8},{10,11... | collective-permute-start | bytes 6291464 | tf_op jit(solution)/shard_map/ppermute | solution.py:70
  597.8 48.0 %collective-permute-start.19 = (bf16[512,2048]{1,0:T(8,128)(2,1)}, bf16[512,2048]{1,0:T(8,128)(2,1)}, u32[]{:S(2)}, u32[]{:S(2)}) collective-permute-start(bf16[512,2048]{1,0:T(8,128)(2,1)} %slice.157), channel_id=1, source_target_pairs={{0,2},{1,3},{2,0},{3,1},{4,6},{5,7},{6,4},{7,5},{8,10},{9,11},{10,... | collective-permute-start | bytes 6291464 | tf_op jit(solution)/shard_map/ppermute | solution.py:70
  660.9 46.8 %collective-permute-start.20 = (bf16[512,2048]{1,0:T(8,128)(2,1)S(1)}, bf16[512,2048]{1,0:T(8,128)(2,1)S(1)}, u32[]{:S(2)}, u32[]{:S(2)}) collective-permute-start(bf16[512,2048]{1,0:T(8,128)(2,1)S(1)} %get-tuple-element.145), channel_id=1, source_target_pairs={{0,2},{1,3},{2,0},{3,1},{4,6},{5,7},{6,4},{7,5},{8,10},{9,11},{10,... | collective-permute-start | bytes 6291464 | tf_op jit(solution)/shard_map/ppermute | solution.py:70
  662.4 45.4 %collective-permute-start.21 = (bf16[512,2048]{1,0:T(8,128)(2,1)S(1)}, bf16[512,2048]{1,0:T(8,128)(2,1)S(1)}, u32[]{:S(2)}, u32[]{:S(2)}) collective-permute-start(bf16[512,2048]{1,0:T(8,128)(2,1)S(1)} %get-tuple-element.145), channel_id=1, source_target_pairs={{0,1},{1,0},{2,3},{3,2},{4,5},{5,4},{6,7},{7,6},{8,9},{9,8},{10,11... | collective-permute-start | bytes 6291464 | tf_op jit(solution)/shard_map/ppermute | solution.py:70
  773.2 309.0 %reduce-scatter.10.cloned.1.call-start = ((), (), s32[]{:S(2)}) async-start(), calls=%async_computation.21 | async-start | bytes 10485760 | tf_op jit(solution)/shard_map/reduce_scatter | solution.py:604
  857.1 235.4 %reduce-scatter.8.cloned.1.call-start = ((), (), s32[]{:S(2)}) async-start(), calls=%async_computation.20 | async-start | bytes 10485760 | tf_op jit(solution)/shard_map/reduce_scatter | solution.py:604
  859.6 48.0 %collective-permute-start.24 = (bf16[512,2048]{1,0:T(8,128)(2,1)S(1)}, bf16[512,2048]{1,0:T(8,128)(2,1)}, u32[]{:S(2)}, u32[]{:S(2)}) collective-permute-start(bf16[512,2048]{1,0:T(8,128)(2,1)S(1)} %slice.156), channel_id=1, source_target_pairs={{0,2},{1,3},{2,0},{3,1},{4,6},{5,7},{6,4},{7,5},{8,10},{9,11},{10,... | collective-permute-start | bytes 6291464 | tf_op jit(solution)/shard_map/ppermute | solution.py:70
  960.4 53.8 %all-to-all-start.4 = ((bf16[8,512,256]{2,1,0:T(8,128)(2,1)}), bf16[8,512,256]{2,1,0:T(8,128)(2,1)}, u32[]{:S(2)}, u32[]{:S(2)}) async-start(bf16[8,512,256]{2,1,0:T(8,128)(2,1)} %bitcast.186), calls=%async_computation.5 | async-start | bytes 4194304 | tf_op jit(solution)/shard_map/all_to_all | solution.py:626
  965.0 201.8 %reduce-scatter.12.cloned.1.call-start = ((), (), s32[]{:S(2)}) async-start(), calls=%async_computation.22 | async-start | bytes 10485760 | tf_op jit(solution)/shard_map/reduce_scatter | solution.py:604
  1015.5 47.2 %collective-permute-start.25 = (bf16[256,2048]{1,0:T(8,128)(2,1)S(1)}, bf16[256,2048]{1,0:T(8,128)(2,1)S(1)}, u32[]{:S(2)}, u32[]{:S(2)}) collective-permute-start(bf16[256,2048]{1,0:T(8,128)(2,1)S(1)} %constant_dynamic-slice_fusion.1), channel_id=1, source_target_pairs={{0,4},{1,5},{2,6},{3,7},{4,0},{5,1},{6,2},{7,3},{8,12},{9,13},{10,... | collective-permute-start | bytes 3145736 | tf_op jit(solution)/shard_map/ppermute | solution.py:70
  1082.2 53.4 %all-to-all-start.5 = ((bf16[8,64,2048]{2,1,0:T(8,128)(2,1)}), bf16[8,64,2048]{2,1,0:T(8,128)(2,1)}, u32[]{:S(2)}, u32[]{:S(2)}) async-start(bf16[8,64,2048]{2,1,0:T(8,128)(2,1)} %bitcast.181), calls=%async_computation.8 | async-start | bytes 4194304 | tf_op jit(solution)/shard_map/all_to_all | solution.py:607
  1144.1 22.8 %collective-permute-start.29 = (bf16[4,512,2048]{2,1,0:T(8,128)(2,1)}, bf16[4,512,2048]{2,1,0:T(8,128)(2,1)}, u32[]{:S(2)}, u32[]{:S(2)}) collective-permute-start(bf16[4,512,2048]{2,1,0:T(8,128)(2,1)} %dynamic-slice_bitcast_fusion), channel_id=1, source_target_pairs={{0,1},{1,0},{2,3},{3,2},{4,5},{5,4},{6,7},{7,6},{8,9},{9,8},{10,11... | collective-permute-start | bytes 25165832 | tf_op jit(solution)/shard_map/ppermute | solution.py:70
  1144.1 52.6 %all-to-all-start.6 = ((bf16[8,64,2048]{2,1,0:T(8,128)(2,1)}), bf16[8,64,2048]{2,1,0:T(8,128)(2,1)S(1)}, u32[]{:S(2)}, u32[]{:S(2)}) async-start(bf16[8,64,2048]{2,1,0:T(8,128)(2,1)} %bitcast.168), calls=%async_computation.9 | async-start | bytes 4194304 | tf_op jit(solution)/shard_map/all_to_all | solution.py:607
  1147.7 159.1 %reduce-scatter.14.cloned.1.call-start = ((), (), s32[]{:S(2)}) async-start(), calls=%async_computation.23 | async-start | bytes 3932160 | tf_op jit(solution)/shard_map/reduce_scatter | solution.py:604
  1196.7 110.1 %all-to-all-start.7 = ((bf16[8,64,2048]{2,1,0:T(8,128)(2,1)}), bf16[8,64,2048]{2,1,0:T(8,128)(2,1)}, u32[]{:S(2)}, u32[]{:S(2)}) async-start(bf16[8,64,2048]{2,1,0:T(8,128)(2,1)} %bitcast.191), calls=%async_computation.11 | async-start | bytes 4194304 | tf_op jit(solution)/shard_map/all_to_all | solution.py:654
  1205.9 75.0 %collective-permute-start.30 = (bf16[512,2048]{1,0:T(8,128)(2,1)}, bf16[512,2048]{1,0:T(8,128)(2,1)S(1)}, u32[]{:S(2)}, u32[]{:S(2)}) collective-permute-start(bf16[512,2048]{1,0:T(8,128)(2,1)} %get-tuple-element.151), channel_id=1, source_target_pairs={{0,2},{1,3},{2,4},{3,5},{4,6},{5,7},{8,10},{9,11},{10,12},{11,13},... | collective-permute-start | bytes 6291464 | tf_op jit(solution)/shard_map/ppermute | solution.py:145
  1209.9 73.1 %collective-permute-start.31 = (bf16[512,2048]{1,0:T(8,128)(2,1)}, bf16[512,2048]{1,0:T(8,128)(2,1)}, u32[]{:S(2)}, u32[]{:S(2)}) collective-permute-start(bf16[512,2048]{1,0:T(8,128)(2,1)} %get-tuple-element.152), channel_id=1, source_target_pairs={{2,0},{3,1},{4,2},{5,3},{6,4},{7,5},{10,8},{11,9},{12,10},{13,11},... | collective-permute-start | bytes 6291464 | tf_op jit(solution)/shard_map/ppermute | solution.py:145
  1290.7 81.9 %collective-permute-start.32 = (bf16[512,2048]{1,0:T(8,128)(2,1)}, bf16[512,2048]{1,0:T(8,128)(2,1)S(1)}, u32[]{:S(2)}, u32[]{:S(2)}) collective-permute-start(bf16[512,2048]{1,0:T(8,128)(2,1)} %get-tuple-element.149), channel_id=1, source_target_pairs={{0,2},{1,3},{2,4},{3,5},{4,6},{5,7},{8,10},{9,11},{10,12},{11,13},... | collective-permute-start | bytes 6291464 | tf_op jit(solution)/shard_map/ppermute | solution.py:145
  1305.5 67.1 %collective-permute-start.33 = (bf16[512,2048]{1,0:T(8,128)(2,1)}, bf16[512,2048]{1,0:T(8,128)(2,1)}, u32[]{:S(2)}, u32[]{:S(2)}) collective-permute-start(bf16[512,2048]{1,0:T(8,128)(2,1)} %get-tuple-element.150), channel_id=1, source_target_pairs={{2,0},{3,1},{4,2},{5,3},{6,4},{7,5},{10,8},{11,9},{12,10},{13,11},... | collective-permute-start | bytes 6291464 | tf_op jit(solution)/shard_map/ppermute | solution.py:145
  1306.9 65.8 %all-to-all-start.8 = ((bf16[8,64,768]{2,1,0:T(8,128)(2,1)}), bf16[8,64,768]{2,1,0:T(8,128)(2,1)S(1)}, u32[]{:S(2)}, u32[]{:S(2)}) async-start(bf16[8,64,768]{2,1,0:T(8,128)(2,1)} %bitcast.206), calls=%async_computation.13 | async-start | bytes 1572864 | tf_op jit(solution)/shard_map/all_to_all | solution.py:662
  1382.1 90.3 %collective-permute-start.35 = (bf16[512,2048]{1,0:T(8,128)(2,1)}, bf16[512,2048]{1,0:T(8,128)(2,1)}, u32[]{:S(2)}, u32[]{:S(2)}) collective-permute-start(bf16[512,2048]{1,0:T(8,128)(2,1)} %get-tuple-element.148), channel_id=1, source_target_pairs={{2,0},{3,1},{4,2},{5,3},{6,4},{7,5},{10,8},{11,9},{12,10},{13,11},... | collective-permute-start | bytes 6291464 | tf_op jit(solution)/shard_map/ppermute | solution.py:145
  1383.4 89.0 %collective-permute-start.34 = (bf16[512,2048]{1,0:T(8,128)(2,1)}, bf16[512,2048]{1,0:T(8,128)(2,1)}, u32[]{:S(2)}, u32[]{:S(2)}) collective-permute-start(bf16[512,2048]{1,0:T(8,128)(2,1)} %get-tuple-element.147), channel_id=1, source_target_pairs={{0,2},{1,3},{2,4},{3,5},{4,6},{5,7},{8,10},{9,11},{10,12},{11,13},... | collective-permute-start | bytes 6291464 | tf_op jit(solution)/shard_map/ppermute | solution.py:145
  1399.8 32.9 %collective-permute-start.39 = (f32[4,2048]{1,0:T(4,128)S(1)}, f32[4,2048]{1,0:T(4,128)S(1)}, u32[]{:S(2)}, u32[]{:S(2)}) collective-permute-start(f32[4,2048]{1,0:T(4,128)S(1)} %add.294), channel_id=1, source_target_pairs={{0,2},{1,3},{2,0},{3,1},{4,6},{5,7},{6,4},{7,5},{8,10},{9,11},{10,... | collective-permute-start | bytes 98312 | tf_op jit(solution)/shard_map/ppermute | solution.py:70
  1432.7 14.0 collective-permute-start.40
  (50 other events, 379.6 us)
Sparse Core Ops, SparseCore 0:
  13.1 170.4 all-gather.5
  186.6 100.1 all-gather.7
  288.7 86.1 all-gather.9
  376.6 87.5 all-gather.11
  465.9 87.5 all-gather.13
  773.3 86.4 reduce-scatter.5
  863.1 86.3 reduce-scatter.9
  960.5 86.5 reduce-scatter.7
  1050.4 86.3 reduce-scatter.11
  1167.0 44.3 reduce-scatter.13

commit v4 on v3

--- a/solution.py
+++ b/solution.py
@@ -614,19 +614,19 @@
     down_grad = weight_grad(act, grad_mproj, dgate)
     share_down = over_rows(down_grad)
     grads = hidden_back(dgate, g_weight, dup, u_weight, down_grad)
+    gate_grad = weight_grad(hidden_low, dgate, grads)
     grads = scatter_near(grads)
-    gate_grad = weight_grad(hidden_low, dgate, grads)
+    up_grad = weight_grad(hidden_low, dup, gate_grad, grads)
     share_gate = over_rows(gate_grad)
-    grad_hidden = grad_rows + scatter_far(grads, gate_grad)
+    grad_hidden = grad_rows + scatter_far(grads, up_grad)
 
     grad_aproj, grad_again = norm_back(grad_hidden, a_proj, a_scale, a_gain)
     grad_aproj = after(grad_aproj.astype(BF16), share_down)
     grad_attn = dot_nt(grad_aproj, o_weight).astype(BF16)
     grad_attn = jnp.moveaxis(grad_attn.reshape(own_rows, seq, local_width), 1, 0)
     grad_heads = lax.all_to_all(grad_attn, "seq", split_axis=0, concat_axis=0, tiled=True)
-    up_grad = weight_grad(hidden_low, dup, gate_grad, grad_attn)
     share_up = over_rows(up_grad)
-    o_grad = weight_grad(attn_rows, grad_aproj, up_grad)
+    o_grad = weight_grad(attn_rows, grad_aproj, grad_attn)
     share_output = over_rows(o_grad)
     grad_heads = after(grad_heads, o_grad)
     share_down = scatter_outer(after(share_down, grad_heads))
@@ -662,7 +662,6 @@
     share_qkv = lax.all_to_all(
         share_qkv.reshape(seq, share, 3 * local_width), "seq", split_axis=0, concat_axis=0, tiled=True
     )
-    middle += (share_qkv,)
     share_qkv = share_qkv.reshape(seq, share, 3, local_width).transpose(2, 1, 0, 3)
     share_qkv = share_qkv.reshape(3, share, width).astype(F32)
     slots = lax.dynamic_update_slice_in_dim(

time: 1500 us -> 1470 us (0.980)
  waiting for transfers between devices: 669 us -> 631 us
    all_to_all x1, waiting for transfers between devices: 60.3 us -> 0.01 us  [on_device(): lax.all_to_all(share_qkv.reshape(seq, share, 3 * local_width), 'seq', spl...]
    all_to_all x1, waiting for transfers between devices: 0.01 us -> 21 us  [on_device(): lax.all_to_all(share_output, 'seq', split_axis=0, concat_axis=0, tiled=True)]
    unnamed x89 -> x83, local copies, waits for them, and re-layouts: 31.5 us -> 31.8 us
  transfers between devices with their start and end apart: 59 -> 59, of which waited for: 34 -> 36; matrix products, arithmetic and copies ran while one was open for 15% -> 16% of each run, Pallas kernels for 18% -> 19%
where the time goes in v4:
time: 1470 us; the launch traced here: 1460 us
  waiting for transfers between devices  631 us (43%)
  Pallas kernels  357 us (24%)
  local copies, waits for them, and re-layouts  131 us (9%)
  other arithmetic  123 us (8%)
  starting transfers between devices  112 us (8%)
  blocking collectives  52.2 us (4%)
  matrix products  37.1 us (3%)
  between operations  15.7 us (1%)
    ppermute x35, waiting for transfers between devices, exchange(): lax.ppermute(values, axis, [(i, i ^ bit) for i in range(lax.axis_size(axi...  377 us
    pallas_call x4, Pallas kernels, by_columns(): pl.pallas_call(ordered(kernel, len(operands), earlier), grid=(cols // 512...  146 us
    pallas_call x5, Pallas kernels, weight_grad(): pl.pallas_call(ordered(weight_kernel, 2, earlier), grid=(rows // block,),...  99 us
    ppermute x6, waiting for transfers between devices, shift(): return lax.ppermute(values, 'seq', pairs)  76.4 us
    all_gather x1, waiting for transfers between devices, on_device(): inputs_all = lax.all_gather(inputs, 'seq', axis=0, tiled=True)  68.9 us
    all_to_all x1, blocking collectives, columns(): return lax.all_to_all(part, 'seq', split_axis=0, concat_axis=0, tiled=True)  52.2 us
    pallas_call x1, Pallas kernels, attend_backward(): pl.pallas_call(ordered(functools.partial(backward_kernel, factor=factor,...  43.2 us
    all_to_all x1, waiting for transfers between devices, on_device(): lax.all_to_all(grad_attn, 'seq', split_axis=0, concat_axis=0, tiled=True)  40.1 us
  transfers between devices with their start and end apart: 59, of which 36 were waited for; matrix products, arithmetic and copies ran while one was open for 16% of the time, Pallas kernels for 19%

profile of v4, /device:TPU:0, one launch (start us, length us, event | category | flops | bytes accessed | tf_op | source)
XLA Modules:
  0.0 1459.3 jit_solution(1846230260256720529)
XLA Ops:
  26.6 25.2 %collective-permute-done.7 = f32[8,768]{1,0:T(8,128)S(1)} collective-permute-done((f32[8,768]{1,0:T(8,128)S(1)}, f32[8,768]{1,0:T(8,128)S(1)}, u32[]{:S(2)}, u32[]{:S(2)}) %collective-permute-start.7) | collective-permute-done | bytes 24608 | tf_op jit(solution)/shard_map/ppermute | solution.py:70
  56.4 15.5 %collective-permute-done.8 = f32[8,768]{1,0:T(8,128)S(1)} collective-permute-done((f32[8,768]{1,0:T(8,128)S(1)}, f32[8,768]{1,0:T(8,128)S(1)}, u32[]{:S(2)}, u32[]{:S(2)}) %collective-permute-start.8) | collective-permute-done | bytes 24608 | tf_op jit(solution)/shard_map/ppermute | solution.py:70
  73.6 7.5 fusion.16
  114.6 68.9 %all-gather.6.cloned.1.call-done.refs_0_ = bf16[4096,2048]{1,0:T(8,128)(2,1)} async-done(((bf16[512,2048]{1,0:T(8,128)(2,1)}), bf16[4096,2048]{1,0:T(8,128)(2,1)}) %all-gather.6.cloned.1.call-update) | async-done | bytes 16777232 | tf_op jit(solution)/shard_map/all_gather | solution.py:542
  194.5 19.2 %shard_map.238 = (f32[4096,768]{1,0:T(8,128)}, f32[8,4096]{1,0:T(8,128)S(1)}) custom-call(bf16[4096,2048]{1,0:T(8,128)(2,1)} %shard_map.237.rows_ref.refs_1_.refs_0_, bf16[2048,768]{1,0:T(8,128)(2,1)S(1)} %copy-done.1), custom_call_target="tpu_custom_call" | custom-call | flops 12884901888 | tf_op jit(solution)/shard_map/pallas_call | solution.py:304
  218.9 26.6 %collective-permute-done.12 = f32[2,4096]{1,0:T(2,128)S(1)} collective-permute-done((f32[2,4096]{1,0:T(2,128)S(1)}, f32[2,4096]{1,0:T(2,128)S(1)}, u32[]{:S(2)}, u32[]{:S(2)}) %collective-permute-start.12) | collective-permute-done | bytes 32800 | tf_op jit(solution)/shard_map/ppermute | solution.py:70
  269.7 11.5 shard_map.239
  290.1 52.2 %all_to_all.88 = bf16[8,64,2048]{2,1,0:T(8,128)(2,1)} all-to-all(bf16[8,64,2048]{2,1,0:T(8,128)(2,1)S(1)} %bitcast.187), channel_id=1, replica_groups=mesh['fsdp'=4,'seq'=8] {'seq'}, dimensions={0} | all-to-all | bytes 4194304 | tf_op jit(solution)/shard_map/all_to_all | solution.py:570
  344.6 23.0 %shard_map.240 = (bf16[8,2,256,256]{3,2,1,0:T(8,128)(2,1)S(1)}, f32[2,2,1,2048]{3,2,1,0:T(1,128)S(1)}) custom-call(bf16[8,2,256,256]{3,2,1,0:T(8,128)(2,1)S(1)} %bitcast.161, bf16[8,2,256,256]{3,2,1,0:T(8,128)(2,1)} %bitcast.177, bf16[8,2,256,256]{3,2,1,0:T(8,128)(2,1)} %bitcast.194, s32[2,1,2048]{2,1,0:T(1,128)S(1)} %copy-done.4), custom_call_target="tpu_custom_call" | custom-call | flops 23622320128 | tf_op jit(solution)/shard_map/pallas_call | solution.py:483
  373.4 39.1 %collective-permute-done.17 = bf16[256,2048]{1,0:T(8,128)(2,1)} collective-permute-done((bf16[256,2048]{1,0:T(8,128)(2,1)}, bf16[256,2048]{1,0:T(8,128)(2,1)}, u32[]{:S(2)}, u32[]{:S(2)}) %collective-permute-start.17) | collective-permute-done | bytes 1048608 | tf_op jit(solution)/shard_map/ppermute | solution.py:70
  416.0 18.8 %all-to-all-done.3 = bf16[8,512,256]{2,1,0:T(8,128)(2,1)} async-done(((bf16[8,512,256]{2,1,0:T(8,128)(2,1)}), bf16[8,512,256]{2,1,0:T(8,128)(2,1)}, u32[]{:S(2)}, u32[]{:S(2)}) %all-to-all-start.3) | async-done | bytes 2097184 | tf_op jit(solution)/shard_map/all_to_all | solution.py:584
  438.1 8.3 multiply_reduce_fusion.5
  448.4 47.5 %collective-permute-done.14 = bf16[512,2048]{1,0:T(8,128)(2,1)S(1)} collective-permute-done((bf16[512,2048]{1,0:T(8,128)(2,1)S(1)}, bf16[512,2048]{1,0:T(8,128)(2,1)S(1)}, u32[]{:S(2)}, u32[]{:S(2)}) %collective-permute-start.14) | collective-permute-done | bytes 2097184 | tf_op jit(solution)/shard_map/ppermute | solution.py:70
  504.2 42.5 %shard_map.245 = (bf16[2048,2048]{1,0:T(8,128)(2,1)}, bf16[2048,2048]{1,0:T(8,128)(2,1)}, bf16[2048,2048]{1,0:T(8,128)(2,1)}) custom-call(bf16[2048,2048]{1,0:T(8,128)(2,1)} %pad_maximum_fusion.refs_0_, bf16[2048,2048]{1,0:T(8,128)(2,1)} %all-gather.10.cloned.1.call-done.refs_1_, bf16[2048,2048]{1,0:T(8,128)(2,1)} %all-gather.12.cloned.1.call-done.refs_2_.refs_3_), custom_call_target="tpu_custom_call" | custom-call | flops 34359738368 | tf_op jit(solution)/shard_map/pallas_call | solution.py:241
  553.5 25.3 %shard_map.247 = bf16[2048,2048]{1,0:T(8,128)(2,1)} custom-call(bf16[2048,2048]{1,0:T(8,128)(2,1)} %get-tuple-element.36.refs_0_, bf16[2048,2048]{1,0:T(8,128)(2,1)} %all-gather.14.cloned.1.call-done.refs_1_), custom_call_target="tpu_custom_call" | custom-call | flops 17179869184 | tf_op jit(solution)/shard_map/pallas_call | solution.py:241
  581.6 7.3 collective-permute-done.18
  599.3 46.4 %collective-permute-done.19.refs_0_ = bf16[512,2048]{1,0:T(8,128)(2,1)} collective-permute-done((bf16[512,2048]{1,0:T(8,128)(2,1)}, bf16[512,2048]{1,0:T(8,128)(2,1)}, u32[]{:S(2)}, u32[]{:S(2)}) %collective-permute-start.19) | collective-permute-done | bytes 2097184 | tf_op jit(solution)/shard_map/ppermute | solution.py:70
  662.4 45.3 %collective-permute-done.20 = bf16[512,2048]{1,0:T(8,128)(2,1)S(1)} collective-permute-done((bf16[512,2048]{1,0:T(8,128)(2,1)S(1)}, bf16[512,2048]{1,0:T(8,128)(2,1)S(1)}, u32[]{:S(2)}, u32[]{:S(2)}) %collective-permute-start.20) | collective-permute-done | bytes 2097184 | tf_op jit(solution)/shard_map/ppermute | solution.py:70
  715.8 33.5 %shard_map.249 = (bf16[2048,2048]{1,0:T(8,128)(2,1)}, bf16[2048,2048]{1,0:T(8,128)(2,1)}) custom-call(bf16[2048,2048]{1,0:T(8,128)(2,1)} %pad_maximum_fusion.1.refs_0_.refs_1_, bf16[2048,2048]{1,0:T(8,128)(2,1)} %all-gather.14.cloned.1.call-done.refs_1_, bf16[2048,2048]{1,0:T(8,128)(2,1)} %get-tuple-element.37.refs_2_, ...), custom_call_target="tpu_custom_call" | custom-call | flops 17179869184 | tf_op jit(solution)/shard_map/pallas_call | solution.py:241
  749.4 23.7 %shard_map.250.refs_4_ = bf16[2048,2048]{1,0:T(8,128)(2,1)} custom-call(bf16[2048,2048]{1,0:T(8,128)(2,1)} %get-tuple-element.36.refs_0_, bf16[2048,2048]{1,0:T(8,128)(2,1)} %pad_maximum_fusion.1.refs_0_.refs_1_, bf16[2048,2048]{1,0:T(8,128)(2,1)} %get-tuple-element.39.refs_2_.refs_0_.refs_1_), custom_call_target="tpu_custom_call" | custom-call | flops 17179869184 | tf_op jit(solution)/shard_map/pallas_call | solution.py:279
  773.1 44.6 %shard_map.251.refs_2_ = bf16[2048,2048]{1,0:T(8,128)(2,1)} custom-call(bf16[2048,2048]{1,0:T(8,128)(2,1)} %get-tuple-element.39.refs_2_.refs_0_.refs_1_, bf16[2048,2048]{1,0:T(8,128)(2,1)} %all-gather.10.cloned.1.call-done.refs_1_, bf16[2048,2048]{1,0:T(8,128)(2,1)} %get-tuple-element.40.refs_2_.refs_1_, ...), custom_call_target="tpu_custom_call" | custom-call | flops 34359738368 | tf_op jit(solution)/shard_map/pallas_call | solution.py:241
  822.7 23.6 %shard_map.252.refs_2_ = bf16[2048,2048]{1,0:T(8,128)(2,1)} custom-call(bf16[2048,2048]{1,0:T(8,128)(2,1)} %pad_maximum_fusion.refs_0_, bf16[2048,2048]{1,0:T(8,128)(2,1)} %get-tuple-element.39.refs_2_.refs_0_.refs_1_, bf16[2048,2048]{1,0:T(8,128)(2,1)} %shard_map.251.refs_2_), custom_call_target="tpu_custom_call" | custom-call | flops 17179869184 | tf_op jit(solution)/shard_map/pallas_call | solution.py:279
  846.3 9.0 convert_add_fusion.1.refs_3_
  855.3 23.6 %shard_map.253.refs_1_ = bf16[2048,2048]{1,0:T(8,128)(2,1)} custom-call(bf16[2048,2048]{1,0:T(8,128)(2,1)} %pad_maximum_fusion.refs_0_, bf16[2048,2048]{1,0:T(8,128)(2,1)} %get-tuple-element.40.refs_2_.refs_1_, bf16[2048,2048]{1,0:T(8,128)(2,1)} %shard_map.252.refs_2_, f32[1024,2048]{1,0:T(8,128)} %convert_add_fusion.1.refs_3_), custom_call_target="tpu_custom_call" | custom-call | flops 17179869184 | tf_op jit(solution)/shard_map/pallas_call | solution.py:279
  883.7 46.4 %collective-permute-done.24.refs_0_ = bf16[512,2048]{1,0:T(8,128)(2,1)} collective-permute-done((bf16[512,2048]{1,0:T(8,128)(2,1)S(1)}, bf16[512,2048]{1,0:T(8,128)(2,1)}, u32[]{:S(2)}, u32[]{:S(2)}) %collective-permute-start.24) | collective-permute-done | bytes 2097184 | tf_op jit(solution)/shard_map/ppermute | solution.py:70
  930.2 6.9 multiply_reduce_fusion
  941.4 9.9 convolution_convert_fusion.1
  963.9 9.0 shard_map.256.refs_1_
  972.9 40.1 %all-to-all-done.4.refs_0_ = bf16[8,512,256]{2,1,0:T(8,128)(2,1)} async-done(((bf16[8,512,256]{2,1,0:T(8,128)(2,1)}), bf16[8,512,256]{2,1,0:T(8,128)(2,1)}, u32[]{:S(2)}, u32[]{:S(2)}) %all-to-all-start.4) | async-done | bytes 2097184 | tf_op jit(solution)/shard_map/all_to_all | solution.py:627
  1014.4 43.2 %shard_map.258 = (bf16[8,2,256,256]{3,2,1,0:T(8,128)(2,1)}, bf16[8,2,256,256]{3,2,1,0:T(8,128)(2,1)}, bf16[8,2,256,256]{3,2,1,0:T(8,128)(2,1)}) custom-call(bf16[8,2,256,256]{3,2,1,0:T(8,128)(2,1)} %bitcast.160, bf16[8,2,256,256]{3,2,1,0:T(8,128)(2,1)} %bitcast.178, bf16[8,2,256,256]{3,2,1,0:T(8,128)(2,1)} %bitcast.195, s32[2,1,2048]{2,1,0:T(1,128)S(1)} %copy-done.4, ...), custom_call_target="tpu_custom_call" | custom-call | flops 42949672960 | tf_op jit(solution)/shard_map/pallas_call | solution.py:499
  1091.5 15.1 %shard_map.262 = (bf16[4096,768]{1,0:T(8,128)(2,1)}, f32[1,512]{1,0:T(1,128)}) custom-call(bf16[4096,256]{1,0:T(8,128)(2,1)} %bitcast.169, bf16[4096,256]{1,0:T(8,128)(2,1)} %bitcast.200, bf16[4096,256]{1,0:T(8,128)(2,1)} %shard_map.261.dv_ref, f32[4096,768]{1,0:T(8,128)} %get-tuple-element.30.proj_ref, f32[4096,2]{1,0:T(8,128)} %rsqrt_bitcast_fusion.scale_ref, ...), custom_call_target="tpu_custom_call" | custom-call | flops 14784921600 | tf_op jit(solution)/shard_map/pallas_call | solution.py:388
  1106.5 18.9 %convolution_convert_fusion.refs_0_ = bf16[4096,2048]{1,0:T(8,128)(2,1)} fusion(bf16[4096,768]{1,0:T(8,128)(2,1)} %get-tuple-element.45.refs_1_, bf16[2048,768]{1,0:T(8,128)(2,1)S(1)} %copy-done.1), kind=kOutput, calls=%fused_computation.2 | convolution fusion | flops 12893290496 | bytes 26214400 | tf_op jit(solution)/shard_map/dot_general | solution.py:39
  1125.5 9.0 all-to-all-done.5
  1134.5 8.5 dynamic-slice_bitcast_fusion
  1146.7 19.1 %shard_map.268.refs_0_ = bf16[2048,768]{1,0:T(8,128)(2,1)} custom-call(bf16[4096,2048]{1,0:T(8,128)(2,1)} %shard_map.237.rows_ref.refs_1_.refs_0_, bf16[4096,768]{1,0:T(8,128)(2,1)} %get-tuple-element.45.refs_1_, bf16[4096,2048]{1,0:T(8,128)(2,1)} %shard_map.264.refs_1_.refs_2_), custom_call_target="tpu_custom_call" | custom-call | flops 12884901888 | tf_op jit(solution)/shard_map/pallas_call | solution.py:279
  1165.8 7.5 fusion
  1184.5 11.6 all-to-all-done.6
  1200.5 27.6 %collective-permute-done.30.refs_0_ = bf16[512,2048]{1,0:T(8,128)(2,1)} collective-permute-done((bf16[512,2048]{1,0:T(8,128)(2,1)}, bf16[512,2048]{1,0:T(8,128)(2,1)}, u32[]{:S(2)}, u32[]{:S(2)}) %collective-permute-start.30) | collective-permute-done | bytes 2097184 | tf_op jit(solution)/shard_map/ppermute | solution.py:145
  1228.1 12.4 collective-permute-done.31.refs_1_
  1240.6 7.8 fusion.10
  1248.3 15.5 %collective-permute-start.32 = (bf16[512,2048]{1,0:T(8,128)(2,1)}, bf16[512,2048]{1,0:T(8,128)(2,1)S(1)}, u32[]{:S(2)}, u32[]{:S(2)}) collective-permute-start(bf16[512,2048]{1,0:T(8,128)(2,1)} %get-tuple-element.149), channel_id=1, source_target_pairs={{0,2},{1,3},{2,4},{3,5},{4,6},{5,7},{8,10},{9,11},{10,12},{11,13},... | collective-permute-start | bytes 6291464 | tf_op jit(solution)/shard_map/ppermute | solution.py:145
  1265.1 21.0 %all-to-all-done.7 = bf16[8,64,2048]{2,1,0:T(8,128)(2,1)} async-done(((bf16[8,64,2048]{2,1,0:T(8,128)(2,1)}), bf16[8,64,2048]{2,1,0:T(8,128)(2,1)}, u32[]{:S(2)}, u32[]{:S(2)}) %all-to-all-start.7) | async-done | bytes 2097184 | tf_op jit(solution)/shard_map/all_to_all | solution.py:654
  1286.1 22.6 %collective-permute-done.32.refs_0_ = bf16[512,2048]{1,0:T(8,128)(2,1)S(1)} collective-permute-done((bf16[512,2048]{1,0:T(8,128)(2,1)}, bf16[512,2048]{1,0:T(8,128)(2,1)S(1)}, u32[]{:S(2)}, u32[]{:S(2)}) %collective-permute-start.32) | collective-permute-done | bytes 2097184 | tf_op jit(solution)/shard_map/ppermute | solution.py:145
  1308.7 13.8 collective-permute-done.33.refs_1_
  1322.5 7.8 fusion.11
  1331.6 12.6 collective-permute-start.34
  1361.4 39.8 %collective-permute-done.39 = f32[4,2048]{1,0:T(4,128)S(1)} collective-permute-done((f32[4,2048]{1,0:T(4,128)S(1)}, f32[4,2048]{1,0:T(4,128)S(1)}, u32[]{:S(2)}, u32[]{:S(2)}) %collective-permute-start.39) | collective-permute-done | bytes 32800 | tf_op jit(solution)/shard_map/ppermute | solution.py:70
  1445.0 7.0 fusion.14
  (334 shorter events, 322.5 us)
Async XLA Ops:
  7.2 176.4 %all-gather.6.cloned.1.call-start = ((), (), s32[]{:S(2)}) async-start(), calls=%async_computation.14 | async-start | bytes 18874368 | tf_op jit(solution)/shard_map/all_gather | solution.py:542
  13.0 425.1 %all-gather.8.cloned.1.call-start = ((), (), s32[]{:S(2)}) async-start(), calls=%async_computation.15 | async-start | bytes 8650752 | tf_op jit(solution)/shard_map/all_gather | solution.py:574
  14.0 10.4 collective-permute-start.6
  18.5 65.8 %all-to-all-start = ((bf16[8,2,24576]{2,1,0:T(2,128)(2,1)}), bf16[8,2,24576]{2,1,0:T(2,128)(2,1)S(1)}, u32[]{:S(2)}, u32[]{:S(2)}) async-start(bf16[8,2,24576]{2,1,0:T(2,128)(2,1)} %reshape.278), calls=%async_computation | async-start | bytes 1572864 | tf_op jit(solution)/shard_map/all_to_all | solution.py:544
  24.6 27.3 %collective-permute-start.7 = (f32[8,768]{1,0:T(8,128)S(1)}, f32[8,768]{1,0:T(8,128)S(1)}, u32[]{:S(2)}, u32[]{:S(2)}) collective-permute-start(f32[8,768]{1,0:T(8,128)S(1)} %add.254), channel_id=1, source_target_pairs={{0,2},{1,3},{2,0},{3,1},{4,6},{5,7},{6,4},{7,5},{8,10},{9,11},{10,... | collective-permute-start | bytes 73736 | tf_op jit(solution)/shard_map/ppermute | solution.py:70
  51.9 20.0 %collective-permute-start.8 = (f32[8,768]{1,0:T(8,128)S(1)}, f32[8,768]{1,0:T(8,128)S(1)}, u32[]{:S(2)}, u32[]{:S(2)}) collective-permute-start(f32[8,768]{1,0:T(8,128)S(1)} %add.255), channel_id=1, source_target_pairs={{0,4},{1,5},{2,6},{3,7},{4,0},{5,1},{6,2},{7,3},{8,12},{9,13},{10,... | collective-permute-start | bytes 73736 | tf_op jit(solution)/shard_map/ppermute | solution.py:70
  72.0 16.3 %collective-permute-start.9 = (f32[4,8,4,64]{3,2,1,0:T(4,128)S(1)}, f32[4,8,4,64]{3,2,1,0:T(4,128)S(1)}, u32[]{:S(2)}, u32[]{:S(2)}) collective-permute-start(f32[4,8,4,64]{3,2,1,0:T(4,128)S(1)} %constant_dynamic-update-slice_fusion.1), channel_id=1, source_target_pairs={{0,8},{8,0},{16,24},{24,16},{1,9},{9,1},{17,25},{25,17},{2,10},{10... | collective-permute-start | bytes 98312 | tf_op jit(solution)/shard_map/ppermute | solution.py:70
  87.8 10.8 collective-permute-start
  88.3 12.9 collective-permute-start.10
  90.2 14.1 collective-permute-start.3
  91.4 15.6 %collective-permute-start.1 = (bf16[256,768]{1,0:T(8,128)(2,1)}, bf16[256,768]{1,0:T(8,128)(2,1)}, u32[]{:S(2)}, u32[]{:S(2)}) collective-permute-start(bf16[256,768]{1,0:T(8,128)(2,1)} %copy.211), channel_id=1, source_target_pairs={{0,16},{8,24},{16,0},{24,8},{1,17},{9,25},{17,1},{25,9},{2,18},{10... | collective-permute-start | bytes 1179656 | tf_op jit(solution)/shard_map/ppermute | solution.py:70
  98.5 12.7 collective-permute-start.2
  102.6 10.8 collective-permute-start.4
  104.4 10.2 collective-permute-start.5
  189.8 91.4 %all-to-all-start.1 = ((bf16[8,64,2048]{2,1,0:T(8,128)(2,1)}), bf16[8,64,2048]{2,1,0:T(8,128)(2,1)}, u32[]{:S(2)}, u32[]{:S(2)}) async-start(bf16[8,64,2048]{2,1,0:T(8,128)(2,1)} %bitcast.182), calls=%async_computation.1 | async-start | bytes 4194304 | tf_op jit(solution)/shard_map/all_to_all | solution.py:570
  194.2 310.1 %all-gather.10.cloned.1.call-start = ((), (), s32[]{:S(2)}) async-start(), calls=%async_computation.16 | async-start | bytes 10485760 | tf_op jit(solution)/shard_map/all_gather | solution.py:580
  214.9 30.5 %collective-permute-start.12 = (f32[2,4096]{1,0:T(2,128)S(1)}, f32[2,4096]{1,0:T(2,128)S(1)}, u32[]{:S(2)}, u32[]{:S(2)}) collective-permute-start(f32[2,4096]{1,0:T(2,128)S(1)} %slice_add_fusion.2), channel_id=1, source_target_pairs={{0,2},{1,3},{2,0},{3,1},{4,6},{5,7},{6,4},{7,5},{8,10},{9,11},{10,... | collective-permute-start | bytes 98312 | tf_op jit(solution)/shard_map/ppermute | solution.py:70
  253.4 10.4 collective-permute-start.13
  281.2 223.0 %all-gather.12.cloned.1.call-start = ((), (), s32[]{:S(2)}) async-start(), calls=%async_computation.17 | async-start | bytes 10485760 | tf_op jit(solution)/shard_map/all_gather | solution.py:593
  342.4 70.1 %collective-permute-start.17 = (bf16[256,2048]{1,0:T(8,128)(2,1)}, bf16[256,2048]{1,0:T(8,128)(2,1)}, u32[]{:S(2)}, u32[]{:S(2)}) collective-permute-start(bf16[256,2048]{1,0:T(8,128)(2,1)} %shard_map.246), channel_id=1, source_target_pairs={{0,4},{1,5},{2,6},{3,7},{4,0},{5,1},{6,2},{7,3},{8,12},{9,13},{10,... | collective-permute-start | bytes 3145736 | tf_op jit(solution)/shard_map/ppermute | solution.py:70
  369.0 65.9 %all-to-all-start.3 = ((bf16[8,512,256]{2,1,0:T(8,128)(2,1)}), bf16[8,512,256]{2,1,0:T(8,128)(2,1)}, u32[]{:S(2)}, u32[]{:S(2)}) async-start(bf16[8,512,256]{2,1,0:T(8,128)(2,1)} %bitcast.162), calls=%async_computation.3 | async-start | bytes 4194304 | tf_op jit(solution)/shard_map/all_to_all | solution.py:584
  373.4 180.2 %all-gather.14.cloned.1.call-start = ((), (), s32[]{:S(2)}) async-start(), calls=%async_computation.18 | async-start | bytes 10485760 | tf_op jit(solution)/shard_map/all_gather | solution.py:593
  415.8 525.6 %reduce-scatter.6.cloned.1.call-start = ((), (), s32[]{:S(2)}) async-start(), calls=%async_computation.19 | async-start | bytes 10485760 | tf_op jit(solution)/shard_map/reduce_scatter | solution.py:604
  448.4 47.6 %collective-permute-start.14 = (bf16[512,2048]{1,0:T(8,128)(2,1)S(1)}, bf16[512,2048]{1,0:T(8,128)(2,1)S(1)}, u32[]{:S(2)}, u32[]{:S(2)}) collective-permute-start(bf16[512,2048]{1,0:T(8,128)(2,1)S(1)} %fusion.15), channel_id=1, source_target_pairs={{0,2},{1,3},{2,0},{3,1},{4,6},{5,7},{6,4},{7,5},{8,10},{9,11},{10,... | collective-permute-start | bytes 6291464 | tf_op jit(solution)/shard_map/ppermute | solution.py:70
  448.4 47.6 %collective-permute-start.15 = (bf16[512,2048]{1,0:T(8,128)(2,1)S(1)}, bf16[512,2048]{1,0:T(8,128)(2,1)S(1)}, u32[]{:S(2)}, u32[]{:S(2)}) collective-permute-start(bf16[512,2048]{1,0:T(8,128)(2,1)S(1)} %fusion.15), channel_id=1, source_target_pairs={{0,1},{1,0},{2,3},{3,2},{4,5},{5,4},{6,7},{7,6},{8,9},{9,8},{10,11... | collective-permute-start | bytes 6291464 | tf_op jit(solution)/shard_map/ppermute | solution.py:70
  597.8 48.0 %collective-permute-start.19 = (bf16[512,2048]{1,0:T(8,128)(2,1)}, bf16[512,2048]{1,0:T(8,128)(2,1)}, u32[]{:S(2)}, u32[]{:S(2)}) collective-permute-start(bf16[512,2048]{1,0:T(8,128)(2,1)} %slice.157), channel_id=1, source_target_pairs={{0,2},{1,3},{2,0},{3,1},{4,6},{5,7},{6,4},{7,5},{8,10},{9,11},{10,... | collective-permute-start | bytes 6291464 | tf_op jit(solution)/shard_map/ppermute | solution.py:70
  660.9 46.8 %collective-permute-start.20 = (bf16[512,2048]{1,0:T(8,128)(2,1)S(1)}, bf16[512,2048]{1,0:T(8,128)(2,1)S(1)}, u32[]{:S(2)}, u32[]{:S(2)}) collective-permute-start(bf16[512,2048]{1,0:T(8,128)(2,1)S(1)} %get-tuple-element.145), channel_id=1, source_target_pairs={{0,2},{1,3},{2,0},{3,1},{4,6},{5,7},{6,4},{7,5},{8,10},{9,11},{10,... | collective-permute-start | bytes 6291464 | tf_op jit(solution)/shard_map/ppermute | solution.py:70
  662.4 45.4 %collective-permute-start.21 = (bf16[512,2048]{1,0:T(8,128)(2,1)S(1)}, bf16[512,2048]{1,0:T(8,128)(2,1)S(1)}, u32[]{:S(2)}, u32[]{:S(2)}) collective-permute-start(bf16[512,2048]{1,0:T(8,128)(2,1)S(1)} %get-tuple-element.145), channel_id=1, source_target_pairs={{0,1},{1,0},{2,3},{3,2},{4,5},{5,4},{6,7},{7,6},{8,9},{9,8},{10,11... | collective-permute-start | bytes 6291464 | tf_op jit(solution)/shard_map/ppermute | solution.py:70
  773.1 308.0 %reduce-scatter.8.cloned.1.call-start = ((), (), s32[]{:S(2)}) async-start(), calls=%async_computation.20 | async-start | bytes 10485760 | tf_op jit(solution)/shard_map/reduce_scatter | solution.py:604
  822.4 23.9 %collective-permute-start.23 = (bf16[1024,2048]{1,0:T(8,128)(2,1)}, bf16[1024,2048]{1,0:T(8,128)(2,1)}, u32[]{:S(2)}, u32[]{:S(2)}) collective-permute-start(bf16[1024,2048]{1,0:T(8,128)(2,1)} %slice.123), channel_id=1, source_target_pairs={{0,1},{1,0},{2,3},{3,2},{4,5},{5,4},{6,7},{7,6},{8,9},{9,8},{10,11... | collective-permute-start | bytes 12582920 | tf_op jit(solution)/shard_map/ppermute | solution.py:70
  878.9 202.2 %reduce-scatter.10.cloned.1.call-start = ((), (), s32[]{:S(2)}) async-start(), calls=%async_computation.21 | async-start | bytes 10485760 | tf_op jit(solution)/shard_map/reduce_scatter | solution.py:604
  882.2 48.0 %collective-permute-start.24 = (bf16[512,2048]{1,0:T(8,128)(2,1)S(1)}, bf16[512,2048]{1,0:T(8,128)(2,1)}, u32[]{:S(2)}, u32[]{:S(2)}) collective-permute-start(bf16[512,2048]{1,0:T(8,128)(2,1)S(1)} %slice.156), channel_id=1, source_target_pairs={{0,2},{1,3},{2,0},{3,1},{4,6},{5,7},{6,4},{7,5},{8,10},{9,11},{10,... | collective-permute-start | bytes 6291464 | tf_op jit(solution)/shard_map/ppermute | solution.py:70
  959.2 53.8 %all-to-all-start.4 = ((bf16[8,512,256]{2,1,0:T(8,128)(2,1)}), bf16[8,512,256]{2,1,0:T(8,128)(2,1)}, u32[]{:S(2)}, u32[]{:S(2)}) async-start(bf16[8,512,256]{2,1,0:T(8,128)(2,1)} %bitcast.183), calls=%async_computation.5 | async-start | bytes 4194304 | tf_op jit(solution)/shard_map/all_to_all | solution.py:627
  963.8 201.9 %reduce-scatter.12.cloned.1.call-start = ((), (), s32[]{:S(2)}) async-start(), calls=%async_computation.22 | async-start | bytes 10485760 | tf_op jit(solution)/shard_map/reduce_scatter | solution.py:604
  1014.3 47.2 %collective-permute-start.25 = (bf16[256,2048]{1,0:T(8,128)(2,1)S(1)}, bf16[256,2048]{1,0:T(8,128)(2,1)S(1)}, u32[]{:S(2)}, u32[]{:S(2)}) collective-permute-start(bf16[256,2048]{1,0:T(8,128)(2,1)S(1)} %constant_dynamic-slice_fusion.1), channel_id=1, source_target_pairs={{0,4},{1,5},{2,6},{3,7},{4,0},{5,1},{6,2},{7,3},{8,12},{9,13},{10,... | collective-permute-start | bytes 3145736 | tf_op jit(solution)/shard_map/ppermute | solution.py:70
  1081.1 53.4 %all-to-all-start.5 = ((bf16[8,64,2048]{2,1,0:T(8,128)(2,1)}), bf16[8,64,2048]{2,1,0:T(8,128)(2,1)}, u32[]{:S(2)}, u32[]{:S(2)}) async-start(bf16[8,64,2048]{2,1,0:T(8,128)(2,1)} %bitcast.179), calls=%async_computation.8 | async-start | bytes 4194304 | tf_op jit(solution)/shard_map/all_to_all | solution.py:607
  1143.0 22.8 %collective-permute-start.29 = (bf16[4,512,2048]{2,1,0:T(8,128)(2,1)}, bf16[4,512,2048]{2,1,0:T(8,128)(2,1)}, u32[]{:S(2)}, u32[]{:S(2)}) collective-permute-start(bf16[4,512,2048]{2,1,0:T(8,128)(2,1)} %dynamic-slice_bitcast_fusion), channel_id=1, source_target_pairs={{0,1},{1,0},{2,3},{3,2},{4,5},{5,4},{6,7},{7,6},{8,9},{9,8},{10,11... | collective-permute-start | bytes 25165832 | tf_op jit(solution)/shard_map/ppermute | solution.py:70
  1143.0 53.1 %all-to-all-start.6 = ((bf16[8,64,2048]{2,1,0:T(8,128)(2,1)}), bf16[8,64,2048]{2,1,0:T(8,128)(2,1)S(1)}, u32[]{:S(2)}, u32[]{:S(2)}) async-start(bf16[8,64,2048]{2,1,0:T(8,128)(2,1)} %bitcast.168), calls=%async_computation.9 | async-start | bytes 4194304 | tf_op jit(solution)/shard_map/all_to_all | solution.py:607
  1146.6 198.8 %reduce-scatter.14.cloned.1.call-start = ((), (), s32[]{:S(2)}) async-start(), calls=%async_computation.23 | async-start | bytes 3932160 | tf_op jit(solution)/shard_map/reduce_scatter | solution.py:604
  1178.1 50.0 %collective-permute-start.30 = (bf16[512,2048]{1,0:T(8,128)(2,1)}, bf16[512,2048]{1,0:T(8,128)(2,1)}, u32[]{:S(2)}, u32[]{:S(2)}) collective-permute-start(bf16[512,2048]{1,0:T(8,128)(2,1)} %get-tuple-element.151), channel_id=1, source_target_pairs={{0,2},{1,3},{2,4},{3,5},{4,6},{5,7},{8,10},{9,11},{10,12},{11,13},... | collective-permute-start | bytes 6291464 | tf_op jit(solution)/shard_map/ppermute | solution.py:145
  1183.2 57.4 %collective-permute-start.31 = (bf16[512,2048]{1,0:T(8,128)(2,1)}, bf16[512,2048]{1,0:T(8,128)(2,1)}, u32[]{:S(2)}, u32[]{:S(2)}) collective-permute-start(bf16[512,2048]{1,0:T(8,128)(2,1)} %get-tuple-element.152), channel_id=1, source_target_pairs={{2,0},{3,1},{4,2},{5,3},{6,4},{7,5},{10,8},{11,9},{12,10},{13,11},... | collective-permute-start | bytes 6291464 | tf_op jit(solution)/shard_map/ppermute | solution.py:145
  1196.1 90.0 %all-to-all-start.7 = ((bf16[8,64,2048]{2,1,0:T(8,128)(2,1)}), bf16[8,64,2048]{2,1,0:T(8,128)(2,1)}, u32[]{:S(2)}, u32[]{:S(2)}) async-start(bf16[8,64,2048]{2,1,0:T(8,128)(2,1)} %bitcast.189), calls=%async_computation.11 | async-start | bytes 4194304 | tf_op jit(solution)/shard_map/all_to_all | solution.py:654
  1248.3 60.4 %collective-permute-start.32 = (bf16[512,2048]{1,0:T(8,128)(2,1)}, bf16[512,2048]{1,0:T(8,128)(2,1)S(1)}, u32[]{:S(2)}, u32[]{:S(2)}) collective-permute-start(bf16[512,2048]{1,0:T(8,128)(2,1)} %get-tuple-element.149), channel_id=1, source_target_pairs={{0,2},{1,3},{2,4},{3,5},{4,6},{5,7},{8,10},{9,11},{10,12},{11,13},... | collective-permute-start | bytes 6291464 | tf_op jit(solution)/shard_map/ppermute | solution.py:145
  1263.8 58.7 %collective-permute-start.33 = (bf16[512,2048]{1,0:T(8,128)(2,1)}, bf16[512,2048]{1,0:T(8,128)(2,1)}, u32[]{:S(2)}, u32[]{:S(2)}) collective-permute-start(bf16[512,2048]{1,0:T(8,128)(2,1)} %get-tuple-element.150), channel_id=1, source_target_pairs={{2,0},{3,1},{4,2},{5,3},{6,4},{7,5},{10,8},{11,9},{12,10},{13,11},... | collective-permute-start | bytes 6291464 | tf_op jit(solution)/shard_map/ppermute | solution.py:145
  1330.3 114.7 %collective-permute-start.35 = (bf16[512,2048]{1,0:T(8,128)(2,1)}, bf16[512,2048]{1,0:T(8,128)(2,1)}, u32[]{:S(2)}, u32[]{:S(2)}) collective-permute-start(bf16[512,2048]{1,0:T(8,128)(2,1)} %get-tuple-element.148), channel_id=1, source_target_pairs={{2,0},{3,1},{4,2},{5,3},{6,4},{7,5},{10,8},{11,9},{12,10},{13,11},... | collective-permute-start | bytes 6291464 | tf_op jit(solution)/shard_map/ppermute | solution.py:145
  1331.6 113.4 %collective-permute-start.34 = (bf16[512,2048]{1,0:T(8,128)(2,1)}, bf16[512,2048]{1,0:T(8,128)(2,1)}, u32[]{:S(2)}, u32[]{:S(2)}) collective-permute-start(bf16[512,2048]{1,0:T(8,128)(2,1)} %get-tuple-element.147), channel_id=1, source_target_pairs={{0,2},{1,3},{2,4},{3,5},{4,6},{5,7},{8,10},{9,11},{10,12},{11,13},... | collective-permute-start | bytes 6291464 | tf_op jit(solution)/shard_map/ppermute | solution.py:145
  1345.4 88.5 %all-to-all-start.8 = ((bf16[8,64,768]{2,1,0:T(8,128)(2,1)}), bf16[8,64,768]{2,1,0:T(8,128)(2,1)S(1)}, u32[]{:S(2)}, u32[]{:S(2)}) async-start(bf16[8,64,768]{2,1,0:T(8,128)(2,1)} %bitcast.206), calls=%async_computation.13 | async-start | bytes 1572864 | tf_op jit(solution)/shard_map/all_to_all | solution.py:662
  1359.3 41.9 %collective-permute-start.39 = (f32[4,2048]{1,0:T(4,128)S(1)}, f32[4,2048]{1,0:T(4,128)S(1)}, u32[]{:S(2)}, u32[]{:S(2)}) collective-permute-start(f32[4,2048]{1,0:T(4,128)S(1)} %add.294), channel_id=1, source_target_pairs={{0,2},{1,3},{2,0},{3,1},{4,6},{5,7},{6,4},{7,5},{8,10},{9,11},{10,... | collective-permute-start | bytes 98312 | tf_op jit(solution)/shard_map/ppermute | solution.py:70
  (47 other events, 439.6 us)
Sparse Core Ops, SparseCore 0:
  13.1 170.4 all-gather.5
  186.5 100.1 all-gather.7
  288.6 86.1 all-gather.9
  376.5 87.6 all-gather.11
  465.9 87.5 all-gather.13
  773.2 86.3 reduce-scatter.5
  879.0 86.4 reduce-scatter.7
  968.6 86.3 reduce-scatter.9
  1058.3 86.4 reduce-scatter.11
  1165.9 44.3 reduce-scatter.13
